TPU v7x, 32 devices: a whole 2x2x4 slice. The times are simulated.
32 devices in a mesh: dp: 4 (over x, core), ctx: 8 (over z, y).
Axes of the slice: x: 2, y: 2, z: 4, core: 2. Of those that a mesh axis runs over, the one named last changes fastest.
Arguments:
- out_grad: bfloat16 [16384, 4608], P(('dp', 'ctx')), may hold values from -1 to 1
- adapter_inner: bfloat16 [16384, 16], P(('dp', 'ctx')), may hold values from -32 to 32
- doc_lengths: int32 [4, 4], P('dp'), may hold values from 1 to 1536, 4096 in all within a row
- slab_offset: int32 [4], P('dp'), may hold values from 1 to 1535
- included: int32 [4, 4], P('dp'), may hold values 0 or 1
Outputs:
- adapter_second_gradient: float32 [4608, 16], P(('dp', 'ctx'))
- doc_norms: float32 [4, 4], P('dp')
Inputs may be any that keep to these rules, and one draw needn't show every extreme that they name: `doc_lengths`: in each row the lengths sum to 4096, and the largest is exactly 1536.
All inputs are finite; a program needn't handle non-finite values. No bound on the sum of `included` on one device may be relied on, other than what follows from the above.
Results may differ from a plain program's by a relative error of at most 0.0022.
Values may be sent and summed in bfloat16 or wider, within the bound.
No kernel may reach another device: no remote copies, remote signals or barrier semaphores. Data moves between devices by JAX's collectives and lax.ppermute only.
A program may use at most 64 MiB of HBM per device.

v0:
```python
import jax
import jax.numpy as jnp
from jax import lax
from jax.sharding import PartitionSpec as P

SPAN = 3


clip_norm = 128.0


def from_behind(block, axis, distance):
    devices = range(lax.axis_size(axis))
    route = [((i - distance) % len(devices), i) for i in devices]
    return lax.ppermute(block, axis, route)


def document_ids(lengths, offset, positions, all_tokens):
    doc_ends = jnp.cumsum(lengths)
    starts = doc_ends - lengths
    longest = jnp.argmax(lengths)
    labels = jnp.arange(lengths.shape[0], dtype=jnp.int32)
    doc_shift = jnp.sum(jnp.where(labels == longest, starts, 0)) + offset
    packed = (positions + doc_shift) % all_tokens
    return jnp.sum((doc_ends[None, :] <= packed[:, None]).astype(jnp.int32), axis=1)


def pair_terms(
    left_ids, left_inner, left_grad, right_ids, right_inner, right_grad, keep_rows, member
):
    inner_gram = jnp.einsum(
        "ir,jr->ij", left_inner, right_inner, preferred_element_type=jnp.float32
    )
    grad_gram = jnp.einsum("id,jd->ij", left_grad, right_grad, preferred_element_type=jnp.float32)
    same_doc = (left_ids[:, None] == right_ids[None, :]) & keep_rows[:, None]
    weight = jnp.sum(jnp.where(same_doc, inner_gram * grad_gram, 0.0), axis=1)
    return jnp.dot(weight, member, precision=lax.Precision.HIGHEST)


def boundary_crossing_plan(
    ids_of, local_document_index, adapter_inner, out_grad, member, my_block, block_rows, all_tokens
):
    first_doc = local_document_index[0]
    last_doc = local_document_index[block_rows - 1]
    before_id = ids_of(jnp.reshape((my_block * block_rows - 1) % all_tokens, (1,)))[0]
    after_id = ids_of(jnp.reshape((my_block + 1) * block_rows % all_tokens, (1,)))[0]
    starts_before = before_id == first_doc
    continues = after_id == last_doc
    crossing = starts_before & (local_document_index == first_doc) | continues & (
        local_document_index == last_doc
    )
    norm_terms = pair_terms(
        local_document_index,
        adapter_inner,
        out_grad,
        local_document_index,
        adapter_inner,
        out_grad,
        jnp.logical_not(crossing),
        member,
    )
    in_first = (local_document_index == first_doc).astype(jnp.bfloat16)
    in_last = (local_document_index == last_doc).astype(jnp.bfloat16)
    first_part = jnp.einsum(
        "tr,td->rd", adapter_inner * in_first[:, None], out_grad, preferred_element_type=jnp.float32
    )
    last_part = jnp.einsum(
        "tr,td->rd", adapter_inner * in_last[:, None], out_grad, preferred_element_type=jnp.float32
    )
    finish = (starts_before & jnp.logical_not((first_doc == last_doc) & continues)).astype(
        jnp.float32
    )
    return (first_doc, last_doc, starts_before, norm_terms, first_part, last_part, finish)


def on_device(out_grad, adapter_inner, doc_lengths, slab_offset, included):
    block_rows = out_grad.shape[0]
    ctx_size = lax.axis_size("ctx")
    my_block = lax.axis_index("ctx")
    all_tokens = ctx_size * block_rows
    lengths = doc_lengths[0]
    doc_count = lengths.shape[0]
    row_index = jnp.arange(block_rows, dtype=jnp.int32)
    labels = jnp.arange(doc_count, dtype=jnp.int32)

    def ids_of(positions):
        return document_ids(lengths, slab_offset[0], positions, all_tokens)

    local_document_index = ids_of(my_block * block_rows + row_index)
    member = (local_document_index[:, None] == labels[None, :]).astype(jnp.float32)
    first_doc, last_doc, starts_before, norm_terms, first_part, last_part, finish = (
        boundary_crossing_plan(
            ids_of,
            local_document_index,
            adapter_inner,
            out_grad,
            member,
            my_block,
            block_rows,
            all_tokens,
        )
    )
    chain_flag = (starts_before & (first_doc == last_doc)).astype(jnp.float32)
    running = last_part
    received = jnp.zeros_like(last_part)
    for distance in range(SPAN):
        received = from_behind(running, "ctx", 1)
        running = last_part + chain_flag * received
    complete_document = received + first_part
    end_term = finish * jnp.sum(complete_document * complete_document)
    norm_terms = norm_terms + end_term * (labels == first_doc).astype(jnp.float32)
    squares = lax.psum(norm_terms, "ctx")
    document_grad_norm = jnp.sqrt(squares)
    clip_factor = (
        included[0].astype(jnp.float32) * clip_norm / jnp.maximum(document_grad_norm, clip_norm)
    )
    token_factor = jnp.dot(member, clip_factor, precision=lax.Precision.HIGHEST)
    scaled = (token_factor[:, None] * adapter_inner.astype(jnp.float32)).astype(jnp.bfloat16)
    adapter_second_gradient = lax.psum_scatter(
        jnp.einsum("td,tr->dr", out_grad, scaled, preferred_element_type=jnp.float32),
        ("dp", "ctx"),
        scatter_dimension=0,
        tiled=True,
    )
    return (adapter_second_gradient, document_grad_norm[None, :])


def solution(mesh):
    placed = (P(("dp", "ctx"), None), P(("dp", "ctx"), None), P("dp", None), P("dp"), P("dp", None))
    return jax.shard_map(
        on_device,
        mesh=mesh,
        in_specs=placed,
        out_specs=(P(("dp", "ctx"), None), P("dp", None)),
        check_vma=False,
    )
```

profile of v0, /device:TPU:0, one launch (start us, length us, event | category | flops | bytes accessed | tf_op | source)
XLA Modules:
  0.0 183.1 jit_solution(12775303348443742558)
XLA Ops:
  7.9 1.3 bitcast_reduce_fusion
  9.2 0.8 reduce-window.4
  10.0 1.9 %fusion.14 = s32[]{:T(128)} fusion(s32[1,4]{1,0:T(1,128)} %param.7, s32[]{:T(128)} %get-tuple-element.3, s32[4,1]{0,1:T(1,128)S(1)} %reduce-window.4), kind=kLoop, calls=%fused_computation.33 | loop fusion | flops 15 | bytes 40 | tf_op jit(solution)/shard_map/reduce_sum | solution.py:23
  12.6 0.1 convert_reduce_fusion
  12.7 0.6 fusion.27
  13.3 1.3 fusion.25
  14.6 3.1 %fusion.9 = f32[16,4608]{1,0:T(8,128)S(1)} fusion(bf16[512,4608]{1,0:T(8,128)(2,1)} %param.5, bf16[512,16]{0,1:T(8,128)(2,1)} %param.6, bf16[512]{0:T(512)(128)(2,1)S(1)} %get-tuple-element.10), kind=kOutput, calls=%fused_computation.17 | convolution fusion | flops 75505664 | bytes 5030912 | tf_op jit(solution)/shard_map/tr,td->rd/dot_general | solution.py:67
  17.7 3.0 %collective-permute-start = (f32[16,4608]{1,0:T(8,128)S(1)}, f32[16,4608]{1,0:T(8,128)S(1)}, u32[]{:S(2)}, u32[]{:S(2)}) collective-permute-start(f32[16,4608]{1,0:T(8,128)S(1)} %fusion.9), channel_id=1, source_target_pairs={{7,0},{0,1},{1,2},{2,3},{3,4},{4,5},{5,6},{6,7},{15,8},{8,9},{9,10... | collective-permute-start | bytes 884744 | tf_op jit(solution)/shard_map/ppermute | solution.py:15
  20.7 0.7 fusion.15
  25.3 0.3 fusion.28
  25.6 5.1 %collective-permute-done = f32[16,4608]{1,0:T(8,128)S(1)} collective-permute-done((f32[16,4608]{1,0:T(8,128)S(1)}, f32[16,4608]{1,0:T(8,128)S(1)}, u32[]{:S(2)}, u32[]{:S(2)}) %collective-permute-start) | collective-permute-done | bytes 294944 | tf_op jit(solution)/shard_map/ppermute | solution.py:15
  30.8 6.5 %fusion.1 = f32[512]{0:T(512)S(1)} fusion(f32[512,512]{0,1:T(8,128)S(1)} %fusion.28, bf16[512,4608]{1,0:T(8,128)(2,1)} %param.5, s32[512]{0:T(512)S(1)} %convert_reduce_fusion, pred[512]{0:T(512)(128)(4,1)S(1)} %or_not_fusion), kind=kOutput, calls=%fused_computation.3 | convolution fusion | flops 2417229312 | bytes 5771776 | tf_op jit(solution)/shard_map/id,jd->ij/dot_general | solution.py:34
  37.3 4.3 %collective-permute-done.1 = f32[16,4608]{1,0:T(8,128)S(1)} collective-permute-done((f32[16,4608]{1,0:T(8,128)S(1)}, f32[16,4608]{1,0:T(8,128)S(1)}, u32[]{:S(2)}, u32[]{:S(2)}) %collective-permute-start.1) | collective-permute-done | bytes 294944 | tf_op jit(solution)/shard_map/ppermute | solution.py:15
  41.8 3.1 %fusion.7 = f32[16,4608]{1,0:T(8,128)S(1)} fusion(bf16[512,4608]{1,0:T(8,128)(2,1)} %param.5, bf16[512,16]{0,1:T(8,128)(2,1)S(1)} %copy-done, bf16[512]{0:T(512)(128)(2,1)S(1)} %get-tuple-element.6), kind=kOutput, calls=%fused_computation.15 | convolution fusion | flops 75505664 | bytes 5030912 | tf_op jit(solution)/shard_map/tr,td->rd/dot_general | solution.py:64
  44.8 6.9 %collective-permute-done.2 = f32[16,4608]{1,0:T(8,128)S(1)} collective-permute-done((f32[16,4608]{1,0:T(8,128)S(1)}, f32[16,4608]{1,0:T(8,128)S(1)}, u32[]{:S(2)}, u32[]{:S(2)}) %collective-permute-start.2) | collective-permute-done | bytes 294944 | tf_op jit(solution)/shard_map/ppermute | solution.py:15
  51.8 0.7 multiply_reduce_fusion
  53.1 0.9 fusion.2
  54.0 17.1 %psum.7 = f32[4]{0:T(128)S(1)} all-reduce(f32[4]{0:T(128)S(1)} %fusion.2), channel_id=1, replica_groups=mesh['dp'=4,'ctx'=8] {'ctx'}, use_global_device_ids=true, to_apply=%region_8.9 | all-reduce | flops 4 | bytes 32 | tf_op jit(solution)/shard_map/psum | solution.py:112
  71.2 0.3 fusion.3
  71.5 3.0 %convolution_bitcast_fusion = f32[4608,16]{0,1:T(8,128)S(1)} fusion(bf16[512,4608]{1,0:T(8,128)(2,1)} %param.5, bf16[512,16]{0,1:T(8,128)(2,1)S(1)} %copy-done, f32[512]{0:T(512)S(1)} %bitcast.44), kind=kOutput, calls=%fused_computation | convolution fusion | flops 75522048 | bytes 5031936 | tf_op jit(solution)/shard_map/td,tr->dr/dot_general | solution.py:120
  74.5 2.1 %copy.8 = f32[4608,16]{1,0:T(8,128)} copy(f32[4608,16]{0,1:T(8,128)S(1)} %convolution_bitcast_fusion) | data formatting | bytes 589824
  76.7 0.5 sqrt_bitcast_fusion
  77.2 97.6 %reduce-scatter.4.cloned.1.call-done = f32[144,16]{1,0:T(8,128)} async-done(((f32[4608,16]{1,0:T(8,128)}), f32[144,16]{1,0:T(8,128)}) %reduce-scatter.4.cloned.1.call-update) | async-done | bytes 9232
  174.7 1.6 copy.9
  (12 shorter events, 0.3 us)
Async XLA Ops:
  7.2 18.1 %copy-start = (bf16[512,16]{0,1:T(8,128)(2,1)S(1)}, bf16[512,16]{0,1:T(8,128)(2,1)}, u32[]{:S(2)}) copy-start(bf16[512,16]{0,1:T(8,128)(2,1)} %param.6) | copy-start | bytes 49156
  7.2 167.6 %reduce-scatter.4.cloned.1.call-start = ((), (), s32[]{:S(2)}) async-start(), calls=%async_computation.1 | async-start | bytes 2433024
  17.7 13.1 %collective-permute-start = (f32[16,4608]{1,0:T(8,128)S(1)}, f32[16,4608]{1,0:T(8,128)S(1)}, u32[]{:S(2)}, u32[]{:S(2)}) collective-permute-start(f32[16,4608]{1,0:T(8,128)S(1)} %fusion.9), channel_id=1, source_target_pairs={{7,0},{0,1},{1,2},{2,3},{3,4},{4,5},{5,6},{6,7},{15,8},{8,9},{9,10... | collective-permute-start | bytes 884744 | tf_op jit(solution)/shard_map/ppermute | solution.py:15
  30.7 10.9 %collective-permute-start.1 = (f32[16,4608]{1,0:T(8,128)S(1)}, f32[16,4608]{1,0:T(8,128)S(1)}, u32[]{:S(2)}, u32[]{:S(2)}) collective-permute-start(f32[16,4608]{1,0:T(8,128)S(1)} %multiply_add_fusion.1), channel_id=1, source_target_pairs={{7,0},{0,1},{1,2},{2,3},{3,4},{4,5},{5,6},{6,7},{15,8},{8,9},{9,10... | collective-permute-start | bytes 884744 | tf_op jit(solution)/shard_map/ppermute | solution.py:15
  37.3 33.9 %copy-start.1 = (s32[1,4]{1,0:T(1,128)S(1)}, s32[1,4]{1,0:T(1,128)}, u32[]{:S(2)}) copy-start(s32[1,4]{1,0:T(1,128)} %param.9) | copy-start | bytes 52
  41.7 10.1 %collective-permute-start.2 = (f32[16,4608]{1,0:T(8,128)S(1)}, f32[16,4608]{1,0:T(8,128)S(1)}, u32[]{:S(2)}, u32[]{:S(2)}) collective-permute-start(f32[16,4608]{1,0:T(8,128)S(1)} %multiply_add_fusion), channel_id=1, source_target_pairs={{7,0},{0,1},{1,2},{2,3},{3,4},{4,5},{5,6},{6,7},{15,8},{8,9},{9,10... | collective-permute-start | bytes 884744 | tf_op jit(solution)/shard_map/ppermute | solution.py:15
Sparse Core Ops, SparseCore 0:
  76.8 97.9 reduce-scatter.3
where the time goes:
time: 184 us; the launch traced here: 183 us
  waiting for transfers between devices  114 us (62%)
  between operations  19.9 us (11%)
  matrix products  17.2 us (9%)
  blocking collectives  17.1 us (9%)
  other arithmetic  6.91 us (4%)
  local copies, waits for them, and re-layouts  4.78 us (3%)
  starting transfers between devices  3.16 us (2%)
    unnamed x2, waiting for transfers between devices  97.6 us
    psum x1, blocking collectives, on_device(): squares = lax.psum(norm_terms, 'ctx')  17.1 us
    ppermute x3, waiting for transfers between devices, from_behind(): return lax.ppermute(block, axis, route)  16.4 us
    dot_general x1, matrix products, pair_terms(): jnp.einsum('id,jd->ij', left_grad, right_grad, preferred_element_type=jnp...  6.49 us
  transfers between devices with their start and end apart: 4, of which 4 were waited for; matrix products, arithmetic and copies ran while one was open for 6% of the time, Pallas kernels for 0%

commit v1 on v0

--- a/solution.py
+++ b/solution.py
@@ -1,6 +1,10 @@
+import functools
+
 import jax
 import jax.numpy as jnp
 from jax import lax
+from jax.experimental import pallas as pl
+from jax.experimental.pallas import tpu as pltpu
 from jax.sharding import PartitionSpec as P
 
 SPAN = 3
@@ -73,7 +77,7 @@
     return (first_doc, last_doc, starts_before, norm_terms, first_part, last_part, finish)
 
 
-def on_device(out_grad, adapter_inner, doc_lengths, slab_offset, included):
+def chain_plan(out_grad, adapter_inner, doc_lengths, slab_offset, included):
     block_rows = out_grad.shape[0]
     ctx_size = lax.axis_size("ctx")
     my_block = lax.axis_index("ctx")
@@ -125,6 +129,197 @@
     return (adapter_second_gradient, document_grad_norm[None, :])
 
 
+def bits_of(n):
+    return n.bit_length() - 1
+
+
+def halving_orders(n_ctx):
+    even = list(range(bits_of(n_ctx)))
+    odd = list(even)
+    if len(odd) >= 2:
+        odd[0], odd[1] = odd[1], odd[0]
+    return even, odd
+
+
+def partials_kernel(
+    n_dp, n_ctx, docs, len_ref, off_ref, inner_ref, grad_hbm, send_ref, keep_ref, grad_buf, spread, parts, sems
+):
+    rank, rows = inner_ref.shape
+    span = grad_hbm.shape[1] // n_dp
+    width = span // n_ctx
+    copies = []
+    for d in range(n_dp):
+        copy = pltpu.make_async_copy(
+            grad_hbm.at[:, pl.ds(d * span, span)], grad_buf.at[d], sems.at[d]
+        )
+        copy.start()
+        copies.append(copy)
+    me = lax.axis_index("ctx")
+    odd = lax.rem(lax.axis_index("dp"), 2) == 1
+    total = n_ctx * rows
+    ends, starts = [], []
+    running = jnp.int32(0)
+    for k in range(docs):
+        starts.append(running)
+        running = running + len_ref[0, k]
+        ends.append(running)
+    longest, best = starts[0], len_ref[0, 0]
+    for k in range(1, docs):
+        better = len_ref[0, k] > best
+        longest = jnp.where(better, starts[k], longest)
+        best = jnp.where(better, len_ref[0, k], best)
+    shift = longest + off_ref[0]
+    packed = me * rows + shift + lax.broadcasted_iota(jnp.int32, (rank, rows), 1)
+    packed = jnp.where(packed >= total, packed - total, packed)
+    inner = inner_ref[...].astype(jnp.float32)
+    for k in range(docs):
+        inside = (packed >= starts[k]) & (packed < ends[k])
+        spread[k * rank : (k + 1) * rank, :] = jnp.where(inside, inner, 0.0).astype(jnp.bfloat16)
+    left = spread[...]
+    even_order, odd_order = halving_orders(n_ctx)
+    places = []
+    for c in range(n_ctx):
+        rel = me ^ c
+        place_even = jnp.int32(0)
+        place_odd = jnp.int32(0)
+        for i in range(len(even_order)):
+            weight = n_ctx >> (i + 1)
+            place_even = place_even + ((rel >> even_order[i]) & 1) * weight
+            place_odd = place_odd + ((rel >> odd_order[i]) & 1) * weight
+        places.append(jnp.where(odd, place_odd, place_even))
+    for d in range(n_dp):
+        copies[d].wait()
+        product = jnp.dot(left, grad_buf[d], preferred_element_type=jnp.float32)
+        for c in range(n_ctx):
+            parts[places[c], :, d * width : (d + 1) * width] = product[:, c * width : (c + 1) * width]
+    half = n_ctx // 2
+    keep_ref[...] = parts[0:half]
+    send_ref[...] = parts[half:]
+
+
+def norms_kernel(docs, rank, keep_ref, recv_ref, full_ref, square_ref):
+    full = keep_ref[...] + recv_ref[...]
+    full_ref[...] = full
+    for k in range(docs):
+        piece = full[k * rank : (k + 1) * rank]
+        square_ref[k : k + 1, :] = jnp.broadcast_to(
+            jnp.sum(piece * piece, keepdims=True), (1, square_ref.shape[1])
+        )
+
+
+def clip_kernel(n_dp, docs, rank, inc_ref, one_ref, two_ref, full_ref, send_ref, keep_ref, norm_ref):
+    width = full_ref.shape[1] // n_dp
+    lanes = lax.broadcasted_iota(jnp.int32, (1, one_ref.shape[1]), 1)
+    norms = jnp.zeros((1, one_ref.shape[1]), jnp.float32)
+    total = None
+    for k in range(docs):
+        norm = jnp.sqrt(one_ref[k : k + 1, :] + two_ref[k : k + 1, :])
+        norms = jnp.where(lanes == k, norm, norms)
+        factor = inc_ref[0, k].astype(jnp.float32) * clip_norm / jnp.maximum(norm, clip_norm)
+        term = factor[:, 0:1] * full_ref[k * rank : (k + 1) * rank, :]
+        total = term if total is None else total + term
+    norm_ref[...] = norms[:, :docs]
+    mine = lax.axis_index("dp")
+    for d in range(n_dp):
+        rel = mine ^ d
+        piece = total[:, d * width : (d + 1) * width]
+
+        @pl.when((rel & 1) == 1)
+        def _():
+            send_ref[rel >> 1] = piece
+
+        @pl.when((rel & 1) == 0)
+        def _():
+            keep_ref[rel >> 1] = piece
+
+
+def exchange(block, n_dp, n_ctx, even_bit, odd_bit):
+    route = [
+        (d * n_ctx + c, d * n_ctx + (c ^ (1 << (odd_bit if d % 2 else even_bit))))
+        for d in range(n_dp)
+        for c in range(n_ctx)
+    ]
+    return lax.ppermute(block, ("dp", "ctx"), route)
+
+
+def swap_dp(block, n_dp, bit):
+    return lax.ppermute(block, "dp", [(d, d ^ (1 << bit)) for d in range(n_dp)])
+
+
+def dense_plan(out_grad, adapter_inner, doc_lengths, slab_offset, included):
+    n_dp, n_ctx = lax.axis_size("dp"), lax.axis_size("ctx")
+    rows, features = out_grad.shape
+    rank = adapter_inner.shape[1]
+    docs = doc_lengths.shape[1]
+    high = docs * rank
+    span = features // n_dp
+    slab = features // n_ctx
+    half = n_ctx // 2
+    f32 = jnp.float32
+    vmem = pl.BlockSpec(memory_space=pltpu.VMEM)
+    smem = pl.BlockSpec(memory_space=pltpu.SMEM)
+    send, keep = pl.pallas_call(
+        functools.partial(partials_kernel, n_dp, n_ctx, docs),
+        out_shape=[jax.ShapeDtypeStruct((half, high, slab), f32)] * 2,
+        in_specs=[smem, smem, vmem, pl.BlockSpec(memory_space=pl.ANY)],
+        out_specs=[vmem, vmem],
+        scratch_shapes=[
+            pltpu.VMEM((n_dp, rows, span), jnp.bfloat16),
+            pltpu.VMEM((high, rows), jnp.bfloat16),
+            pltpu.VMEM((n_ctx, high, slab), f32),
+            pltpu.SemaphoreType.DMA((n_dp,)),
+        ],
+    )(doc_lengths, slab_offset, adapter_inner.T, out_grad)
+    even, odd = halving_orders(n_ctx)
+    rounds = list(zip(even, odd))
+    for i, (e, o) in enumerate(rounds[:-1]):
+        received = exchange(send, n_dp, n_ctx, e, o)
+        half //= 2
+        send = keep[half:] + received[half:]
+        keep = keep[:half] + received[:half]
+    received = exchange(send, n_dp, n_ctx, *rounds[-1])
+    full, squares = pl.pallas_call(
+        functools.partial(norms_kernel, docs, rank),
+        out_shape=[
+            jax.ShapeDtypeStruct((high, slab), f32),
+            jax.ShapeDtypeStruct((docs, 128), f32),
+        ],
+        in_specs=[vmem, vmem],
+        out_specs=[vmem, vmem],
+    )(keep[0], received[0])
+    for e, o in rounds[:-1]:
+        squares = squares + exchange(squares, n_dp, n_ctx, e, o)
+    other = exchange(squares, n_dp, n_ctx, *rounds[-1])
+    width = slab // n_dp
+    send, keep, norms = pl.pallas_call(
+        functools.partial(clip_kernel, n_dp, docs, rank),
+        out_shape=[
+            jax.ShapeDtypeStruct((n_dp // 2, rank, width), f32),
+            jax.ShapeDtypeStruct((n_dp // 2, rank, width), f32),
+            jax.ShapeDtypeStruct((1, docs), f32),
+        ],
+        in_specs=[smem, vmem, vmem, vmem],
+        out_specs=[vmem, vmem, vmem],
+    )(included, squares, other, full)
+    received = swap_dp(send, n_dp, 0)
+    send = keep[1] + received[1]
+    result = (keep[0] + received[0]) + swap_dp(send, n_dp, 1)
+    return (result.T, norms)
+
+
+def on_device(out_grad, adapter_inner, doc_lengths, slab_offset, included):
+    n_dp, n_ctx = lax.axis_size("dp"), lax.axis_size("ctx")
+    dense = (
+        n_dp == 4
+        and n_ctx >= 4
+        and n_ctx & (n_ctx - 1) == 0
+        and doc_lengths.shape[1] <= n_ctx
+        and out_grad.shape[1] // n_dp % 128 == 0
+    )
+    plan = dense_plan if dense else chain_plan
+    return plan(out_grad, adapter_inner, doc_lengths, slab_offset, included)
+
+
 def solution(mesh):
     placed = (P(("dp", "ctx"), None), P(("dp", "ctx"), None), P("dp", None), P("dp"), P("dp", None))
     return jax.shard_map(

time: 184 us -> 61.2 us (0.33)
  waiting for transfers between devices: 114 us -> 30.9 us
  between operations: 19.9 us -> 1.3 us
  matrix products: 17.2 us -> 0 us
  blocking collectives: 17.1 us -> 0 us
  starting transfers between devices: 3.16 us -> 14.2 us
  Pallas kernels: 0 us -> 8.53 us
  local copies, waits for them, and re-layouts: 4.78 us -> 1.23 us
  other arithmetic: 6.91 us -> 4.58 us
    unnamed x2 -> x0, waiting for transfers between devices: 97.6 us -> none
    dot_general x7 -> x0, matrix products: 17.2 us -> none  [the longest x1 6.49 us: pair_terms(): jnp.einsum('id,jd->ij', left_grad, right_grad, preferred_element_type=jnp...]
    psum x1 -> x0, blocking collectives: 17.1 us -> none  [on_device(): squares = lax.psum(norm_terms, 'ctx')]
    ppermute x3 -> x8, waiting for transfers between devices: 16.4 us -> 30.9 us  [the longest x6 27.3 us: exchange(): return lax.ppermute(block, ('dp', 'ctx'), route)]
    ppermute x3 -> x8, starting transfers between devices: 3.13 us -> 14.2 us  [the longest x6 12.6 us: exchange(): return lax.ppermute(block, ('dp', 'ctx'), route)]
    pallas_call x0 -> x3, Pallas kernels: none -> 8.53 us  [the longest x1 4.97 us: dense_plan(): pl.pallas_call(functools.partial(partials_kernel, n_dp, n_ctx, docs), out...]
    reduce_sum x4 -> x0, other arithmetic: 3.4 us -> none  [the longest x1 1.94 us: document_ids(): doc_shift = jnp.sum(jnp.where(labels == longest, starts, 0)) + offset]
    add x2 -> x5, other arithmetic: 0.06 us -> 3.25 us  [the longest x1 1.14 us: dense_plan(): keep = keep[:half] + received[:half]]
  transfers between devices with their start and end apart: 4 -> 8, of which waited for: 4 -> 8; matrix products, arithmetic and copies ran while one was open for 6% -> 0% of each run, Pallas kernels for 0% -> 0%
where the time goes in v1:
time: 61.2 us; the launch traced here: 60.7 us
  waiting for transfers between devices  30.9 us (50%)
  starting transfers between devices  14.2 us (23%)
  Pallas kernels  8.53 us (14%)
  other arithmetic  4.58 us (7%)
  between operations  1.3 us (2%)
  local copies, waits for them, and re-layouts  1.23 us (2%)
    ppermute x6, waiting for transfers between devices, exchange(): return lax.ppermute(block, ('dp', 'ctx'), route)  27.3 us
    ppermute x6, starting transfers between devices, exchange(): return lax.ppermute(block, ('dp', 'ctx'), route)  12.6 us
    pallas_call x1, Pallas kernels, dense_plan(): pl.pallas_call(functools.partial(partials_kernel, n_dp, n_ctx, docs), out...  4.97 us
    ppermute x2, waiting for transfers between devices, swap_dp(): return lax.ppermute(block, 'dp', [(d, d ^ 1 << bit) for d in range(n_dp)])  3.61 us
    pallas_call x1, Pallas kernels, dense_plan(): pl.pallas_call(functools.partial(clip_kernel, n_dp, docs, rank), out_shap...  1.84 us
    pallas_call x1, Pallas kernels, dense_plan(): pl.pallas_call(functools.partial(norms_kernel, docs, rank), out_shape=[ja...  1.72 us
    ppermute x2, starting transfers between devices, swap_dp(): return lax.ppermute(block, 'dp', [(d, d ^ 1 << bit) for d in range(n_dp)])  1.55 us
    transpose x1, other arithmetic, dense_plan(): return (result.T, norms)  1.33 us
  transfers between devices with their start and end apart: 8, of which 8 were waited for; matrix products, arithmetic and copies ran while one was open for 0% of the time, Pallas kernels for 0%

profile of v1, /device:TPU:0, one launch (start us, length us, event | category | flops | bytes accessed | tf_op | source)
XLA Modules:
  0.0 60.7 jit_solution(9032013470093508226)
XLA Ops:
  1.3 5.0 %shard_map.68 = (f32[4,64,576]{2,1,0:T(8,128)}, f32[4,64,576]{2,1,0:T(8,128)}) custom-call(s32[1,4]{1,0:T(1,128)} %len_ref.1, s32[1]{0:T(128)S(6)} %copy.7.off_ref, bf16[16,512]{1,0:T(8,128)(2,1)} %bitcast.15, bf16[512,4608]{1,0:T(8,128)(2,1)} %grad_hbm.1), custom_call_target="tpu_custom_call" | custom-call | tf_op jit(solution)/shard_map/pallas_call | solution.py:261
  6.3 3.1 %collective-permute-start = (f32[4,64,576]{2,1,0:T(8,128)}, f32[4,64,576]{2,1,0:T(8,128)S(1)}, u32[]{:S(2)}, u32[]{:S(2)}) collective-permute-start(f32[4,64,576]{2,1,0:T(8,128)} %get-tuple-element.10), channel_id=1, source_target_pairs={{0,1},{1,0},{2,3},{3,2},{4,5},{5,4},{6,7},{7,6},{8,10},{9,11},{10,... | collective-permute-start | bytes 1769480 | tf_op jit(solution)/shard_map/ppermute | solution.py:242
  9.3 8.8 %collective-permute-done = f32[4,64,576]{2,1,0:T(8,128)S(1)} collective-permute-done((f32[4,64,576]{2,1,0:T(8,128)}, f32[4,64,576]{2,1,0:T(8,128)S(1)}, u32[]{:S(2)}, u32[]{:S(2)}) %collective-permute-start) | collective-permute-done | bytes 589856 | tf_op jit(solution)/shard_map/ppermute | solution.py:242
  18.1 1.1 %slice_add_fusion.1 = (f32[2,64,576]{2,1,0:T(8,128)S(1)}, f32[2,64,576]{2,1,0:T(8,128)S(1)}) fusion(f32[4,64,576]{2,1,0:T(8,128)S(1)} %collective-permute-done, f32[4,64,576]{2,1,0:T(8,128)} %get-tuple-element.9), kind=kLoop, calls=%fused_computation.1 | loop fusion | flops 147456 | bytes 1769472 | tf_op jit(solution)/shard_map/add | solution.py:279
  19.2 2.1 %collective-permute-start.1 = (f32[2,64,576]{2,1,0:T(8,128)S(1)}, f32[2,64,576]{2,1,0:T(8,128)S(1)}, u32[]{:S(2)}, u32[]{:S(2)}) collective-permute-start(f32[2,64,576]{2,1,0:T(8,128)S(1)} %get-tuple-element.17), channel_id=1, source_target_pairs={{0,2},{1,3},{2,0},{3,1},{4,6},{5,7},{6,4},{7,5},{8,9},{9,8},{10,11... | collective-permute-start | bytes 884744 | tf_op jit(solution)/shard_map/ppermute | solution.py:242
  21.4 5.1 %collective-permute-done.1 = f32[2,64,576]{2,1,0:T(8,128)S(1)} collective-permute-done((f32[2,64,576]{2,1,0:T(8,128)S(1)}, f32[2,64,576]{2,1,0:T(8,128)S(1)}, u32[]{:S(2)}, u32[]{:S(2)}) %collective-permute-start.1) | collective-permute-done | bytes 294944 | tf_op jit(solution)/shard_map/ppermute | solution.py:242
  26.4 0.7 %slice_add_fusion.2 = (f32[1,64,576]{2,1,0:T(8,128)S(1)}, f32[64,576]{1,0:T(8,128)}) fusion(f32[2,64,576]{2,1,0:T(8,128)S(1)} %collective-permute-done.1, f32[2,64,576]{2,1,0:T(8,128)S(1)} %get-tuple-element.16), kind=kLoop, calls=%fused_computation.2 | loop fusion | flops 73728 | bytes 884736 | tf_op jit(solution)/shard_map/add | solution.py:278
  27.1 3.0 %collective-permute-start.2 = (f32[1,64,576]{2,1,0:T(8,128)S(1)}, f32[1,64,576]{2,1,0:T(8,128)S(1)}, u32[]{:S(2)}, u32[]{:S(2)}) collective-permute-start(f32[1,64,576]{2,1,0:T(8,128)S(1)} %get-tuple-element.18), channel_id=1, source_target_pairs={{0,4},{1,5},{2,6},{3,7},{4,0},{5,1},{6,2},{7,3},{8,12},{9,13},{10,... | collective-permute-start | bytes 442376 | tf_op jit(solution)/shard_map/ppermute | solution.py:242
  30.2 6.0 %collective-permute-done.2 = f32[1,64,576]{2,1,0:T(8,128)S(1)} collective-permute-done((f32[1,64,576]{2,1,0:T(8,128)S(1)}, f32[1,64,576]{2,1,0:T(8,128)S(1)}, u32[]{:S(2)}, u32[]{:S(2)}) %collective-permute-start.2) | collective-permute-done | bytes 147488 | tf_op jit(solution)/shard_map/ppermute | solution.py:242
  36.2 0.7 %copy-done = f32[1,64,576]{2,1,0:T(8,128)} copy-done((f32[1,64,576]{2,1,0:T(8,128)}, f32[1,64,576]{2,1,0:T(8,128)S(1)}, u32[]{:S(2)}) %copy-start) | copy-done | bytes 147480
  36.8 1.7 %shard_map.69 = (f32[64,576]{1,0:T(8,128)}, f32[4,128]{1,0:T(4,128)}) custom-call(f32[64,576]{1,0:T(8,128)} %get-tuple-element.19.keep_ref, f32[64,576]{1,0:T(8,128)} %bitcast.14), custom_call_target="tpu_custom_call" | custom-call | tf_op jit(solution)/shard_map/pallas_call | solution.py:281
  38.5 1.6 %collective-permute-start.3 = (f32[4,128]{1,0:T(4,128)}, f32[4,128]{1,0:T(4,128)S(1)}, u32[]{:S(2)}, u32[]{:S(2)}) collective-permute-start(f32[4,128]{1,0:T(4,128)} %get-tuple-element.11), channel_id=1, source_target_pairs={{0,1},{1,0},{2,3},{3,2},{4,5},{5,4},{6,7},{7,6},{8,10},{9,11},{10,... | collective-permute-start | bytes 6152 | tf_op jit(solution)/shard_map/ppermute | solution.py:242
  40.1 2.2 %collective-permute-done.3 = f32[4,128]{1,0:T(4,128)S(1)} collective-permute-done((f32[4,128]{1,0:T(4,128)}, f32[4,128]{1,0:T(4,128)S(1)}, u32[]{:S(2)}, u32[]{:S(2)}) %collective-permute-start.3) | collective-permute-done | bytes 2080 | tf_op jit(solution)/shard_map/ppermute | solution.py:242
  42.3 0.7 %add.37 = f32[4,128]{1,0:T(4,128)S(1)} add(f32[4,128]{1,0:T(4,128)} %get-tuple-element.11, f32[4,128]{1,0:T(4,128)S(1)} %collective-permute-done.3) | non-fusion elementwise | flops 512 | bytes 6144 | tf_op jit(solution)/shard_map/add | solution.py:291
  43.0 0.7 %collective-permute-start.4 = (f32[4,128]{1,0:T(4,128)S(1)}, f32[4,128]{1,0:T(4,128)S(1)}, u32[]{:S(2)}, u32[]{:S(2)}) collective-permute-start(f32[4,128]{1,0:T(4,128)S(1)} %add.37), channel_id=1, source_target_pairs={{0,2},{1,3},{2,0},{3,1},{4,6},{5,7},{6,4},{7,5},{8,9},{9,8},{10,11... | collective-permute-start | bytes 6152 | tf_op jit(solution)/shard_map/ppermute | solution.py:242
  43.7 2.9 %collective-permute-done.4 = f32[4,128]{1,0:T(4,128)S(1)} collective-permute-done((f32[4,128]{1,0:T(4,128)S(1)}, f32[4,128]{1,0:T(4,128)S(1)}, u32[]{:S(2)}, u32[]{:S(2)}) %collective-permute-start.4) | collective-permute-done | bytes 2080 | tf_op jit(solution)/shard_map/ppermute | solution.py:242
  46.6 2.1 %collective-permute-start.5 = (f32[4,128]{1,0:T(4,128)S(1)}, f32[4,128]{1,0:T(4,128)S(1)}, u32[]{:S(2)}, u32[]{:S(2)}) collective-permute-start(f32[4,128]{1,0:T(4,128)S(1)} %add.38.one_ref), channel_id=1, source_target_pairs={{0,4},{1,5},{2,6},{3,7},{4,0},{5,1},{6,2},{7,3},{8,12},{9,13},{10,... | collective-permute-start | bytes 6152 | tf_op jit(solution)/shard_map/ppermute | solution.py:242
  48.7 2.4 %collective-permute-done.5.two_ref = f32[4,128]{1,0:T(4,128)S(1)} collective-permute-done((f32[4,128]{1,0:T(4,128)S(1)}, f32[4,128]{1,0:T(4,128)S(1)}, u32[]{:S(2)}, u32[]{:S(2)}) %collective-permute-start.5) | collective-permute-done | bytes 2080 | tf_op jit(solution)/shard_map/ppermute | solution.py:242
  51.7 1.8 %shard_map.70 = (f32[2,16,144]{2,1,0:T(8,128)}, f32[2,16,144]{2,1,0:T(8,128)}, f32[1,4]{1,0:T(1,128)}) custom-call(s32[1,4]{1,0:T(1,128)} %inc_ref.1, f32[4,128]{1,0:T(4,128)} %copy-done.1, f32[4,128]{1,0:T(4,128)} %copy-done.2, f32[64,576]{1,0:T(8,128)} %get-tuple-element.12.full_ref), custom_call_target="tpu_custom_call" | custom-call | tf_op jit(solution)/shard_map/pallas_call | solution.py:294
  53.5 1.4 %collective-permute-done.6 = f32[2,16,144]{2,1,0:T(8,128)S(1)} collective-permute-done((f32[2,16,144]{2,1,0:T(8,128)}, f32[2,16,144]{2,1,0:T(8,128)S(1)}, u32[]{:S(2)}, u32[]{:S(2)}) %collective-permute-start.6) | collective-permute-done | bytes 18464 | tf_op jit(solution)/shard_map/ppermute | solution.py:246
  54.9 0.7 %fusion.1 = f32[16,144]{1,0:T(8,128)S(1)} fusion(f32[2,16,144]{2,1,0:T(8,128)S(1)} %collective-permute-done.6, f32[2,16,144]{2,1,0:T(8,128)} %get-tuple-element.13), kind=kLoop, calls=%fused_computation.6 | loop fusion | flops 2304 | bytes 27648 | tf_op jit(solution)/shard_map/add | solution.py:305
  55.7 1.5 %collective-permute-start.7 = (f32[16,144]{1,0:T(8,128)S(1)}, f32[16,144]{1,0:T(8,128)S(1)}, u32[]{:S(2)}, u32[]{:S(2)}) collective-permute-start(f32[16,144]{1,0:T(8,128)S(1)} %fusion.1), channel_id=1, source_target_pairs={{0,16},{8,24},{16,0},{24,8},{1,17},{9,25},{17,1},{25,9},{2,18},{10... | collective-permute-start | bytes 27656 | tf_op jit(solution)/shard_map/ppermute | solution.py:246
  57.2 2.2 %collective-permute-done.7 = f32[16,144]{1,0:T(8,128)S(1)} collective-permute-done((f32[16,144]{1,0:T(8,128)S(1)}, f32[16,144]{1,0:T(8,128)S(1)}, u32[]{:S(2)}, u32[]{:S(2)}) %collective-permute-start.7) | collective-permute-done | bytes 9248 | tf_op jit(solution)/shard_map/ppermute | solution.py:246
  59.4 1.3 %fusion.4 = f32[144,16]{0,1:T(8,128)} fusion(f32[16,144]{1,0:T(8,128)S(1)} %collective-permute-done.7, f32[2,16,144]{2,1,0:T(8,128)S(1)} %collective-permute-done.6, f32[2,16,144]{2,1,0:T(8,128)} %get-tuple-element.13), kind=kLoop, calls=%fused_computation.10 | loop fusion | flops 4608 | bytes 36864 | tf_op jit(solution)/shard_map/transpose | solution.py:307
  (7 shorter events, 0.6 us)
Async XLA Ops:
  6.3 11.8 %collective-permute-start = (f32[4,64,576]{2,1,0:T(8,128)}, f32[4,64,576]{2,1,0:T(8,128)S(1)}, u32[]{:S(2)}, u32[]{:S(2)}) collective-permute-start(f32[4,64,576]{2,1,0:T(8,128)} %get-tuple-element.10), channel_id=1, source_target_pairs={{0,1},{1,0},{2,3},{3,2},{4,5},{5,4},{6,7},{7,6},{8,10},{9,11},{10,... | collective-permute-start | bytes 1769480 | tf_op jit(solution)/shard_map/ppermute | solution.py:242
  19.2 7.2 %collective-permute-start.1 = (f32[2,64,576]{2,1,0:T(8,128)S(1)}, f32[2,64,576]{2,1,0:T(8,128)S(1)}, u32[]{:S(2)}, u32[]{:S(2)}) collective-permute-start(f32[2,64,576]{2,1,0:T(8,128)S(1)} %get-tuple-element.17), channel_id=1, source_target_pairs={{0,2},{1,3},{2,0},{3,1},{4,6},{5,7},{6,4},{7,5},{8,9},{9,8},{10,11... | collective-permute-start | bytes 884744 | tf_op jit(solution)/shard_map/ppermute | solution.py:242
  27.1 9.0 %collective-permute-start.2 = (f32[1,64,576]{2,1,0:T(8,128)S(1)}, f32[1,64,576]{2,1,0:T(8,128)S(1)}, u32[]{:S(2)}, u32[]{:S(2)}) collective-permute-start(f32[1,64,576]{2,1,0:T(8,128)S(1)} %get-tuple-element.18), channel_id=1, source_target_pairs={{0,4},{1,5},{2,6},{3,7},{4,0},{5,1},{6,2},{7,3},{8,12},{9,13},{10,... | collective-permute-start | bytes 442376 | tf_op jit(solution)/shard_map/ppermute | solution.py:242
  36.2 0.7 %copy-start = (f32[1,64,576]{2,1,0:T(8,128)}, f32[1,64,576]{2,1,0:T(8,128)S(1)}, u32[]{:S(2)}) copy-start(f32[1,64,576]{2,1,0:T(8,128)S(1)} %collective-permute-done.2) | copy-start | bytes 442372
  38.5 3.8 %collective-permute-start.3 = (f32[4,128]{1,0:T(4,128)}, f32[4,128]{1,0:T(4,128)S(1)}, u32[]{:S(2)}, u32[]{:S(2)}) collective-permute-start(f32[4,128]{1,0:T(4,128)} %get-tuple-element.11), channel_id=1, source_target_pairs={{0,1},{1,0},{2,3},{3,2},{4,5},{5,4},{6,7},{7,6},{8,10},{9,11},{10,... | collective-permute-start | bytes 6152 | tf_op jit(solution)/shard_map/ppermute | solution.py:242
  43.0 3.6 %collective-permute-start.4 = (f32[4,128]{1,0:T(4,128)S(1)}, f32[4,128]{1,0:T(4,128)S(1)}, u32[]{:S(2)}, u32[]{:S(2)}) collective-permute-start(f32[4,128]{1,0:T(4,128)S(1)} %add.37), channel_id=1, source_target_pairs={{0,2},{1,3},{2,0},{3,1},{4,6},{5,7},{6,4},{7,5},{8,9},{9,8},{10,11... | collective-permute-start | bytes 6152 | tf_op jit(solution)/shard_map/ppermute | solution.py:242
  46.6 4.5 %copy-start.1 = (f32[4,128]{1,0:T(4,128)}, f32[4,128]{1,0:T(4,128)S(1)}, u32[]{:S(2)}) copy-start(f32[4,128]{1,0:T(4,128)S(1)} %add.38.one_ref) | copy-start | bytes 6148
  46.6 4.5 %collective-permute-start.5 = (f32[4,128]{1,0:T(4,128)S(1)}, f32[4,128]{1,0:T(4,128)S(1)}, u32[]{:S(2)}, u32[]{:S(2)}) collective-permute-start(f32[4,128]{1,0:T(4,128)S(1)} %add.38.one_ref), channel_id=1, source_target_pairs={{0,4},{1,5},{2,6},{3,7},{4,0},{5,1},{6,2},{7,3},{8,12},{9,13},{10,... | collective-permute-start | bytes 6152 | tf_op jit(solution)/shard_map/ppermute | solution.py:242
  51.1 0.6 copy-start.2
  53.5 1.4 %collective-permute-start.6 = (f32[2,16,144]{2,1,0:T(8,128)}, f32[2,16,144]{2,1,0:T(8,128)S(1)}, u32[]{:S(2)}, u32[]{:S(2)}) collective-permute-start(f32[2,16,144]{2,1,0:T(8,128)} %get-tuple-element.14), channel_id=1, source_target_pairs={{0,8},{8,0},{16,24},{24,16},{1,9},{9,1},{17,25},{25,17},{2,10},{10... | collective-permute-start | bytes 55304 | tf_op jit(solution)/shard_map/ppermute | solution.py:246
  55.7 3.7 %collective-permute-start.7 = (f32[16,144]{1,0:T(8,128)S(1)}, f32[16,144]{1,0:T(8,128)S(1)}, u32[]{:S(2)}, u32[]{:S(2)}) collective-permute-start(f32[16,144]{1,0:T(8,128)S(1)} %fusion.1), channel_id=1, source_target_pairs={{0,16},{8,24},{16,0},{24,8},{1,17},{9,25},{17,1},{25,9},{2,18},{10... | collective-permute-start | bytes 27656 | tf_op jit(solution)/shard_map/ppermute | solution.py:246

commit v2 on v0

--- a/solution.py
+++ b/solution.py
@@ -1,6 +1,10 @@
+import functools
+
 import jax
 import jax.numpy as jnp
 from jax import lax
+from jax.experimental import pallas as pl
+from jax.experimental.pallas import tpu as pltpu
 from jax.sharding import PartitionSpec as P
 
 SPAN = 3
@@ -73,7 +77,7 @@
     return (first_doc, last_doc, starts_before, norm_terms, first_part, last_part, finish)
 
 
-def on_device(out_grad, adapter_inner, doc_lengths, slab_offset, included):
+def chain_plan(out_grad, adapter_inner, doc_lengths, slab_offset, included):
     block_rows = out_grad.shape[0]
     ctx_size = lax.axis_size("ctx")
     my_block = lax.axis_index("ctx")
@@ -125,6 +129,208 @@
     return (adapter_second_gradient, document_grad_norm[None, :])
 
 
+def bits_of(n):
+    return n.bit_length() - 1
+
+
+def halving_orders(n_ctx):
+    even = list(range(bits_of(n_ctx)))
+    odd = list(even)
+    odd[0], odd[1] = odd[1], odd[0]
+    return even, odd
+
+
+def my_bits(n_ctx):
+    me = lax.axis_index("ctx")
+    odd = lax.rem(lax.axis_index("dp"), 2) == 1
+    even_order, odd_order = halving_orders(n_ctx)
+    return [
+        jnp.where(odd, (me >> o) & 1, (me >> e) & 1) for e, o in zip(even_order, odd_order)
+    ]
+
+
+def document_of(bits, flips):
+    document = jnp.int32(0)
+    for bit, flip in zip(bits, flips):
+        document = document * 2 + (bit ^ flip)
+    return document
+
+
+def partials_kernel(
+    flip, n_ctx, docs, chunks, len_ref, off_ref, inner_ref, grad_hbm, out_ref, grad_buf, spread, sems
+):
+    rank, rows = inner_ref.shape
+    width = grad_hbm.shape[1] // chunks
+    copies = []
+    for j in range(chunks):
+        copy = pltpu.make_async_copy(
+            grad_hbm.at[:, pl.ds(j * width, width)], grad_buf.at[j], sems.at[j]
+        )
+        copy.start()
+        copies.append(copy)
+    total = n_ctx * rows
+    running = jnp.int32(0)
+    longest, best = jnp.int32(0), len_ref[0, 0]
+    for k in range(1, docs):
+        running = running + len_ref[0, k - 1]
+        better = len_ref[0, k] > best
+        longest = jnp.where(better, running, longest)
+        best = jnp.where(better, len_ref[0, k], best)
+    shift = longest + off_ref[0]
+    packed = lax.axis_index("ctx") * rows + shift + lax.broadcasted_iota(jnp.int32, (rank, rows), 1)
+    packed = jnp.where(packed >= total, packed - total, packed)
+    inner = inner_ref[...].astype(jnp.float32)
+    bits = my_bits(n_ctx)
+    depth = bits_of(docs)
+    places = docs // 2
+    for place in range(places):
+        flips = [flip] + [(place >> (depth - 2 - i)) & 1 for i in range(depth - 1)]
+        document = document_of(bits[:depth], flips)
+        start, length = jnp.int32(0), jnp.int32(0)
+        for k in range(docs):
+            start = start + jnp.where(k < document, len_ref[0, k], 0)
+            length = length + jnp.where(k == document, len_ref[0, k], 0)
+        inside = (packed >= start) & (packed < start + length)
+        spread[place * rank : (place + 1) * rank, :] = jnp.where(inside, inner, 0.0).astype(
+            jnp.bfloat16
+        )
+    left = spread[...]
+    for j in range(chunks):
+        copies[j].wait()
+        product = jnp.dot(left, grad_buf[j], preferred_element_type=jnp.float32)
+        for place in range(places):
+            out_ref[place, :, j * width : (j + 1) * width] = product[
+                place * rank : (place + 1) * rank
+            ]
+
+
+def clip_kernel(
+    n_dp, n_ctx, docs, inc_ref, own_ref, mine_ref, other_ref, send_ref, keep_ref, norm_ref
+):
+    rank, features = own_ref.shape
+    depth = bits_of(docs)
+    span = features // n_dp
+    slab = span // 2
+    places = n_ctx // 2
+    width = slab // places
+    document = document_of(my_bits(n_ctx)[:depth], [0] * depth)
+    flag = jnp.int32(0)
+    for k in range(docs):
+        flag = flag + jnp.where(k == document, inc_ref[0, k], 0)
+    other = other_ref[...].astype(jnp.float32)
+    whole = mine_ref[...].astype(jnp.float32) + other
+    norm = jnp.sqrt(jnp.sum(whole * whole, keepdims=True))
+    factor = flag.astype(jnp.float32) * clip_norm / jnp.maximum(norm, clip_norm)
+    clipped = (own_ref[...] + other) * factor
+    me = lax.axis_index("ctx")
+    upper = me // places == 1
+    low = lax.rem(me, places)
+    dp = lax.axis_index("dp")
+    core, chip = lax.rem(dp, 2), dp // 2
+    halves = []
+    for d in range(n_dp):
+        base = d * span
+        halves.append(
+            jnp.where(
+                upper, clipped[:, base + slab : base + span], clipped[:, base : base + slab]
+            )
+        )
+    for target, ref in ((0, keep_ref), (1, send_ref)):
+        for x in range(n_dp // 2):
+            piece = jnp.where(core == target, halves[2 * x], halves[2 * x + 1])
+            for q in range(places):
+                ref[chip ^ x, low ^ q] = piece[:, q * width : (q + 1) * width]
+    rows = lax.broadcasted_iota(jnp.int32, norm_ref.shape, 1)
+    norm_ref[...] = jnp.where(rows == document, jnp.reshape(norm, (1, 1, 1)), 0.0)
+
+
+def exchange(block, n_dp, n_ctx, even_bit, odd_bit):
+    route = [
+        (d * n_ctx + c, d * n_ctx + (c ^ (1 << (odd_bit if d % 2 else even_bit))))
+        for d in range(n_dp)
+        for c in range(n_ctx)
+    ]
+    return lax.ppermute(block, ("dp", "ctx"), route)
+
+
+def swap_dp(block, n_dp, bit):
+    return lax.ppermute(block, "dp", [(d, d ^ (1 << bit)) for d in range(n_dp)])
+
+
+def halving_plan(out_grad, adapter_inner, doc_lengths, slab_offset, included):
+    n_dp, n_ctx = lax.axis_size("dp"), lax.axis_size("ctx")
+    rows, features = out_grad.shape
+    rank = adapter_inner.shape[1]
+    docs = doc_lengths.shape[1]
+    f32 = jnp.float32
+    vmem = pl.BlockSpec(memory_space=pltpu.VMEM)
+    smem = pl.BlockSpec(memory_space=pltpu.SMEM)
+    places = docs // 2
+    chunks = max(1, features // 768)
+
+    def partials(flip):
+        return pl.pallas_call(
+            functools.partial(partials_kernel, flip, n_ctx, docs, chunks),
+            out_shape=jax.ShapeDtypeStruct((places, rank, features), f32),
+            in_specs=[smem, smem, vmem, pl.BlockSpec(memory_space=pl.ANY)],
+            out_specs=vmem,
+            scratch_shapes=[
+                pltpu.VMEM((chunks, rows, features // chunks), jnp.bfloat16),
+                pltpu.VMEM((places * rank, rows), jnp.bfloat16),
+                pltpu.SemaphoreType.DMA((chunks,)),
+            ],
+            cost_estimate=pl.CostEstimate(
+                flops=2 * places * rank * rows * features,
+                bytes_accessed=2 * rows * features,
+                transcendentals=0,
+            ),
+        )(doc_lengths, slab_offset, adapter_inner.T, out_grad)
+
+    even, odd = halving_orders(n_ctx)
+    rounds = list(zip(even, odd))
+    received = exchange(partials(1), n_dp, n_ctx, *rounds[0])
+    keep = partials(0)
+    for e, o in rounds[1:-1]:
+        places //= 2
+        send = keep[places:] + received[places:]
+        keep = keep[:places] + received[:places]
+        received = exchange(send, n_dp, n_ctx, e, o)
+    own = keep[0] + received[0]
+    mine = own.astype(jnp.bfloat16)
+    other = exchange(mine, n_dp, n_ctx, *rounds[-1])
+    places = n_ctx // 2
+    width = features // (n_dp * n_ctx)
+    pieces = jax.ShapeDtypeStruct((n_dp // 2, places, rank, width), f32)
+    send, keep, norms = pl.pallas_call(
+        functools.partial(clip_kernel, n_dp, n_ctx, docs),
+        out_shape=[pieces, pieces, jax.ShapeDtypeStruct((1, rank, width), f32)],
+        in_specs=[smem, vmem, vmem, vmem],
+        out_specs=[vmem, vmem, vmem],
+    )(included, own, mine, other)
+    total = keep + swap_dp(send, n_dp, 0)
+    total = total[0] + swap_dp(total[1], n_dp, 1)
+    for bit in reversed(range(bits_of(places))):
+        places //= 2
+        received = exchange(jnp.concatenate([total[places:], norms]), n_dp, n_ctx, bit, bit)
+        total = total[:places] + received[:places]
+        norms = norms + received[places:]
+    return (total[0].T, norms[:, :docs, 0])
+
+
+def on_device(out_grad, adapter_inner, doc_lengths, slab_offset, included):
+    n_dp, n_ctx = lax.axis_size("dp"), lax.axis_size("ctx")
+    halving = (
+        n_dp == 4
+        and n_ctx >= 4
+        and n_ctx & (n_ctx - 1) == 0
+        and 2 * doc_lengths.shape[1] == n_ctx
+        and doc_lengths.shape[1] <= adapter_inner.shape[1]
+        and out_grad.shape[1] % 768 == 0
+    )
+    plan = halving_plan if halving else chain_plan
+    return plan(out_grad, adapter_inner, doc_lengths, slab_offset, included)
+
+
 def solution(mesh):
     placed = (P(("dp", "ctx"), None), P(("dp", "ctx"), None), P("dp", None), P("dp"), P("dp", None))
     return jax.shard_map(

time: 184 us -> 55.8 us (0.30)
  waiting for transfers between devices: 114 us -> 23.7 us
  between operations: 19.9 us -> 1.33 us
  matrix products: 17.2 us -> 0 us
  blocking collectives: 17.1 us -> 0 us
  Pallas kernels: 0 us -> 11 us
  starting transfers between devices: 3.16 us -> 12.2 us
  local copies, waits for them, and re-layouts: 4.78 us -> 0.69 us
    unnamed x2 -> x0, waiting for transfers between devices: 97.6 us -> none
    dot_general x7 -> x0, matrix products: 17.2 us -> none  [the longest x1 6.49 us: pair_terms(): jnp.einsum('id,jd->ij', left_grad, right_grad, preferred_element_type=jnp...]
    psum x1 -> x0, blocking collectives: 17.1 us -> none  [on_device(): squares = lax.psum(norm_terms, 'ctx')]
    pallas_call x0 -> x3, Pallas kernels: none -> 11 us  [the longest x2 8.74 us: partials(): pl.pallas_call(functools.partial(partials_kernel, flip, n_ctx, docs, chun...]
    ppermute x3 -> x7, starting transfers between devices: 3.13 us -> 12.2 us  [the longest x5 10.6 us: exchange(): return lax.ppermute(block, ('dp', 'ctx'), route)]
    ppermute x3 -> x7, waiting for transfers between devices: 16.4 us -> 23.7 us  [the longest x5 19.4 us: exchange(): return lax.ppermute(block, ('dp', 'ctx'), route)]
    reduce_sum x4 -> x0, other arithmetic: 3.4 us -> none  [the longest x1 1.94 us: document_ids(): doc_shift = jnp.sum(jnp.where(labels == longest, starts, 0)) + offset]
    unnamed x6 -> x4, local copies, waits for them, and re-layouts: 3.68 us -> 0.67 us
  transfers between devices with their start and end apart: 4 -> 7, of which waited for: 4 -> 7; matrix products, arithmetic and copies ran while one was open for 6% -> 0% of each run, Pallas kernels for 0% -> 8%
where the time goes in v2:
time: 55.8 us; the launch traced here: 55.2 us
  waiting for transfers between devices  23.7 us (42%)
  starting transfers between devices  12.2 us (22%)
  Pallas kernels  11 us (20%)
  other arithmetic  6.37 us (11%)
  between operations  1.33 us (2%)
  local copies, waits for them, and re-layouts  0.69 us (1%)
    ppermute x5, waiting for transfers between devices, exchange(): return lax.ppermute(block, ('dp', 'ctx'), route)  19.4 us
    ppermute x5, starting transfers between devices, exchange(): return lax.ppermute(block, ('dp', 'ctx'), route)  10.6 us
    pallas_call x2, Pallas kernels, partials(): pl.pallas_call(functools.partial(partials_kernel, flip, n_ctx, docs, chun...  8.74 us
    ppermute x2, waiting for transfers between devices, swap_dp(): return lax.ppermute(block, 'dp', [(d, d ^ 1 << bit) for d in range(n_dp)])  4.28 us
    pallas_call x1, Pallas kernels, halving_plan(): pl.pallas_call(functools.partial(clip_kernel, n_dp, n_ctx, docs), out_sha...  2.22 us
    convert_element_type x1, other arithmetic, halving_plan(): mine = own.astype(jnp.bfloat16)  1.75 us
    ppermute x2, starting transfers between devices, swap_dp(): return lax.ppermute(block, 'dp', [(d, d ^ 1 << bit) for d in range(n_dp)])  1.61 us
  transfers between devices with their start and end apart: 7, of which 7 were waited for; matrix products, arithmetic and copies ran while one was open for 0% of the time, Pallas kernels for 8%

profile of v2, /device:TPU:0, one launch (start us, length us, event | category | flops | bytes accessed | tf_op | source)
XLA Modules:
  0.0 55.2 jit_solution(11674705768714377083)
XLA Ops:
  1.3 4.4 %shard_map.69 = f32[2,16,4608]{2,1,0:T(8,128)} custom-call(s32[1,4]{1,0:T(1,128)} %len_ref.3, s32[1]{0:T(128)S(6)} %copy.7.off_ref, bf16[16,512]{1,0:T(8,128)(2,1)} %bitcast.15, bf16[512,4608]{1,0:T(8,128)(2,1)} %grad_hbm.3), custom_call_target="tpu_custom_call" | custom-call | flops 150994944 | bytes 4718592 | tf_op jit(solution)/shard_map/pallas_call | solution.py:272
  5.7 3.1 %collective-permute-start = (f32[2,16,4608]{2,1,0:T(8,128)}, f32[2,16,4608]{2,1,0:T(8,128)S(1)}, u32[]{:S(2)}, u32[]{:S(2)}) collective-permute-start(f32[2,16,4608]{2,1,0:T(8,128)} %shard_map.69), channel_id=1, source_target_pairs={{0,1},{1,0},{2,3},{3,2},{4,5},{5,4},{6,7},{7,6},{8,10},{9,11},{10,... | collective-permute-start | bytes 1769480 | tf_op jit(solution)/shard_map/ppermute | solution.py:253
  8.7 4.4 %shard_map.68 = f32[2,16,4608]{2,1,0:T(8,128)} custom-call(s32[1,4]{1,0:T(1,128)} %len_ref.3, s32[1]{0:T(128)S(6)} %copy.7.off_ref, bf16[16,512]{1,0:T(8,128)(2,1)} %bitcast.16, bf16[512,4608]{1,0:T(8,128)(2,1)} %grad_hbm.3), custom_call_target="tpu_custom_call" | custom-call | flops 150994944 | bytes 4718592 | tf_op jit(solution)/shard_map/pallas_call | solution.py:272
  13.1 3.7 %collective-permute-done = f32[2,16,4608]{2,1,0:T(8,128)S(1)} collective-permute-done((f32[2,16,4608]{2,1,0:T(8,128)}, f32[2,16,4608]{2,1,0:T(8,128)S(1)}, u32[]{:S(2)}, u32[]{:S(2)}) %collective-permute-start) | collective-permute-done | bytes 589856 | tf_op jit(solution)/shard_map/ppermute | solution.py:253
  16.8 1.0 %slice_add_fusion = f32[1,16,4608]{2,1,0:T(8,128)S(1)} fusion(f32[2,16,4608]{2,1,0:T(8,128)S(1)} %collective-permute-done, f32[2,16,4608]{2,1,0:T(8,128)} %shard_map.68), kind=kLoop, calls=%fused_computation | loop fusion | flops 73728 | bytes 884736 | tf_op jit(solution)/shard_map/add | solution.py:295
  17.8 2.1 %collective-permute-start.1 = (f32[1,16,4608]{2,1,0:T(8,128)S(1)}, f32[1,16,4608]{2,1,0:T(8,128)S(1)}, u32[]{:S(2)}, u32[]{:S(2)}) collective-permute-start(f32[1,16,4608]{2,1,0:T(8,128)S(1)} %slice_add_fusion), channel_id=1, source_target_pairs={{0,2},{1,3},{2,0},{3,1},{4,6},{5,7},{6,4},{7,5},{8,9},{9,8},{10,11... | collective-permute-start | bytes 884744 | tf_op jit(solution)/shard_map/ppermute | solution.py:253
  19.9 4.7 %collective-permute-done.1 = f32[1,16,4608]{2,1,0:T(8,128)S(1)} collective-permute-done((f32[1,16,4608]{2,1,0:T(8,128)S(1)}, f32[1,16,4608]{2,1,0:T(8,128)S(1)}, u32[]{:S(2)}, u32[]{:S(2)}) %collective-permute-start.1) | collective-permute-done | bytes 294944 | tf_op jit(solution)/shard_map/ppermute | solution.py:253
  24.6 1.7 %fusion.5 = (bf16[16,4608]{1,0:T(8,128)(2,1)S(1)}, f32[16,4608]{1,0:T(8,128)}) fusion(f32[1,16,4608]{2,1,0:T(8,128)S(1)} %collective-permute-done.1, f32[2,16,4608]{2,1,0:T(8,128)S(1)} %collective-permute-done, f32[2,16,4608]{2,1,0:T(8,128)} %shard_map.68), kind=kLoop, calls=%fused_computation.15 | loop fusion | flops 221184 | bytes 1327104 | tf_op jit(solution)/shard_map/convert_element_type | solution.py:299
  26.4 3.0 %collective-permute-start.2 = (bf16[16,4608]{1,0:T(8,128)(2,1)S(1)}, bf16[16,4608]{1,0:T(8,128)(2,1)S(1)}, u32[]{:S(2)}, u32[]{:S(2)}) collective-permute-start(bf16[16,4608]{1,0:T(8,128)(2,1)S(1)} %get-tuple-element.8.mine_ref), channel_id=1, source_target_pairs={{0,4},{1,5},{2,6},{3,7},{4,0},{5,1},{6,2},{7,3},{8,12},{9,13},{10,... | collective-permute-start | bytes 442376 | tf_op jit(solution)/shard_map/ppermute | solution.py:253
  29.4 5.3 %collective-permute-done.2.other_ref = bf16[16,4608]{1,0:T(8,128)(2,1)S(1)} collective-permute-done((bf16[16,4608]{1,0:T(8,128)(2,1)S(1)}, bf16[16,4608]{1,0:T(8,128)(2,1)S(1)}, u32[]{:S(2)}, u32[]{:S(2)}) %collective-permute-start.2) | collective-permute-done | bytes 147488 | tf_op jit(solution)/shard_map/ppermute | solution.py:253
  34.7 0.7 %copy-done.1 = bf16[16,4608]{1,0:T(8,128)(2,1)} copy-done((bf16[16,4608]{1,0:T(8,128)(2,1)}, bf16[16,4608]{1,0:T(8,128)(2,1)S(1)}, u32[]{:S(2)}) %copy-start.1) | copy-done | bytes 147480
  35.4 2.2 %shard_map.70 = (f32[2,4,16,144]{3,2,1,0:T(8,128)}, f32[2,4,16,144]{3,2,1,0:T(8,128)}, f32[1,16,144]{2,1,0:T(8,128)}) custom-call(s32[1,4]{1,0:T(1,128)} %inc_ref.1, f32[16,4608]{1,0:T(8,128)} %get-tuple-element.9.own_ref, bf16[16,4608]{1,0:T(8,128)(2,1)} %copy-done, bf16[16,4608]{1,0:T(8,128)(2,1)} %copy-done.1), custom_call_target="tpu_custom_call" | custom-call | tf_op jit(solution)/shard_map/pallas_call | solution.py:304
  37.6 1.6 %collective-permute-done.3 = f32[2,4,16,144]{3,2,1,0:T(8,128)S(1)} collective-permute-done((f32[2,4,16,144]{3,2,1,0:T(8,128)}, f32[2,4,16,144]{3,2,1,0:T(8,128)S(1)}, u32[]{:S(2)}, u32[]{:S(2)}) %collective-permute-start.3) | collective-permute-done | bytes 73760 | tf_op jit(solution)/shard_map/ppermute | solution.py:257
  39.2 0.9 %add.33 = f32[2,4,16,144]{3,2,1,0:T(8,128)S(1)} add(f32[2,4,16,144]{3,2,1,0:T(8,128)} %get-tuple-element.5, f32[2,4,16,144]{3,2,1,0:T(8,128)S(1)} %collective-permute-done.3) | non-fusion elementwise | flops 18432 | bytes 221184 | tf_op jit(solution)/shard_map/add | solution.py:310
  40.1 1.6 %collective-permute-start.4 = (f32[4,16,144]{2,1,0:T(8,128)S(1)}, f32[4,16,144]{2,1,0:T(8,128)S(1)}, u32[]{:S(2)}, u32[]{:S(2)}) collective-permute-start(f32[4,16,144]{2,1,0:T(8,128)S(1)} %slice_bitcast_fusion), channel_id=1, source_target_pairs={{0,16},{8,24},{16,0},{24,8},{1,17},{9,25},{17,1},{25,9},{2,18},{10... | collective-permute-start | bytes 110600 | tf_op jit(solution)/shard_map/ppermute | solution.py:257
  41.7 2.7 %collective-permute-done.4 = f32[4,16,144]{2,1,0:T(8,128)S(1)} collective-permute-done((f32[4,16,144]{2,1,0:T(8,128)S(1)}, f32[4,16,144]{2,1,0:T(8,128)S(1)}, u32[]{:S(2)}, u32[]{:S(2)}) %collective-permute-start.4) | collective-permute-done | bytes 36896 | tf_op jit(solution)/shard_map/ppermute | solution.py:257
  44.5 0.7 %pad_maximum_fusion = f32[3,16,144]{2,1,0:T(8,128)S(1)} fusion(f32[1,16,144]{2,1,0:T(8,128)} %get-tuple-element.7, f32[2,16,144]{2,1,0:T(8,128)S(1)} %slice.67), kind=kLoop, calls=%fused_computation.7 | loop fusion | flops 6912 | bytes 55296 | tf_op jit(solution)/shard_map/concatenate | solution.py:314
  45.2 0.7 %collective-permute-start.5 = (f32[3,16,144]{2,1,0:T(8,128)S(1)}, f32[3,16,144]{2,1,0:T(8,128)S(1)}, u32[]{:S(2)}, u32[]{:S(2)}) collective-permute-start(f32[3,16,144]{2,1,0:T(8,128)S(1)} %pad_maximum_fusion), channel_id=1, source_target_pairs={{0,2},{1,3},{2,0},{3,1},{4,6},{5,7},{6,4},{7,5},{8,10},{9,11},{10,... | collective-permute-start | bytes 82952 | tf_op jit(solution)/shard_map/ppermute | solution.py:253
  45.9 3.4 %collective-permute-done.5 = f32[3,16,144]{2,1,0:T(8,128)S(1)} collective-permute-done((f32[3,16,144]{2,1,0:T(8,128)S(1)}, f32[3,16,144]{2,1,0:T(8,128)S(1)}, u32[]{:S(2)}, u32[]{:S(2)}) %collective-permute-start.5) | collective-permute-done | bytes 27680 | tf_op jit(solution)/shard_map/ppermute | solution.py:253
  49.3 0.7 %slice_add_fusion.4 = f32[1,16,144]{2,1,0:T(8,128)S(1)} fusion(f32[1,16,144]{2,1,0:T(8,128)} %get-tuple-element.7, f32[3,16,144]{2,1,0:T(8,128)S(1)} %collective-permute-done.5), kind=kLoop, calls=%fused_computation.12 | loop fusion | flops 2304 | bytes 27648 | tf_op jit(solution)/shard_map/add | solution.py:316
  50.0 1.6 %collective-permute-start.6 = (f32[2,16,144]{2,1,0:T(8,128)S(1)}, f32[2,16,144]{2,1,0:T(8,128)S(1)}, u32[]{:S(2)}, u32[]{:S(2)}) collective-permute-start(f32[2,16,144]{2,1,0:T(8,128)S(1)} %pad_maximum_fusion.1), channel_id=1, source_target_pairs={{0,1},{1,0},{2,3},{3,2},{4,5},{5,4},{6,7},{7,6},{8,9},{9,8},{10,11... | collective-permute-start | bytes 55304 | tf_op jit(solution)/shard_map/ppermute | solution.py:253
  51.7 2.3 %collective-permute-done.6 = f32[2,16,144]{2,1,0:T(8,128)S(1)} collective-permute-done((f32[2,16,144]{2,1,0:T(8,128)S(1)}, f32[2,16,144]{2,1,0:T(8,128)S(1)}, u32[]{:S(2)}, u32[]{:S(2)}) %collective-permute-start.6) | collective-permute-done | bytes 18464 | tf_op jit(solution)/shard_map/ppermute | solution.py:253
  54.0 0.6 %fusion.7 = (f32[1,16,144]{2,1,0:T(8,128)S(1)}, f32[144,16]{0,1:T(8,128)}) fusion(f32[2,16,144]{2,1,0:T(8,128)S(1)} %collective-permute-done.6, f32[2,16,144]{2,1,0:T(8,128)S(1)} %slice_add_fusion.2), kind=kLoop, calls=%fused_computation.16 | loop fusion | flops 2304 | bytes 46080 | tf_op jit(solution)/shard_map/slice | solution.py:316
  54.6 0.6 %fusion.4 = f32[4]{0:T(128)} fusion(f32[1,16,144]{2,1,0:T(8,128)S(1)} %get-tuple-element.10, f32[1,16,144]{2,1,0:T(8,128)S(1)} %slice_add_fusion.4), kind=kLoop, calls=%fused_computation.14 | loop fusion | flops 4 | bytes 48 | tf_op jit(solution)/shard_map/slice | solution.py:317
  (10 shorter events, 0.0 us)
Async XLA Ops:
  5.7 11.1 %collective-permute-start = (f32[2,16,4608]{2,1,0:T(8,128)}, f32[2,16,4608]{2,1,0:T(8,128)S(1)}, u32[]{:S(2)}, u32[]{:S(2)}) collective-permute-start(f32[2,16,4608]{2,1,0:T(8,128)} %shard_map.69), channel_id=1, source_target_pairs={{0,1},{1,0},{2,3},{3,2},{4,5},{5,4},{6,7},{7,6},{8,10},{9,11},{10,... | collective-permute-start | bytes 1769480 | tf_op jit(solution)/shard_map/ppermute | solution.py:253
  17.8 6.8 %collective-permute-start.1 = (f32[1,16,4608]{2,1,0:T(8,128)S(1)}, f32[1,16,4608]{2,1,0:T(8,128)S(1)}, u32[]{:S(2)}, u32[]{:S(2)}) collective-permute-start(f32[1,16,4608]{2,1,0:T(8,128)S(1)} %slice_add_fusion), channel_id=1, source_target_pairs={{0,2},{1,3},{2,0},{3,1},{4,6},{5,7},{6,4},{7,5},{8,9},{9,8},{10,11... | collective-permute-start | bytes 884744 | tf_op jit(solution)/shard_map/ppermute | solution.py:253
  26.4 8.3 %copy-start = (bf16[16,4608]{1,0:T(8,128)(2,1)}, bf16[16,4608]{1,0:T(8,128)(2,1)S(1)}, u32[]{:S(2)}) copy-start(bf16[16,4608]{1,0:T(8,128)(2,1)S(1)} %get-tuple-element.8.mine_ref) | copy-start | bytes 442372
  26.4 8.3 %collective-permute-start.2 = (bf16[16,4608]{1,0:T(8,128)(2,1)S(1)}, bf16[16,4608]{1,0:T(8,128)(2,1)S(1)}, u32[]{:S(2)}, u32[]{:S(2)}) collective-permute-start(bf16[16,4608]{1,0:T(8,128)(2,1)S(1)} %get-tuple-element.8.mine_ref), channel_id=1, source_target_pairs={{0,4},{1,5},{2,6},{3,7},{4,0},{5,1},{6,2},{7,3},{8,12},{9,13},{10,... | collective-permute-start | bytes 442376 | tf_op jit(solution)/shard_map/ppermute | solution.py:253
  34.7 0.7 %copy-start.1 = (bf16[16,4608]{1,0:T(8,128)(2,1)}, bf16[16,4608]{1,0:T(8,128)(2,1)S(1)}, u32[]{:S(2)}) copy-start(bf16[16,4608]{1,0:T(8,128)(2,1)S(1)} %collective-permute-done.2.other_ref) | copy-start | bytes 442372
  37.6 1.6 %collective-permute-start.3 = (f32[2,4,16,144]{3,2,1,0:T(8,128)}, f32[2,4,16,144]{3,2,1,0:T(8,128)S(1)}, u32[]{:S(2)}, u32[]{:S(2)}) collective-permute-start(f32[2,4,16,144]{3,2,1,0:T(8,128)} %get-tuple-element.6), channel_id=1, source_target_pairs={{0,8},{8,0},{16,24},{24,16},{1,9},{9,1},{17,25},{25,17},{2,10},{10... | collective-permute-start | bytes 221192 | tf_op jit(solution)/shard_map/ppermute | solution.py:257
  40.1 4.3 %collective-permute-start.4 = (f32[4,16,144]{2,1,0:T(8,128)S(1)}, f32[4,16,144]{2,1,0:T(8,128)S(1)}, u32[]{:S(2)}, u32[]{:S(2)}) collective-permute-start(f32[4,16,144]{2,1,0:T(8,128)S(1)} %slice_bitcast_fusion), channel_id=1, source_target_pairs={{0,16},{8,24},{16,0},{24,8},{1,17},{9,25},{17,1},{25,9},{2,18},{10... | collective-permute-start | bytes 110600 | tf_op jit(solution)/shard_map/ppermute | solution.py:257
  45.2 4.1 %collective-permute-start.5 = (f32[3,16,144]{2,1,0:T(8,128)S(1)}, f32[3,16,144]{2,1,0:T(8,128)S(1)}, u32[]{:S(2)}, u32[]{:S(2)}) collective-permute-start(f32[3,16,144]{2,1,0:T(8,128)S(1)} %pad_maximum_fusion), channel_id=1, source_target_pairs={{0,2},{1,3},{2,0},{3,1},{4,6},{5,7},{6,4},{7,5},{8,10},{9,11},{10,... | collective-permute-start | bytes 82952 | tf_op jit(solution)/shard_map/ppermute | solution.py:253
  50.0 4.0 %collective-permute-start.6 = (f32[2,16,144]{2,1,0:T(8,128)S(1)}, f32[2,16,144]{2,1,0:T(8,128)S(1)}, u32[]{:S(2)}, u32[]{:S(2)}) collective-permute-start(f32[2,16,144]{2,1,0:T(8,128)S(1)} %pad_maximum_fusion.1), channel_id=1, source_target_pairs={{0,1},{1,0},{2,3},{3,2},{4,5},{5,4},{6,7},{7,6},{8,9},{9,8},{10,11... | collective-permute-start | bytes 55304 | tf_op jit(solution)/shard_map/ppermute | solution.py:253

commit v3 on v2

--- a/solution.py
+++ b/solution.py
@@ -157,17 +157,25 @@
 
 
 def partials_kernel(
-    flip, n_ctx, docs, chunks, len_ref, off_ref, inner_ref, grad_hbm, out_ref, grad_buf, spread, sems
+    flip, n_ctx, docs, chunks, len_hbm, off_hbm, inner_hbm, grad_hbm, out_ref, grad_buf, inner_ref, spread, len_ref, off_ref, small_sems, sems
 ):
     rank, rows = inner_ref.shape
     width = grad_hbm.shape[1] // chunks
-    copies = []
-    for j in range(chunks):
-        copy = pltpu.make_async_copy(
+    small = [
+        pltpu.make_async_copy(len_hbm, len_ref, small_sems.at[0]),
+        pltpu.make_async_copy(off_hbm, off_ref, small_sems.at[1]),
+        pltpu.make_async_copy(inner_hbm, inner_ref, small_sems.at[2]),
+    ]
+    copies = [
+        pltpu.make_async_copy(
             grad_hbm.at[:, pl.ds(j * width, width)], grad_buf.at[j], sems.at[j]
         )
+        for j in range(chunks)
+    ]
+    for copy in small + copies:
         copy.start()
-        copies.append(copy)
+    for copy in small:
+        copy.wait()
     total = n_ctx * rows
     running = jnp.int32(0)
     longest, best = jnp.int32(0), len_ref[0, 0]
@@ -204,6 +212,33 @@
             ]
 
 
+def fold_kernel(keep_ref, recv_ref, send_ref, left_ref):
+    half = keep_ref.shape[0] // 2
+    send_ref[...] = keep_ref[half:] + recv_ref[half:]
+    left_ref[...] = keep_ref[:half] + recv_ref[:half]
+
+
+def round_kernel(keep_ref, recv_ref, own_ref, mine_ref):
+    own = keep_ref[0] + recv_ref[0]
+    own_ref[...] = own
+    mine_ref[...] = own.astype(jnp.bfloat16)
+
+
+def swapped(pieces, bit):
+    half = len(pieces) // 2
+    low, high = pieces[:half], pieces[half:]
+    first = [jnp.where(bit == 1, b, a) for a, b in zip(low, high)]
+    second = [jnp.where(bit == 1, a, b) for a, b in zip(low, high)]
+    return first, second
+
+
+def relative(pieces, low):
+    if len(pieces) == 1:
+        return pieces
+    first, second = swapped(pieces, (low >> (bits_of(len(pieces)) - 1)) & 1)
+    return relative(first, low) + relative(second, low)
+
+
 def clip_kernel(
     n_dp, n_ctx, docs, inc_ref, own_ref, mine_ref, other_ref, send_ref, keep_ref, norm_ref
 ):
@@ -238,10 +273,48 @@
     for target, ref in ((0, keep_ref), (1, send_ref)):
         for x in range(n_dp // 2):
             piece = jnp.where(core == target, halves[2 * x], halves[2 * x + 1])
-            for q in range(places):
-                ref[chip ^ x, low ^ q] = piece[:, q * width : (q + 1) * width]
-    rows = lax.broadcasted_iota(jnp.int32, norm_ref.shape, 1)
-    norm_ref[...] = jnp.where(rows == document, jnp.reshape(norm, (1, 1, 1)), 0.0)
+            pieces = relative([piece[:, q * width : (q + 1) * width] for q in range(places)], low)
+            ref[chip ^ x] = jnp.concatenate(pieces, axis=1)
+    rows = lax.broadcasted_iota(jnp.int32, norm_ref.shape, 0)
+    norm_ref[...] = jnp.where(rows == document, norm, 0.0)
+
+
+def core_kernel(keep_ref, recv_ref, send_ref):
+    send_ref[...] = keep_ref[1] + recv_ref[1]
+
+
+def with_norms(block, norms, send_ref):
+    width = block.shape[1]
+    spare = send_ref.shape[1] - width
+    send_ref[...] = jnp.concatenate([block, norms[:, :spare]], axis=1)
+
+
+def chip_kernel(keep_ref, core_ref, recv_ref, norm_ref, send_ref, left_ref):
+    total = keep_ref[0] + core_ref[0] + recv_ref[...]
+    half = total.shape[1] // 2
+    left_ref[...] = total[:, :half]
+    with_norms(total[:, half:], norm_ref[...], send_ref)
+
+
+def step_kernel(keep_ref, recv_ref, norm_ref, send_ref, left_ref, norms_ref):
+    width = keep_ref.shape[1]
+    half = width // 2
+    received = recv_ref[...]
+    total = keep_ref[...] + received[:, :width]
+    norms = norm_ref[...] + received[:, width : width + 1]
+    left_ref[...] = total[:, :half]
+    norms_ref[...] = norms
+    with_norms(total[:, half:], norms, send_ref)
+
+
+def last_kernel(docs, keep_ref, recv_ref, norm_ref, out_ref, norms_ref):
+    width = keep_ref.shape[1]
+    received = recv_ref[...]
+    out_ref[...] = keep_ref[...] + received[:, :width]
+    norms = norm_ref[...] + received[:, width : width + 1]
+    rows = lax.broadcasted_iota(jnp.int32, norms.shape, 0)
+    lanes = lax.broadcasted_iota(jnp.int32, norms.shape, 1)
+    norms_ref[...] = jnp.sum(jnp.where(rows == lanes, norms, 0.0), axis=0, keepdims=True)[:, :docs]
 
 
 def exchange(block, n_dp, n_ctx, even_bit, odd_bit):
@@ -257,6 +330,17 @@
     return lax.ppermute(block, "dp", [(d, d ^ (1 << bit)) for d in range(n_dp)])
 
 
+def in_vmem(kernel, shapes, *operands, scalars=()):
+    vmem = pl.BlockSpec(memory_space=pltpu.VMEM)
+    smem = pl.BlockSpec(memory_space=pltpu.SMEM)
+    return pl.pallas_call(
+        kernel,
+        out_shape=[pltpu.VMEM(shape, dtype) for shape, dtype in shapes],
+        in_specs=[smem] * len(scalars) + [vmem] * len(operands),
+        out_specs=[vmem] * len(shapes),
+    )(*scalars, *[pltpu.with_memory_space_constraint(x, pltpu.VMEM) for x in operands])
+
+
 def halving_plan(out_grad, adapter_inner, doc_lengths, slab_offset, included):
     n_dp, n_ctx = lax.axis_size("dp"), lax.axis_size("ctx")
     rows, features = out_grad.shape
@@ -264,19 +348,23 @@
     docs = doc_lengths.shape[1]
     f32 = jnp.float32
     vmem = pl.BlockSpec(memory_space=pltpu.VMEM)
-    smem = pl.BlockSpec(memory_space=pltpu.SMEM)
+    hbm = pl.BlockSpec(memory_space=pl.ANY)
     places = docs // 2
     chunks = max(1, features // 768)
 
     def partials(flip):
         return pl.pallas_call(
             functools.partial(partials_kernel, flip, n_ctx, docs, chunks),
-            out_shape=jax.ShapeDtypeStruct((places, rank, features), f32),
-            in_specs=[smem, smem, vmem, pl.BlockSpec(memory_space=pl.ANY)],
+            out_shape=pltpu.VMEM((places, rank, features), f32),
+            in_specs=[hbm, hbm, hbm, hbm],
             out_specs=vmem,
             scratch_shapes=[
                 pltpu.VMEM((chunks, rows, features // chunks), jnp.bfloat16),
+                pltpu.VMEM((rank, rows), jnp.bfloat16),
                 pltpu.VMEM((places * rank, rows), jnp.bfloat16),
+                pltpu.SMEM(doc_lengths.shape, jnp.int32),
+                pltpu.SMEM(slab_offset.shape, jnp.int32),
+                pltpu.SemaphoreType.DMA((3,)),
                 pltpu.SemaphoreType.DMA((chunks,)),
             ],
             cost_estimate=pl.CostEstimate(
@@ -292,29 +380,52 @@
     keep = partials(0)
     for e, o in rounds[1:-1]:
         places //= 2
-        send = keep[places:] + received[places:]
-        keep = keep[:places] + received[:places]
+        shape = ((places, rank, features), f32)
+        send, keep = in_vmem(fold_kernel, [shape, shape], keep, received)
         received = exchange(send, n_dp, n_ctx, e, o)
-    own = keep[0] + received[0]
-    mine = own.astype(jnp.bfloat16)
+    own, mine = in_vmem(
+        round_kernel,
+        [((rank, features), f32), ((rank, features), jnp.bfloat16)],
+        keep,
+        received,
+    )
     other = exchange(mine, n_dp, n_ctx, *rounds[-1])
-    places = n_ctx // 2
-    width = features // (n_dp * n_ctx)
-    pieces = jax.ShapeDtypeStruct((n_dp // 2, places, rank, width), f32)
-    send, keep, norms = pl.pallas_call(
+    slab = features // (2 * n_dp)
+    pieces = ((n_dp // 2, rank, slab), f32)
+    column = ((rank, 128), f32)
+    send, keep, norms = in_vmem(
         functools.partial(clip_kernel, n_dp, n_ctx, docs),
-        out_shape=[pieces, pieces, jax.ShapeDtypeStruct((1, rank, width), f32)],
-        in_specs=[smem, vmem, vmem, vmem],
-        out_specs=[vmem, vmem, vmem],
-    )(included, own, mine, other)
-    total = keep + swap_dp(send, n_dp, 0)
-    total = total[0] + swap_dp(total[1], n_dp, 1)
-    for bit in reversed(range(bits_of(places))):
-        places //= 2
-        received = exchange(jnp.concatenate([total[places:], norms]), n_dp, n_ctx, bit, bit)
-        total = total[:places] + received[:places]
-        norms = norms + received[places:]
-    return (total[0].T, norms[:, :docs, 0])
+        [pieces, pieces, column],
+        own,
+        mine,
+        other,
+        scalars=(included,),
+    )
+    core = swap_dp(send, n_dp, 0)
+    (send,) = in_vmem(core_kernel, [((rank, slab), f32)], keep, core)
+    received = swap_dp(send, n_dp, 1)
+
+    def shapes(width):
+        return [((rank, width // 128 * 128 + 128), f32), ((rank, width), f32)]
+
+    width = slab // 2
+    steps = list(reversed(range(bits_of(n_ctx // 2))))
+    send, keep = in_vmem(chip_kernel, shapes(width), keep, core, received, norms)
+    for bit in steps[:-1]:
+        width //= 2
+        received = exchange(send, n_dp, n_ctx, bit, bit)
+        send, keep, norms = in_vmem(step_kernel, shapes(width) + [column], keep, received, norms)
+    received = exchange(send, n_dp, n_ctx, steps[-1], steps[-1])
+    result, norms = pl.pallas_call(
+        functools.partial(last_kernel, docs),
+        out_shape=[
+            jax.ShapeDtypeStruct((rank, width), f32),
+            jax.ShapeDtypeStruct((1, docs), f32),
+        ],
+        in_specs=[vmem] * 3,
+        out_specs=[vmem, vmem],
+    )(*[pltpu.with_memory_space_constraint(x, pltpu.VMEM) for x in (keep, received, norms)])
+    return (result.T, norms)
 
 
 def on_device(out_grad, adapter_inner, doc_lengths, slab_offset, included):

time: 55.8 us -> 46.6 us (0.84)
  other arithmetic: 6.37 us -> 0 us
  Pallas kernels: 11 us -> 9.65 us
  local copies, waits for them, and re-layouts: 0.69 us -> 0 us
  waiting for transfers between devices: 23.7 us -> 23.1 us
    add x5 -> x0, other arithmetic: 2.66 us -> none  [the longest x1 0.99 us: halving_plan(): send = keep[places:] + received[places:]]
    convert_element_type x1 -> x0, other arithmetic: 1.75 us -> none  [halving_plan(): mine = own.astype(jnp.bfloat16)]
    pallas_call x2, Pallas kernels: 8.74 us -> 7.42 us  [partials(): pl.pallas_call(functools.partial(partials_kernel, flip, n_ctx, docs, chun...]
    slice x2 -> x0, other arithmetic: 1.24 us -> none  [the longest x1 0.63 us: halving_plan(): return (total[0].T, norms[:, :docs, 0])]
    concatenate x2 -> x0, other arithmetic: 0.73 us -> none  [halving_plan(): jnp.concatenate([total[places:], norms])]
    unnamed x4 -> x0, local copies, waits for them, and re-layouts: 0.67 us -> none
    pallas_call x1 -> x7, Pallas kernels: 2.22 us -> 2.22 us  [the longest x6 1.61 us: in_vmem(): pl.pallas_call(kernel, out_shape=[pltpu.VMEM(shape, dtype) for shape, dty...]
where the time goes in v3:
time: 46.6 us; the launch traced here: 46.4 us
  waiting for transfers between devices  23.1 us (50%)
  starting transfers between devices  12.3 us (26%)
  Pallas kernels  9.65 us (21%)
  between operations  1.32 us (3%)
    ppermute x5, waiting for transfers between devices, exchange(): return lax.ppermute(block, ('dp', 'ctx'), route)  19.4 us
    ppermute x5, starting transfers between devices, exchange(): return lax.ppermute(block, ('dp', 'ctx'), route)  10.6 us
    pallas_call x2, Pallas kernels, partials(): pl.pallas_call(functools.partial(partials_kernel, flip, n_ctx, docs, chun...  7.42 us
    ppermute x2, waiting for transfers between devices, swap_dp(): return lax.ppermute(block, 'dp', [(d, d ^ 1 << bit) for d in range(n_dp)])  3.72 us
    ppermute x2, starting transfers between devices, swap_dp(): return lax.ppermute(block, 'dp', [(d, d ^ 1 << bit) for d in range(n_dp)])  1.67 us
    pallas_call x6, Pallas kernels, in_vmem(): pl.pallas_call(kernel, out_shape=[pltpu.VMEM(shape, dtype) for shape, dty...  1.61 us
  transfers between devices with their start and end apart: 7, of which 7 were waited for; matrix products, arithmetic and copies ran while one was open for 0% of the time, Pallas kernels for 8%

profile of v3, /device:TPU:0, one launch (start us, length us, event | category | flops | bytes accessed | tf_op | source)
XLA Modules:
  0.0 46.4 jit_solution(399127457680294537)
XLA Ops:
  1.3 3.7 %shard_map.69 = f32[2,16,4608]{2,1,0:T(8,128)S(1)} custom-call(s32[1,4]{1,0:T(1,128)} %len_hbm.3, s32[1]{0:T(128)S(6)} %copy.7.off_hbm, bf16[16,512]{1,0:T(8,128)(2,1)} %bitcast.2, bf16[512,4608]{1,0:T(8,128)(2,1)} %grad_hbm.3), custom_call_target="tpu_custom_call" | custom-call | flops 150994944 | bytes 4718592 | tf_op jit(solution)/shard_map/pallas_call | solution.py:356
  5.0 3.1 %collective-permute-start = (f32[2,16,4608]{2,1,0:T(8,128)S(1)}, f32[2,16,4608]{2,1,0:T(8,128)S(1)}, u32[]{:S(2)}, u32[]{:S(2)}) collective-permute-start(f32[2,16,4608]{2,1,0:T(8,128)S(1)} %shard_map.69), channel_id=1, source_target_pairs={{0,1},{1,0},{2,3},{3,2},{4,5},{5,4},{6,7},{7,6},{8,10},{9,11},{10,... | collective-permute-start | bytes 1769480 | tf_op jit(solution)/shard_map/ppermute | solution.py:326
  8.1 3.7 %shard_map.68.keep_ref = f32[2,16,4608]{2,1,0:T(8,128)S(1)} custom-call(s32[1,4]{1,0:T(1,128)} %len_hbm.3, s32[1]{0:T(128)S(6)} %copy.7.off_hbm, bf16[16,512]{1,0:T(8,128)(2,1)} %bitcast.3, bf16[512,4608]{1,0:T(8,128)(2,1)} %grad_hbm.3), custom_call_target="tpu_custom_call" | custom-call | flops 150994944 | bytes 4718592 | tf_op jit(solution)/shard_map/pallas_call | solution.py:356
  11.8 4.1 %collective-permute-done.recv_ref = f32[2,16,4608]{2,1,0:T(8,128)S(1)} collective-permute-done((f32[2,16,4608]{2,1,0:T(8,128)S(1)}, f32[2,16,4608]{2,1,0:T(8,128)S(1)}, u32[]{:S(2)}, u32[]{:S(2)}) %collective-permute-start) | collective-permute-done | bytes 589856 | tf_op jit(solution)/shard_map/ppermute | solution.py:326
  15.9 0.1 shard_map.70
  16.0 2.1 %collective-permute-start.1 = (f32[1,16,4608]{2,1,0:T(8,128)S(1)}, f32[1,16,4608]{2,1,0:T(8,128)S(1)}, u32[]{:S(2)}, u32[]{:S(2)}) collective-permute-start(f32[1,16,4608]{2,1,0:T(8,128)S(1)} %get-tuple-element.17), channel_id=1, source_target_pairs={{0,2},{1,3},{2,0},{3,1},{4,6},{5,7},{6,4},{7,5},{8,9},{9,8},{10,11... | collective-permute-start | bytes 884744 | tf_op jit(solution)/shard_map/ppermute | solution.py:326
  18.1 4.7 %collective-permute-done.1.recv_ref = f32[1,16,4608]{2,1,0:T(8,128)S(1)} collective-permute-done((f32[1,16,4608]{2,1,0:T(8,128)S(1)}, f32[1,16,4608]{2,1,0:T(8,128)S(1)}, u32[]{:S(2)}, u32[]{:S(2)}) %collective-permute-start.1) | collective-permute-done | bytes 294944 | tf_op jit(solution)/shard_map/ppermute | solution.py:326
  22.9 3.1 %collective-permute-start.2 = (bf16[16,4608]{1,0:T(8,128)(2,1)S(1)}, bf16[16,4608]{1,0:T(8,128)(2,1)S(1)}, u32[]{:S(2)}, u32[]{:S(2)}) collective-permute-start(bf16[16,4608]{1,0:T(8,128)(2,1)S(1)} %get-tuple-element.19.mine_ref), channel_id=1, source_target_pairs={{0,4},{1,5},{2,6},{3,7},{4,0},{5,1},{6,2},{7,3},{8,12},{9,13},{10,... | collective-permute-start | bytes 442376 | tf_op jit(solution)/shard_map/ppermute | solution.py:326
  26.0 5.3 %collective-permute-done.2.other_ref = bf16[16,4608]{1,0:T(8,128)(2,1)S(1)} collective-permute-done((bf16[16,4608]{1,0:T(8,128)(2,1)S(1)}, bf16[16,4608]{1,0:T(8,128)(2,1)S(1)}, u32[]{:S(2)}, u32[]{:S(2)}) %collective-permute-start.2) | collective-permute-done | bytes 147488 | tf_op jit(solution)/shard_map/ppermute | solution.py:326
  31.3 1.3 %shard_map.72 = (f32[2,16,576]{2,1,0:T(8,128)S(1)}, f32[2,16,576]{2,1,0:T(8,128)S(1)}, f32[16,128]{1,0:T(8,128)S(1)}) custom-call(s32[1,4]{1,0:T(1,128)} %inc_ref.1, f32[16,4608]{1,0:T(8,128)S(1)} %get-tuple-element.18.own_ref, bf16[16,4608]{1,0:T(8,128)(2,1)S(1)} %get-tuple-element.19.mine_ref, bf16[16,4608]{1,0:T(8,128)(2,1)S(1)} %collective-permute-done.2.other_ref), custom_call_target="tpu_custom_call" | custom-call | tf_op jit(solution)/shard_map/pallas_call | solution.py:336
  32.6 0.1 collective-permute-start.3
  32.6 1.3 %collective-permute-done.3.recv_ref.core_ref = f32[2,16,576]{2,1,0:T(8,128)S(1)} collective-permute-done((f32[2,16,576]{2,1,0:T(8,128)S(1)}, f32[2,16,576]{2,1,0:T(8,128)S(1)}, u32[]{:S(2)}, u32[]{:S(2)}) %collective-permute-start.3) | collective-permute-done | bytes 73760 | tf_op jit(solution)/shard_map/ppermute | solution.py:330
  33.9 1.6 %collective-permute-start.4 = (f32[16,576]{1,0:T(8,128)S(1)}, f32[16,576]{1,0:T(8,128)S(1)}, u32[]{:S(2)}, u32[]{:S(2)}) collective-permute-start(f32[16,576]{1,0:T(8,128)S(1)} %shard_map.73), channel_id=1, source_target_pairs={{0,16},{8,24},{16,0},{24,8},{1,17},{9,25},{17,1},{25,9},{2,18},{10... | collective-permute-start | bytes 110600 | tf_op jit(solution)/shard_map/ppermute | solution.py:330
  35.5 2.5 %collective-permute-done.4.recv_ref = f32[16,576]{1,0:T(8,128)S(1)} collective-permute-done((f32[16,576]{1,0:T(8,128)S(1)}, f32[16,576]{1,0:T(8,128)S(1)}, u32[]{:S(2)}, u32[]{:S(2)}) %collective-permute-start.4) | collective-permute-done | bytes 36896 | tf_op jit(solution)/shard_map/ppermute | solution.py:330
  38.0 0.1 shard_map.74
  38.1 0.7 %collective-permute-start.5 = (f32[16,384]{1,0:T(8,128)S(1)}, f32[16,384]{1,0:T(8,128)S(1)}, u32[]{:S(2)}, u32[]{:S(2)}) collective-permute-start(f32[16,384]{1,0:T(8,128)S(1)} %get-tuple-element.24), channel_id=1, source_target_pairs={{0,2},{1,3},{2,0},{3,1},{4,6},{5,7},{6,4},{7,5},{8,10},{9,11},{10,... | collective-permute-start | bytes 73736 | tf_op jit(solution)/shard_map/ppermute | solution.py:326
  38.8 3.1 %collective-permute-done.5.recv_ref = f32[16,384]{1,0:T(8,128)S(1)} collective-permute-done((f32[16,384]{1,0:T(8,128)S(1)}, f32[16,384]{1,0:T(8,128)S(1)}, u32[]{:S(2)}, u32[]{:S(2)}) %collective-permute-start.5) | collective-permute-done | bytes 24608 | tf_op jit(solution)/shard_map/ppermute | solution.py:326
  41.9 0.1 shard_map.75
  42.0 1.6 %collective-permute-start.6 = (f32[16,256]{1,0:T(8,128)S(1)}, f32[16,256]{1,0:T(8,128)S(1)}, u32[]{:S(2)}, u32[]{:S(2)}) collective-permute-start(f32[16,256]{1,0:T(8,128)S(1)} %get-tuple-element.26), channel_id=1, source_target_pairs={{0,1},{1,0},{2,3},{3,2},{4,5},{5,4},{6,7},{7,6},{8,9},{9,8},{10,11... | collective-permute-start | bytes 49160 | tf_op jit(solution)/shard_map/ppermute | solution.py:326
  43.6 2.2 %collective-permute-done.6.recv_ref = f32[16,256]{1,0:T(8,128)S(1)} collective-permute-done((f32[16,256]{1,0:T(8,128)S(1)}, f32[16,256]{1,0:T(8,128)S(1)}, u32[]{:S(2)}, u32[]{:S(2)}) %collective-permute-start.6) | collective-permute-done | bytes 16416 | tf_op jit(solution)/shard_map/ppermute | solution.py:326
  45.8 0.6 %shard_map.76 = (f32[16,144]{1,0:T(8,128)}, f32[1,4]{1,0:T(1,128)}) custom-call(f32[16,144]{1,0:T(8,128)S(1)} %get-tuple-element.25.keep_ref, f32[16,256]{1,0:T(8,128)S(1)} %collective-permute-done.6.recv_ref, f32[16,128]{1,0:T(8,128)S(1)} %get-tuple-element.27.norm_ref), custom_call_target="tpu_custom_call" | custom-call | tf_op jit(solution)/shard_map/pallas_call | solution.py:419
  (2 shorter events, 0.0 us)
Async XLA Ops:
  5.0 10.9 %collective-permute-start = (f32[2,16,4608]{2,1,0:T(8,128)S(1)}, f32[2,16,4608]{2,1,0:T(8,128)S(1)}, u32[]{:S(2)}, u32[]{:S(2)}) collective-permute-start(f32[2,16,4608]{2,1,0:T(8,128)S(1)} %shard_map.69), channel_id=1, source_target_pairs={{0,1},{1,0},{2,3},{3,2},{4,5},{5,4},{6,7},{7,6},{8,10},{9,11},{10,... | collective-permute-start | bytes 1769480 | tf_op jit(solution)/shard_map/ppermute | solution.py:326
  16.0 6.8 %collective-permute-start.1 = (f32[1,16,4608]{2,1,0:T(8,128)S(1)}, f32[1,16,4608]{2,1,0:T(8,128)S(1)}, u32[]{:S(2)}, u32[]{:S(2)}) collective-permute-start(f32[1,16,4608]{2,1,0:T(8,128)S(1)} %get-tuple-element.17), channel_id=1, source_target_pairs={{0,2},{1,3},{2,0},{3,1},{4,6},{5,7},{6,4},{7,5},{8,9},{9,8},{10,11... | collective-permute-start | bytes 884744 | tf_op jit(solution)/shard_map/ppermute | solution.py:326
  22.9 8.4 %collective-permute-start.2 = (bf16[16,4608]{1,0:T(8,128)(2,1)S(1)}, bf16[16,4608]{1,0:T(8,128)(2,1)S(1)}, u32[]{:S(2)}, u32[]{:S(2)}) collective-permute-start(bf16[16,4608]{1,0:T(8,128)(2,1)S(1)} %get-tuple-element.19.mine_ref), channel_id=1, source_target_pairs={{0,4},{1,5},{2,6},{3,7},{4,0},{5,1},{6,2},{7,3},{8,12},{9,13},{10,... | collective-permute-start | bytes 442376 | tf_op jit(solution)/shard_map/ppermute | solution.py:326
  32.6 1.3 %collective-permute-start.3 = (f32[2,16,576]{2,1,0:T(8,128)S(1)}, f32[2,16,576]{2,1,0:T(8,128)S(1)}, u32[]{:S(2)}, u32[]{:S(2)}) collective-permute-start(f32[2,16,576]{2,1,0:T(8,128)S(1)} %get-tuple-element.21), channel_id=1, source_target_pairs={{0,8},{8,0},{16,24},{24,16},{1,9},{9,1},{17,25},{25,17},{2,10},{10... | collective-permute-start | bytes 221192 | tf_op jit(solution)/shard_map/ppermute | solution.py:330
  33.9 4.1 %collective-permute-start.4 = (f32[16,576]{1,0:T(8,128)S(1)}, f32[16,576]{1,0:T(8,128)S(1)}, u32[]{:S(2)}, u32[]{:S(2)}) collective-permute-start(f32[16,576]{1,0:T(8,128)S(1)} %shard_map.73), channel_id=1, source_target_pairs={{0,16},{8,24},{16,0},{24,8},{1,17},{9,25},{17,1},{25,9},{2,18},{10... | collective-permute-start | bytes 110600 | tf_op jit(solution)/shard_map/ppermute | solution.py:330
  38.1 3.8 %collective-permute-start.5 = (f32[16,384]{1,0:T(8,128)S(1)}, f32[16,384]{1,0:T(8,128)S(1)}, u32[]{:S(2)}, u32[]{:S(2)}) collective-permute-start(f32[16,384]{1,0:T(8,128)S(1)} %get-tuple-element.24), channel_id=1, source_target_pairs={{0,2},{1,3},{2,0},{3,1},{4,6},{5,7},{6,4},{7,5},{8,10},{9,11},{10,... | collective-permute-start | bytes 73736 | tf_op jit(solution)/shard_map/ppermute | solution.py:326
  42.0 3.7 %collective-permute-start.6 = (f32[16,256]{1,0:T(8,128)S(1)}, f32[16,256]{1,0:T(8,128)S(1)}, u32[]{:S(2)}, u32[]{:S(2)}) collective-permute-start(f32[16,256]{1,0:T(8,128)S(1)} %get-tuple-element.26), channel_id=1, source_target_pairs={{0,1},{1,0},{2,3},{3,2},{4,5},{5,4},{6,7},{7,6},{8,9},{9,8},{10,11... | collective-permute-start | bytes 49160 | tf_op jit(solution)/shard_map/ppermute | solution.py:326

commit v4 on v3

--- a/solution.py
+++ b/solution.py
@@ -8,6 +8,7 @@
 from jax.sharding import PartitionSpec as P
 
 SPAN = 3
+PARTS = 2
 
 
 clip_norm = 128.0
@@ -157,18 +158,22 @@
 
 
 def partials_kernel(
-    flip, n_ctx, docs, chunks, len_hbm, off_hbm, inner_hbm, grad_hbm, out_ref, grad_buf, inner_ref, spread, len_ref, off_ref, small_sems, sems
+    half, n_ctx, docs, chunks, len_hbm, off_hbm, inc_hbm, inner_hbm, grad_hbm, *refs
 ):
+    send_ref, keep_ref, flag_ref, grad_buf, inner_ref, spread = refs[:6]
+    len_ref, off_ref, inc_ref, small_sems, sems = refs[6:]
     rank, rows = inner_ref.shape
-    width = grad_hbm.shape[1] // chunks
+    features = send_ref.shape[2]
+    width = features // chunks
     small = [
         pltpu.make_async_copy(len_hbm, len_ref, small_sems.at[0]),
         pltpu.make_async_copy(off_hbm, off_ref, small_sems.at[1]),
         pltpu.make_async_copy(inner_hbm, inner_ref, small_sems.at[2]),
+        pltpu.make_async_copy(inc_hbm, inc_ref, small_sems.at[3]),
     ]
     copies = [
         pltpu.make_async_copy(
-            grad_hbm.at[:, pl.ds(j * width, width)], grad_buf.at[j], sems.at[j]
+            grad_hbm.at[:, pl.ds(half * features + j * width, width)], grad_buf.at[j], sems.at[j]
         )
         for j in range(chunks)
     ]
@@ -184,30 +189,32 @@
         better = len_ref[0, k] > best
         longest = jnp.where(better, running, longest)
         best = jnp.where(better, len_ref[0, k], best)
-    shift = longest + off_ref[0]
+    shift = longest + off_ref[0, 0]
     packed = lax.axis_index("ctx") * rows + shift + lax.broadcasted_iota(jnp.int32, (rank, rows), 1)
     packed = jnp.where(packed >= total, packed - total, packed)
     inner = inner_ref[...].astype(jnp.float32)
-    bits = my_bits(n_ctx)
     depth = bits_of(docs)
-    places = docs // 2
-    for place in range(places):
-        flips = [flip] + [(place >> (depth - 2 - i)) & 1 for i in range(depth - 1)]
-        document = document_of(bits[:depth], flips)
-        start, length = jnp.int32(0), jnp.int32(0)
+    bits = my_bits(n_ctx)[:depth]
+    for place in range(docs):
+        document = document_of(bits, [(place >> (depth - 1 - i)) & 1 for i in range(depth)])
+        start, length, flag = jnp.int32(0), jnp.int32(0), jnp.int32(0)
         for k in range(docs):
             start = start + jnp.where(k < document, len_ref[0, k], 0)
             length = length + jnp.where(k == document, len_ref[0, k], 0)
+            flag = flag + jnp.where(k == document, inc_ref[0, k], 0)
         inside = (packed >= start) & (packed < start + length)
         spread[place * rank : (place + 1) * rank, :] = jnp.where(inside, inner, 0.0).astype(
             jnp.bfloat16
         )
+        if place == 0:
+            flag_ref[...] = jnp.full(flag_ref.shape, flag.astype(jnp.float32))
     left = spread[...]
     for j in range(chunks):
         copies[j].wait()
         product = jnp.dot(left, grad_buf[j], preferred_element_type=jnp.float32)
-        for place in range(places):
-            out_ref[place, :, j * width : (j + 1) * width] = product[
+        for place in range(docs):
+            ref = keep_ref if place < docs // 2 else send_ref
+            ref[place % (docs // 2), :, j * width : (j + 1) * width] = product[
                 place * rank : (place + 1) * rank
             ]
 
@@ -239,24 +246,24 @@
     return relative(first, low) + relative(second, low)
 
 
-def clip_kernel(
-    n_dp, n_ctx, docs, inc_ref, own_ref, mine_ref, other_ref, send_ref, keep_ref, norm_ref
-):
-    rank, features = own_ref.shape
+def clip_kernel(n_dp, n_ctx, docs, parts, *refs):
+    own_refs, mine_refs, other_refs = refs[:parts], refs[parts : 2 * parts], refs[2 * parts : 3 * parts]
+    flag_ref, send_ref, keep_ref, norm_ref = refs[3 * parts :]
     depth = bits_of(docs)
-    span = features // n_dp
-    slab = span // 2
+    slab = send_ref.shape[2]
+    span = 2 * slab
     places = n_ctx // 2
     width = slab // places
-    document = document_of(my_bits(n_ctx)[:depth], [0] * depth)
-    flag = jnp.int32(0)
-    for k in range(docs):
-        flag = flag + jnp.where(k == document, inc_ref[0, k], 0)
-    other = other_ref[...].astype(jnp.float32)
-    whole = mine_ref[...].astype(jnp.float32) + other
-    norm = jnp.sqrt(jnp.sum(whole * whole, keepdims=True))
-    factor = flag.astype(jnp.float32) * clip_norm / jnp.maximum(norm, clip_norm)
-    clipped = (own_ref[...] + other) * factor
+    square = None
+    wholes = []
+    for own_ref, mine_ref, other_ref in zip(own_refs, mine_refs, other_refs):
+        other = other_ref[...].astype(jnp.float32)
+        whole = mine_ref[...].astype(jnp.float32) + other
+        wholes.append(own_ref[...] + other)
+        term = jnp.sum(whole * whole, keepdims=True)
+        square = term if square is None else square + term
+    norm = jnp.sqrt(square)
+    factor = flag_ref[0:1, 0:1] * clip_norm / jnp.maximum(norm, clip_norm)
     me = lax.axis_index("ctx")
     upper = me // places == 1
     low = lax.rem(me, places)
@@ -264,17 +271,18 @@
     core, chip = lax.rem(dp, 2), dp // 2
     halves = []
     for d in range(n_dp):
-        base = d * span
+        whole = wholes[d * parts // n_dp]
+        base = d % (n_dp // parts) * span
         halves.append(
-            jnp.where(
-                upper, clipped[:, base + slab : base + span], clipped[:, base : base + slab]
-            )
+            jnp.where(upper, whole[:, base + slab : base + span], whole[:, base : base + slab])
+            * factor
         )
     for target, ref in ((0, keep_ref), (1, send_ref)):
         for x in range(n_dp // 2):
             piece = jnp.where(core == target, halves[2 * x], halves[2 * x + 1])
             pieces = relative([piece[:, q * width : (q + 1) * width] for q in range(places)], low)
             ref[chip ^ x] = jnp.concatenate(pieces, axis=1)
+    document = document_of(my_bits(n_ctx)[:depth], [0] * depth)
     rows = lax.broadcasted_iota(jnp.int32, norm_ref.shape, 0)
     norm_ref[...] = jnp.where(rows == document, norm, 0.0)
 
@@ -349,57 +357,62 @@
     f32 = jnp.float32
     vmem = pl.BlockSpec(memory_space=pltpu.VMEM)
     hbm = pl.BlockSpec(memory_space=pl.ANY)
-    places = docs // 2
-    chunks = max(1, features // 768)
-
-    def partials(flip):
+    parts = PARTS
+    part = features // parts
+    chunks = max(1, part // 768)
+    block = pltpu.VMEM((docs // 2, rank, part), f32)
+    column = ((rank, 128), f32)
+
+    def partials(half):
         return pl.pallas_call(
-            functools.partial(partials_kernel, flip, n_ctx, docs, chunks),
-            out_shape=pltpu.VMEM((places, rank, features), f32),
-            in_specs=[hbm, hbm, hbm, hbm],
-            out_specs=vmem,
+            functools.partial(partials_kernel, half, n_ctx, docs, chunks),
+            out_shape=[block, block, pltpu.VMEM(*column)],
+            in_specs=[hbm] * 5,
+            out_specs=[vmem] * 3,
             scratch_shapes=[
-                pltpu.VMEM((chunks, rows, features // chunks), jnp.bfloat16),
+                pltpu.VMEM((chunks, rows, part // chunks), jnp.bfloat16),
                 pltpu.VMEM((rank, rows), jnp.bfloat16),
-                pltpu.VMEM((places * rank, rows), jnp.bfloat16),
+                pltpu.VMEM((docs * rank, rows), jnp.bfloat16),
                 pltpu.SMEM(doc_lengths.shape, jnp.int32),
-                pltpu.SMEM(slab_offset.shape, jnp.int32),
-                pltpu.SemaphoreType.DMA((3,)),
+                pltpu.SMEM((1, 1), jnp.int32),
+                pltpu.SMEM(included.shape, jnp.int32),
+                pltpu.SemaphoreType.DMA((4,)),
                 pltpu.SemaphoreType.DMA((chunks,)),
             ],
             cost_estimate=pl.CostEstimate(
-                flops=2 * places * rank * rows * features,
-                bytes_accessed=2 * rows * features,
+                flops=2 * docs * rank * rows * part,
+                bytes_accessed=2 * rows * part,
                 transcendentals=0,
             ),
-        )(doc_lengths, slab_offset, adapter_inner.T, out_grad)
+        )(doc_lengths, slab_offset[:, None], included, adapter_inner.T, out_grad)
 
     even, odd = halving_orders(n_ctx)
     rounds = list(zip(even, odd))
-    received = exchange(partials(1), n_dp, n_ctx, *rounds[0])
-    keep = partials(0)
-    for e, o in rounds[1:-1]:
-        places //= 2
-        shape = ((places, rank, features), f32)
-        send, keep = in_vmem(fold_kernel, [shape, shape], keep, received)
-        received = exchange(send, n_dp, n_ctx, e, o)
-    own, mine = in_vmem(
-        round_kernel,
-        [((rank, features), f32), ((rank, features), jnp.bfloat16)],
-        keep,
-        received,
-    )
-    other = exchange(mine, n_dp, n_ctx, *rounds[-1])
+    owns, mines, others = [], [], []
+    for half in range(parts):
+        send, keep, flag = partials(half)
+        received = exchange(send, n_dp, n_ctx, *rounds[0])
+        places = docs // 2
+        for e, o in rounds[1:-1]:
+            places //= 2
+            shape = ((places, rank, part), f32)
+            send, keep = in_vmem(fold_kernel, [shape, shape], keep, received)
+            received = exchange(send, n_dp, n_ctx, e, o)
+        own, mine = in_vmem(
+            round_kernel, [((rank, part), f32), ((rank, part), jnp.bfloat16)], keep, received
+        )
+        owns.append(own)
+        mines.append(mine)
+        others.append(exchange(mine, n_dp, n_ctx, *rounds[-1]))
     slab = features // (2 * n_dp)
     pieces = ((n_dp // 2, rank, slab), f32)
-    column = ((rank, 128), f32)
     send, keep, norms = in_vmem(
-        functools.partial(clip_kernel, n_dp, n_ctx, docs),
+        functools.partial(clip_kernel, n_dp, n_ctx, docs, parts),
         [pieces, pieces, column],
-        own,
-        mine,
-        other,
-        scalars=(included,),
+        *owns,
+        *mines,
+        *others,
+        flag,
     )
     core = swap_dp(send, n_dp, 0)
     (send,) = in_vmem(core_kernel, [((rank, slab), f32)], keep, core)
@@ -436,7 +449,7 @@
         and n_ctx & (n_ctx - 1) == 0
         and 2 * doc_lengths.shape[1] == n_ctx
         and doc_lengths.shape[1] <= adapter_inner.shape[1]
-        and out_grad.shape[1] % 768 == 0
+        and out_grad.shape[1] % (768 * PARTS) == 0
     )
     plan = halving_plan if halving else chain_plan
     return plan(out_grad, adapter_inner, doc_lengths, slab_offset, included)

time: 46.6 us -> 43.3 us (0.929)
  starting transfers between devices: 12.3 us -> 17.9 us
  waiting for transfers between devices: 23.1 us -> 18.1 us
  Pallas kernels: 9.65 us -> 5.9 us
    ppermute x5 -> x8, starting transfers between devices: 10.6 us -> 16.2 us  [exchange(): return lax.ppermute(block, ('dp', 'ctx'), route)]
    ppermute x5 -> x8, waiting for transfers between devices: 19.4 us -> 14.3 us  [exchange(): return lax.ppermute(block, ('dp', 'ctx'), route)]
    pallas_call x2, Pallas kernels: 7.42 us -> 4.4 us  [partials(): pl.pallas_call(functools.partial(partials_kernel, half, n_ctx, docs, chun...]
    pallas_call x6 -> x8, Pallas kernels: 1.61 us -> 0.88 us  [in_vmem(): pl.pallas_call(kernel, out_shape=[pltpu.VMEM(shape, dtype) for shape, dty...]
  transfers between devices with their start and end apart: 7 -> 10, of which waited for: 7 -> 8; matrix products, arithmetic and copies ran while one was open for 0% -> 0% of each run, Pallas kernels for 8% -> 5%
where the time goes in v4:
time: 43.3 us; the launch traced here: 43.1 us
  waiting for transfers between devices  18.1 us (42%)
  starting transfers between devices  17.9 us (41%)
  Pallas kernels  5.9 us (14%)
  between operations  1.33 us (3%)
    ppermute x8, starting transfers between devices, exchange(): return lax.ppermute(block, ('dp', 'ctx'), route)  16.2 us
    ppermute x8, waiting for transfers between devices, exchange(): return lax.ppermute(block, ('dp', 'ctx'), route)  14.3 us
    pallas_call x2, Pallas kernels, partials(): pl.pallas_call(functools.partial(partials_kernel, half, n_ctx, docs, chun...  4.4 us
    ppermute x2, waiting for transfers between devices, swap_dp(): return lax.ppermute(block, 'dp', [(d, d ^ 1 << bit) for d in range(n_dp)])  3.79 us
    ppermute x2, starting transfers between devices, swap_dp(): return lax.ppermute(block, 'dp', [(d, d ^ 1 << bit) for d in range(n_dp)])  1.61 us
    pallas_call x8, Pallas kernels, in_vmem(): pl.pallas_call(kernel, out_shape=[pltpu.VMEM(shape, dtype) for shape, dty...  0.88 us
  transfers between devices with their start and end apart: 10, of which 8 were waited for; matrix products, arithmetic and copies ran while one was open for 0% of the time, Pallas kernels for 5%

profile of v4, /device:TPU:0, one launch (start us, length us, event | category | flops | bytes accessed | tf_op | source)
XLA Modules:
  0.0 43.1 jit_solution(13268292249997785750)
XLA Ops:
  1.3 2.4 %shard_map.68 = (f32[2,16,2304]{2,1,0:T(8,128)S(1)}, f32[2,16,2304]{2,1,0:T(8,128)S(1)}, f32[16,128]{1,0:T(8,128)}) custom-call(s32[1,4]{1,0:T(1,128)} %len_hbm.3, s32[1,1]{1,0:T(1,128)} %bitcast.3.off_hbm, s32[1,4]{1,0:T(1,128)} %inc_hbm.3, bf16[16,512]{1,0:T(8,128)(2,1)} %bitcast.5, bf16[512,4608]{1,0:T(8,128)(2,1)} %grad_hbm.3), custom_call_target="tpu_custom_call" | custom-call | flops 150994944 | bytes 2359296 | tf_op jit(solution)/shard_map/pallas_call | solution.py:367
  3.7 3.1 %collective-permute-start = (f32[2,16,2304]{2,1,0:T(8,128)S(1)}, f32[2,16,2304]{2,1,0:T(8,128)S(1)}, u32[]{:S(2)}, u32[]{:S(2)}) collective-permute-start(f32[2,16,2304]{2,1,0:T(8,128)S(1)} %get-tuple-element.26), channel_id=1, source_target_pairs={{0,1},{1,0},{2,3},{3,2},{4,5},{5,4},{6,7},{7,6},{8,10},{9,11},{10,... | collective-permute-start | bytes 884744 | tf_op jit(solution)/shard_map/ppermute | solution.py:334
  6.7 2.0 %shard_map.71 = (f32[2,16,2304]{2,1,0:T(8,128)S(1)}, f32[2,16,2304]{2,1,0:T(8,128)S(1)}, f32[16,128]{1,0:T(8,128)S(1)}) custom-call(s32[1,4]{1,0:T(1,128)} %len_hbm.3, s32[1,1]{1,0:T(1,128)} %bitcast.4.off_hbm, s32[1,4]{1,0:T(1,128)} %inc_hbm.3, bf16[16,512]{1,0:T(8,128)(2,1)} %bitcast.6, bf16[512,4608]{1,0:T(8,128)(2,1)} %grad_hbm.3), custom_call_target="tpu_custom_call" | custom-call | flops 150994944 | bytes 2359296 | tf_op jit(solution)/shard_map/pallas_call | solution.py:367
  8.8 0.1 collective-permute-start.2
  8.8 2.6 %collective-permute-done.recv_ref = f32[2,16,2304]{2,1,0:T(8,128)S(1)} collective-permute-done((f32[2,16,2304]{2,1,0:T(8,128)S(1)}, f32[2,16,2304]{2,1,0:T(8,128)S(1)}, u32[]{:S(2)}, u32[]{:S(2)}) %collective-permute-start) | collective-permute-done | bytes 294944 | tf_op jit(solution)/shard_map/ppermute | solution.py:334
  11.4 2.1 %collective-permute-start.1 = (f32[1,16,2304]{2,1,0:T(8,128)S(1)}, f32[1,16,2304]{2,1,0:T(8,128)S(1)}, u32[]{:S(2)}, u32[]{:S(2)}) collective-permute-start(f32[1,16,2304]{2,1,0:T(8,128)S(1)} %get-tuple-element.28), channel_id=1, source_target_pairs={{0,2},{1,3},{2,0},{3,1},{4,6},{5,7},{6,4},{7,5},{8,9},{9,8},{10,11... | collective-permute-start | bytes 442376 | tf_op jit(solution)/shard_map/ppermute | solution.py:334
  13.6 3.6 %collective-permute-done.2.recv_ref = f32[2,16,2304]{2,1,0:T(8,128)S(1)} collective-permute-done((f32[2,16,2304]{2,1,0:T(8,128)S(1)}, f32[2,16,2304]{2,1,0:T(8,128)S(1)}, u32[]{:S(2)}, u32[]{:S(2)}) %collective-permute-start.2) | collective-permute-done | bytes 294944 | tf_op jit(solution)/shard_map/ppermute | solution.py:334
  17.3 1.9 %collective-permute-start.3 = (f32[1,16,2304]{2,1,0:T(8,128)S(1)}, f32[1,16,2304]{2,1,0:T(8,128)S(1)}, u32[]{:S(2)}, u32[]{:S(2)}) collective-permute-start(f32[1,16,2304]{2,1,0:T(8,128)S(1)} %get-tuple-element.33), channel_id=1, source_target_pairs={{0,2},{1,3},{2,0},{3,1},{4,6},{5,7},{6,4},{7,5},{8,9},{9,8},{10,11... | collective-permute-start | bytes 442376 | tf_op jit(solution)/shard_map/ppermute | solution.py:334
  19.2 2.7 %collective-permute-start.4 = (bf16[16,2304]{1,0:T(8,128)(2,1)S(1)}, bf16[16,2304]{1,0:T(8,128)(2,1)S(1)}, u32[]{:S(2)}, u32[]{:S(2)}) collective-permute-start(bf16[16,2304]{1,0:T(8,128)(2,1)S(1)} %get-tuple-element.35.refs_2_), channel_id=1, source_target_pairs={{0,4},{1,5},{2,6},{3,7},{4,0},{5,1},{6,2},{7,3},{8,12},{9,13},{10,... | collective-permute-start | bytes 221192 | tf_op jit(solution)/shard_map/ppermute | solution.py:334
  21.9 0.9 %collective-permute-done.3.recv_ref = f32[1,16,2304]{2,1,0:T(8,128)S(1)} collective-permute-done((f32[1,16,2304]{2,1,0:T(8,128)S(1)}, f32[1,16,2304]{2,1,0:T(8,128)S(1)}, u32[]{:S(2)}, u32[]{:S(2)}) %collective-permute-start.3) | collective-permute-done | bytes 147488 | tf_op jit(solution)/shard_map/ppermute | solution.py:334
  22.8 3.2 %collective-permute-start.5 = (bf16[16,2304]{1,0:T(8,128)(2,1)S(1)}, bf16[16,2304]{1,0:T(8,128)(2,1)S(1)}, u32[]{:S(2)}, u32[]{:S(2)}) collective-permute-start(bf16[16,2304]{1,0:T(8,128)(2,1)S(1)} %get-tuple-element.36.refs_3_), channel_id=1, source_target_pairs={{0,4},{1,5},{2,6},{3,7},{4,0},{5,1},{6,2},{7,3},{8,12},{9,13},{10,... | collective-permute-start | bytes 221192 | tf_op jit(solution)/shard_map/ppermute | solution.py:334
  26.0 2.3 %collective-permute-done.5.refs_5_ = bf16[16,2304]{1,0:T(8,128)(2,1)S(1)} collective-permute-done((bf16[16,2304]{1,0:T(8,128)(2,1)S(1)}, bf16[16,2304]{1,0:T(8,128)(2,1)S(1)}, u32[]{:S(2)}, u32[]{:S(2)}) %collective-permute-start.5) | collective-permute-done | bytes 73760 | tf_op jit(solution)/shard_map/ppermute | solution.py:334
  28.3 0.6 %shard_map.74 = (f32[2,16,576]{2,1,0:T(8,128)S(1)}, f32[2,16,576]{2,1,0:T(8,128)S(1)}, f32[16,128]{1,0:T(8,128)S(1)}) custom-call(f32[16,2304]{1,0:T(8,128)S(1)} %get-tuple-element.29.refs_0_, f32[16,2304]{1,0:T(8,128)S(1)} %get-tuple-element.34.refs_1_, bf16[16,2304]{1,0:T(8,128)(2,1)S(1)} %get-tuple-element.35.refs_2_, ...), custom_call_target="tpu_custom_call" | custom-call | tf_op jit(solution)/shard_map/pallas_call | solution.py:344
  28.9 0.1 collective-permute-start.6
  29.0 1.3 %collective-permute-done.6.recv_ref.core_ref = f32[2,16,576]{2,1,0:T(8,128)S(1)} collective-permute-done((f32[2,16,576]{2,1,0:T(8,128)S(1)}, f32[2,16,576]{2,1,0:T(8,128)S(1)}, u32[]{:S(2)}, u32[]{:S(2)}) %collective-permute-start.6) | collective-permute-done | bytes 73760 | tf_op jit(solution)/shard_map/ppermute | solution.py:338
  30.2 1.5 %collective-permute-start.7 = (f32[16,576]{1,0:T(8,128)S(1)}, f32[16,576]{1,0:T(8,128)S(1)}, u32[]{:S(2)}, u32[]{:S(2)}) collective-permute-start(f32[16,576]{1,0:T(8,128)S(1)} %shard_map.75), channel_id=1, source_target_pairs={{0,16},{8,24},{16,0},{24,8},{1,17},{9,25},{17,1},{25,9},{2,18},{10... | collective-permute-start | bytes 110600 | tf_op jit(solution)/shard_map/ppermute | solution.py:338
  31.8 2.5 %collective-permute-done.7.recv_ref = f32[16,576]{1,0:T(8,128)S(1)} collective-permute-done((f32[16,576]{1,0:T(8,128)S(1)}, f32[16,576]{1,0:T(8,128)S(1)}, u32[]{:S(2)}, u32[]{:S(2)}) %collective-permute-start.7) | collective-permute-done | bytes 36896 | tf_op jit(solution)/shard_map/ppermute | solution.py:338
  34.3 0.1 shard_map.76
  34.4 2.5 %collective-permute-start.8 = (f32[16,384]{1,0:T(8,128)S(1)}, f32[16,384]{1,0:T(8,128)S(1)}, u32[]{:S(2)}, u32[]{:S(2)}) collective-permute-start(f32[16,384]{1,0:T(8,128)S(1)} %get-tuple-element.42), channel_id=1, source_target_pairs={{0,2},{1,3},{2,0},{3,1},{4,6},{5,7},{6,4},{7,5},{8,10},{9,11},{10,... | collective-permute-start | bytes 73736 | tf_op jit(solution)/shard_map/ppermute | solution.py:334
  36.8 1.8 %collective-permute-done.8.recv_ref = f32[16,384]{1,0:T(8,128)S(1)} collective-permute-done((f32[16,384]{1,0:T(8,128)S(1)}, f32[16,384]{1,0:T(8,128)S(1)}, u32[]{:S(2)}, u32[]{:S(2)}) %collective-permute-start.8) | collective-permute-done | bytes 24608 | tf_op jit(solution)/shard_map/ppermute | solution.py:334
  38.7 0.1 shard_map.77
  38.8 0.7 %collective-permute-start.9 = (f32[16,256]{1,0:T(8,128)S(1)}, f32[16,256]{1,0:T(8,128)S(1)}, u32[]{:S(2)}, u32[]{:S(2)}) collective-permute-start(f32[16,256]{1,0:T(8,128)S(1)} %get-tuple-element.44), channel_id=1, source_target_pairs={{0,1},{1,0},{2,3},{3,2},{4,5},{5,4},{6,7},{7,6},{8,9},{9,8},{10,11... | collective-permute-start | bytes 49160 | tf_op jit(solution)/shard_map/ppermute | solution.py:334
  39.5 3.0 %collective-permute-done.9.recv_ref = f32[16,256]{1,0:T(8,128)S(1)} collective-permute-done((f32[16,256]{1,0:T(8,128)S(1)}, f32[16,256]{1,0:T(8,128)S(1)}, u32[]{:S(2)}, u32[]{:S(2)}) %collective-permute-start.9) | collective-permute-done | bytes 16416 | tf_op jit(solution)/shard_map/ppermute | solution.py:334
  42.5 0.6 %shard_map.78 = (f32[16,144]{1,0:T(8,128)}, f32[1,4]{1,0:T(1,128)}) custom-call(f32[16,144]{1,0:T(8,128)S(1)} %get-tuple-element.43.keep_ref, f32[16,256]{1,0:T(8,128)S(1)} %collective-permute-done.9.recv_ref, f32[16,128]{1,0:T(8,128)S(1)} %get-tuple-element.45.norm_ref), custom_call_target="tpu_custom_call" | custom-call | tf_op jit(solution)/shard_map/pallas_call | solution.py:432
  (7 shorter events, 0.1 us)
Async XLA Ops:
  3.7 7.8 %collective-permute-start = (f32[2,16,2304]{2,1,0:T(8,128)S(1)}, f32[2,16,2304]{2,1,0:T(8,128)S(1)}, u32[]{:S(2)}, u32[]{:S(2)}) collective-permute-start(f32[2,16,2304]{2,1,0:T(8,128)S(1)} %get-tuple-element.26), channel_id=1, source_target_pairs={{0,1},{1,0},{2,3},{3,2},{4,5},{5,4},{6,7},{7,6},{8,10},{9,11},{10,... | collective-permute-start | bytes 884744 | tf_op jit(solution)/shard_map/ppermute | solution.py:334
  8.8 8.5 %collective-permute-start.2 = (f32[2,16,2304]{2,1,0:T(8,128)S(1)}, f32[2,16,2304]{2,1,0:T(8,128)S(1)}, u32[]{:S(2)}, u32[]{:S(2)}) collective-permute-start(f32[2,16,2304]{2,1,0:T(8,128)S(1)} %get-tuple-element.31), channel_id=1, source_target_pairs={{0,1},{1,0},{2,3},{3,2},{4,5},{5,4},{6,7},{7,6},{8,10},{9,11},{10,... | collective-permute-start | bytes 884744 | tf_op jit(solution)/shard_map/ppermute | solution.py:334
  11.4 7.7 %collective-permute-start.1 = (f32[1,16,2304]{2,1,0:T(8,128)S(1)}, f32[1,16,2304]{2,1,0:T(8,128)S(1)}, u32[]{:S(2)}, u32[]{:S(2)}) collective-permute-start(f32[1,16,2304]{2,1,0:T(8,128)S(1)} %get-tuple-element.28), channel_id=1, source_target_pairs={{0,2},{1,3},{2,0},{3,1},{4,6},{5,7},{6,4},{7,5},{8,9},{9,8},{10,11... | collective-permute-start | bytes 442376 | tf_op jit(solution)/shard_map/ppermute | solution.py:334
  17.3 5.5 %collective-permute-start.3 = (f32[1,16,2304]{2,1,0:T(8,128)S(1)}, f32[1,16,2304]{2,1,0:T(8,128)S(1)}, u32[]{:S(2)}, u32[]{:S(2)}) collective-permute-start(f32[1,16,2304]{2,1,0:T(8,128)S(1)} %get-tuple-element.33), channel_id=1, source_target_pairs={{0,2},{1,3},{2,0},{3,1},{4,6},{5,7},{6,4},{7,5},{8,9},{9,8},{10,11... | collective-permute-start | bytes 442376 | tf_op jit(solution)/shard_map/ppermute | solution.py:334
  19.2 6.8 %collective-permute-start.4 = (bf16[16,2304]{1,0:T(8,128)(2,1)S(1)}, bf16[16,2304]{1,0:T(8,128)(2,1)S(1)}, u32[]{:S(2)}, u32[]{:S(2)}) collective-permute-start(bf16[16,2304]{1,0:T(8,128)(2,1)S(1)} %get-tuple-element.35.refs_2_), channel_id=1, source_target_pairs={{0,4},{1,5},{2,6},{3,7},{4,0},{5,1},{6,2},{7,3},{8,12},{9,13},{10,... | collective-permute-start | bytes 221192 | tf_op jit(solution)/shard_map/ppermute | solution.py:334
  22.8 5.5 %collective-permute-start.5 = (bf16[16,2304]{1,0:T(8,128)(2,1)S(1)}, bf16[16,2304]{1,0:T(8,128)(2,1)S(1)}, u32[]{:S(2)}, u32[]{:S(2)}) collective-permute-start(bf16[16,2304]{1,0:T(8,128)(2,1)S(1)} %get-tuple-element.36.refs_3_), channel_id=1, source_target_pairs={{0,4},{1,5},{2,6},{3,7},{4,0},{5,1},{6,2},{7,3},{8,12},{9,13},{10,... | collective-permute-start | bytes 221192 | tf_op jit(solution)/shard_map/ppermute | solution.py:334
  28.9 1.3 %collective-permute-start.6 = (f32[2,16,576]{2,1,0:T(8,128)S(1)}, f32[2,16,576]{2,1,0:T(8,128)S(1)}, u32[]{:S(2)}, u32[]{:S(2)}) collective-permute-start(f32[2,16,576]{2,1,0:T(8,128)S(1)} %get-tuple-element.39), channel_id=1, source_target_pairs={{0,8},{8,0},{16,24},{24,16},{1,9},{9,1},{17,25},{25,17},{2,10},{10... | collective-permute-start | bytes 221192 | tf_op jit(solution)/shard_map/ppermute | solution.py:338
  30.2 4.1 %collective-permute-start.7 = (f32[16,576]{1,0:T(8,128)S(1)}, f32[16,576]{1,0:T(8,128)S(1)}, u32[]{:S(2)}, u32[]{:S(2)}) collective-permute-start(f32[16,576]{1,0:T(8,128)S(1)} %shard_map.75), channel_id=1, source_target_pairs={{0,16},{8,24},{16,0},{24,8},{1,17},{9,25},{17,1},{25,9},{2,18},{10... | collective-permute-start | bytes 110600 | tf_op jit(solution)/shard_map/ppermute | solution.py:338
  34.4 4.3 %collective-permute-start.8 = (f32[16,384]{1,0:T(8,128)S(1)}, f32[16,384]{1,0:T(8,128)S(1)}, u32[]{:S(2)}, u32[]{:S(2)}) collective-permute-start(f32[16,384]{1,0:T(8,128)S(1)} %get-tuple-element.42), channel_id=1, source_target_pairs={{0,2},{1,3},{2,0},{3,1},{4,6},{5,7},{6,4},{7,5},{8,10},{9,11},{10,... | collective-permute-start | bytes 73736 | tf_op jit(solution)/shard_map/ppermute | solution.py:334
  38.8 3.7 %collective-permute-start.9 = (f32[16,256]{1,0:T(8,128)S(1)}, f32[16,256]{1,0:T(8,128)S(1)}, u32[]{:S(2)}, u32[]{:S(2)}) collective-permute-start(f32[16,256]{1,0:T(8,128)S(1)} %get-tuple-element.44), channel_id=1, source_target_pairs={{0,1},{1,0},{2,3},{3,2},{4,5},{5,4},{6,7},{7,6},{8,9},{9,8},{10,11... | collective-permute-start | bytes 49160 | tf_op jit(solution)/shard_map/ppermute | solution.py:334

commit v5 on v4

--- a/solution.py
+++ b/solution.py
@@ -9,6 +9,7 @@
 
 SPAN = 3
 PARTS = 2
+LONGEST = 1536
 
 
 clip_norm = 128.0
@@ -141,20 +142,10 @@
     return even, odd
 
 
-def my_bits(n_ctx):
-    me = lax.axis_index("ctx")
+def bit_in_use(block, place, n_ctx):
     odd = lax.rem(lax.axis_index("dp"), 2) == 1
     even_order, odd_order = halving_orders(n_ctx)
-    return [
-        jnp.where(odd, (me >> o) & 1, (me >> e) & 1) for e, o in zip(even_order, odd_order)
-    ]
-
-
-def document_of(bits, flips):
-    document = jnp.int32(0)
-    for bit, flip in zip(bits, flips):
-        document = document * 2 + (bit ^ flip)
-    return document
+    return jnp.where(odd, (block >> odd_order[place]) & 1, (block >> even_order[place]) & 1)
 
 
 def partials_kernel(
@@ -163,7 +154,7 @@
     send_ref, keep_ref, flag_ref, grad_buf, inner_ref, spread = refs[:6]
     len_ref, off_ref, inc_ref, small_sems, sems = refs[6:]
     rank, rows = inner_ref.shape
-    features = send_ref.shape[2]
+    features = send_ref.shape[1]
     width = features // chunks
     small = [
         pltpu.make_async_copy(len_hbm, len_ref, small_sems.at[0]),
@@ -182,51 +173,80 @@
     for copy in small:
         copy.wait()
     total = n_ctx * rows
-    running = jnp.int32(0)
-    longest, best = jnp.int32(0), len_ref[0, 0]
+    me = lax.axis_index("ctx")
+    lengths = [len_ref[0, k] for k in range(docs)]
+    starts = [jnp.int32(0)]
     for k in range(1, docs):
-        running = running + len_ref[0, k - 1]
-        better = len_ref[0, k] > best
-        longest = jnp.where(better, running, longest)
-        best = jnp.where(better, len_ref[0, k], best)
+        starts.append(starts[-1] + lengths[k - 1])
+    longest, best = starts[0], lengths[0]
+    for k in range(1, docs):
+        better = lengths[k] > best
+        longest = jnp.where(better, starts[k], longest)
+        best = jnp.where(better, lengths[k], best)
     shift = longest + off_ref[0, 0]
-    packed = lax.axis_index("ctx") * rows + shift + lax.broadcasted_iota(jnp.int32, (rank, rows), 1)
+    firsts = []
+    for k in range(docs):
+        first = starts[k] - shift
+        firsts.append(jnp.where(first < 0, first + total, first))
+    flip = jnp.int32(0)
+    for k in range(docs):
+        block = lax.div(firsts[k], jnp.int32(rows))
+        offset = firsts[k] - block * rows
+        inside = (offset >= 1) & (offset + lengths[k] <= rows - 1)
+        flip = flip + jnp.where(inside, ((k + 1) & 1) ^ bit_in_use(block, 0, n_ctx), 0)
+    first_bit, second_bit = bit_in_use(me, 0, n_ctx), bit_in_use(me, 1, n_ctx)
+    even_order, odd_order = halving_orders(n_ctx)
+    odd = lax.rem(lax.axis_index("dp"), 2) == 1
+    other = me ^ jnp.where(odd, 1 << odd_order[0], 1 << even_order[0])
+
+    def wrapped(x):
+        return jnp.where(x < 0, x + total, x)
+
+    packed = me * rows + shift + lax.broadcasted_iota(jnp.int32, (rank, rows), 1)
     packed = jnp.where(packed >= total, packed - total, packed)
     inner = inner_ref[...].astype(jnp.float32)
-    depth = bits_of(docs)
-    bits = my_bits(n_ctx)[:depth]
-    for place in range(docs):
-        document = document_of(bits, [(place >> (depth - 1 - i)) & 1 for i in range(depth)])
-        start, length, flag = jnp.int32(0), jnp.int32(0), jnp.int32(0)
-        for k in range(docs):
-            start = start + jnp.where(k < document, len_ref[0, k], 0)
-            length = length + jnp.where(k == document, len_ref[0, k], 0)
-            flag = flag + jnp.where(k == document, inc_ref[0, k], 0)
-        inside = (packed >= start) & (packed < start + length)
-        spread[place * rank : (place + 1) * rank, :] = jnp.where(inside, inner, 0.0).astype(
-            jnp.bfloat16
-        )
-        if place == 0:
-            flag_ref[...] = jnp.full(flag_ref.shape, flag.astype(jnp.float32))
+    slots = [jnp.zeros_like(inner) for _ in range(3)]
+    weights = [jnp.int32(0)] * 2
+    flag = jnp.int32(0)
+    for k in range(docs):
+        mine = ((k & 1) ^ flip) == first_bit
+        near = (k >> 1) == second_bit
+        belongs = [mine & near, mine & jnp.logical_not(near), jnp.logical_not(mine)]
+        inside = (packed >= starts[k]) & (packed < starts[k] + lengths[k])
+        rows_of = jnp.where(inside, inner, 0.0)
+        for i in range(3):
+            slots[i] = slots[i] + jnp.where(belongs[i], 1.0, 0.0) * rows_of
+        ahead, behind = firsts[k] - other * rows, other * rows - firsts[k]
+        present = (wrapped(ahead) < rows) | (wrapped(behind) < lengths[k])
+        for i in range(2):
+            weights[i] = weights[i] + jnp.where(belongs[i] & present, 1, 0)
+        flag = flag + jnp.where(belongs[0], inc_ref[0, k], 0)
+    for i in range(3):
+        spread[i * rank : (i + 1) * rank, :] = slots[i].astype(jnp.bfloat16)
+    document = 2 * second_bit + (first_bit ^ flip)
+    line = lax.broadcasted_iota(jnp.int32, flag_ref.shape, 0)
+    facts = jnp.zeros(flag_ref.shape, jnp.float32)
+    for i, fact in enumerate([flag, weights[0], weights[1], document]):
+        facts = jnp.where(line == i, fact.astype(jnp.float32), facts)
+    flag_ref[...] = facts
     left = spread[...]
     for j in range(chunks):
         copies[j].wait()
         product = jnp.dot(left, grad_buf[j], preferred_element_type=jnp.float32)
-        for place in range(docs):
-            ref = keep_ref if place < docs // 2 else send_ref
-            ref[place % (docs // 2), :, j * width : (j + 1) * width] = product[
-                place * rank : (place + 1) * rank
-            ]
-
-
-def fold_kernel(keep_ref, recv_ref, send_ref, left_ref):
-    half = keep_ref.shape[0] // 2
-    send_ref[...] = keep_ref[half:] + recv_ref[half:]
-    left_ref[...] = keep_ref[:half] + recv_ref[:half]
+        columns = slice(j * width, (j + 1) * width)
+        keep_ref[0, :, columns] = product[:rank]
+        keep_ref[1, :, columns] = product[rank : 2 * rank]
+        send_ref[:, columns] = product[2 * rank :]
+
+
+def fold_kernel(keep_ref, recv_ref, fact_ref, send_ref, left_ref):
+    received = recv_ref[...]
+    send_ref[...] = keep_ref[1] + fact_ref[2:3, 0:1] * received
+    left_ref[...] = keep_ref[0] + fact_ref[1:2, 0:1] * received
 
 
 def round_kernel(keep_ref, recv_ref, own_ref, mine_ref):
-    own = keep_ref[0] + recv_ref[0]
+    own = keep_ref[...] + recv_ref[...]
     own_ref[...] = own
     mine_ref[...] = own.astype(jnp.bfloat16)
 
@@ -249,7 +269,6 @@
 def clip_kernel(n_dp, n_ctx, docs, parts, *refs):
     own_refs, mine_refs, other_refs = refs[:parts], refs[parts : 2 * parts], refs[2 * parts : 3 * parts]
     flag_ref, send_ref, keep_ref, norm_ref = refs[3 * parts :]
-    depth = bits_of(docs)
     slab = send_ref.shape[2]
     span = 2 * slab
     places = n_ctx // 2
@@ -282,9 +301,8 @@
             piece = jnp.where(core == target, halves[2 * x], halves[2 * x + 1])
             pieces = relative([piece[:, q * width : (q + 1) * width] for q in range(places)], low)
             ref[chip ^ x] = jnp.concatenate(pieces, axis=1)
-    document = document_of(my_bits(n_ctx)[:depth], [0] * depth)
-    rows = lax.broadcasted_iota(jnp.int32, norm_ref.shape, 0)
-    norm_ref[...] = jnp.where(rows == document, norm, 0.0)
+    rows = lax.broadcasted_iota(jnp.int32, norm_ref.shape, 0).astype(jnp.float32)
+    norm_ref[...] = jnp.where(rows == flag_ref[3:4, :], norm, 0.0)
 
 
 def core_kernel(keep_ref, recv_ref, send_ref):
@@ -360,19 +378,23 @@
     parts = PARTS
     part = features // parts
     chunks = max(1, part // 768)
-    block = pltpu.VMEM((docs // 2, rank, part), f32)
     column = ((rank, 128), f32)
+    single = ((rank, part), f32)
 
     def partials(half):
         return pl.pallas_call(
             functools.partial(partials_kernel, half, n_ctx, docs, chunks),
-            out_shape=[block, block, pltpu.VMEM(*column)],
+            out_shape=[
+                pltpu.VMEM(*single),
+                pltpu.VMEM((2, rank, part), f32),
+                pltpu.VMEM((8, 128), f32),
+            ],
             in_specs=[hbm] * 5,
             out_specs=[vmem] * 3,
             scratch_shapes=[
                 pltpu.VMEM((chunks, rows, part // chunks), jnp.bfloat16),
                 pltpu.VMEM((rank, rows), jnp.bfloat16),
-                pltpu.VMEM((docs * rank, rows), jnp.bfloat16),
+                pltpu.VMEM((3 * rank, rows), jnp.bfloat16),
                 pltpu.SMEM(doc_lengths.shape, jnp.int32),
                 pltpu.SMEM((1, 1), jnp.int32),
                 pltpu.SMEM(included.shape, jnp.int32),
@@ -380,7 +402,7 @@
                 pltpu.SemaphoreType.DMA((chunks,)),
             ],
             cost_estimate=pl.CostEstimate(
-                flops=2 * docs * rank * rows * part,
+                flops=2 * 3 * rank * rows * part,
                 bytes_accessed=2 * rows * part,
                 transcendentals=0,
             ),
@@ -392,14 +414,10 @@
     for half in range(parts):
         send, keep, flag = partials(half)
         received = exchange(send, n_dp, n_ctx, *rounds[0])
-        places = docs // 2
-        for e, o in rounds[1:-1]:
-            places //= 2
-            shape = ((places, rank, part), f32)
-            send, keep = in_vmem(fold_kernel, [shape, shape], keep, received)
-            received = exchange(send, n_dp, n_ctx, e, o)
+        send, keep = in_vmem(fold_kernel, [single, single], keep, received, flag)
+        received = exchange(send, n_dp, n_ctx, *rounds[1])
         own, mine = in_vmem(
-            round_kernel, [((rank, part), f32), ((rank, part), jnp.bfloat16)], keep, received
+            round_kernel, [single, ((rank, part), jnp.bfloat16)], keep, received
         )
         owns.append(own)
         mines.append(mine)
@@ -443,12 +461,14 @@
 
 def on_device(out_grad, adapter_inner, doc_lengths, slab_offset, included):
     n_dp, n_ctx = lax.axis_size("dp"), lax.axis_size("ctx")
+    docs = doc_lengths.shape[1]
+    rows = out_grad.shape[0]
     halving = (
         n_dp == 4
-        and n_ctx >= 4
-        and n_ctx & (n_ctx - 1) == 0
-        and 2 * doc_lengths.shape[1] == n_ctx
-        and doc_lengths.shape[1] <= adapter_inner.shape[1]
+        and docs == 4
+        and n_ctx == 2 * docs
+        and docs <= adapter_inner.shape[1]
+        and 2 * (rows - 2) + (docs - 2) * LONGEST < n_ctx * rows
         and out_grad.shape[1] % (768 * PARTS) == 0
     )
     plan = halving_plan if halving else chain_plan

time: 43.3 us -> 41 us (0.947)
  waiting for transfers between devices: 18.1 us -> 16.7 us
  starting transfers between devices: 17.9 us -> 17.2 us
    ppermute x8, waiting for transfers between devices: 14.3 us -> 12.9 us  [exchange(): return lax.ppermute(block, ('dp', 'ctx'), route)]
    ppermute x8, starting transfers between devices: 16.2 us -> 15.6 us  [exchange(): return lax.ppermute(block, ('dp', 'ctx'), route)]
where the time goes in v5:
time: 41 us; the launch traced here: 40.8 us
  starting transfers between devices  17.2 us (42%)
  waiting for transfers between devices  16.7 us (41%)
  Pallas kernels  5.6 us (14%)
  between operations  1.34 us (3%)
    ppermute x8, starting transfers between devices, exchange(): return lax.ppermute(block, ('dp', 'ctx'), route)  15.6 us
    ppermute x8, waiting for transfers between devices, exchange(): return lax.ppermute(block, ('dp', 'ctx'), route)  12.9 us
    pallas_call x2, Pallas kernels, partials(): pl.pallas_call(functools.partial(partials_kernel, half, n_ctx, docs, chun...  4.03 us
    ppermute x2, waiting for transfers between devices, swap_dp(): return lax.ppermute(block, 'dp', [(d, d ^ 1 << bit) for d in range(n_dp)])  3.79 us
    ppermute x2, starting transfers between devices, swap_dp(): return lax.ppermute(block, 'dp', [(d, d ^ 1 << bit) for d in range(n_dp)])  1.61 us
    pallas_call x8, Pallas kernels, in_vmem(): pl.pallas_call(kernel, out_shape=[pltpu.VMEM(shape, dtype) for shape, dty...  0.96 us
  transfers between devices with their start and end apart: 10, of which 8 were waited for; matrix products, arithmetic and copies ran while one was open for 0% of the time, Pallas kernels for 5%

profile of v5, /device:TPU:0, one launch (start us, length us, event | category | flops | bytes accessed | tf_op | source)
XLA Modules:
  0.0 40.8 jit_solution(12304137398084997486)
XLA Ops:
  1.3 2.0 %shard_map.68 = (f32[16,2304]{1,0:T(8,128)S(1)}, f32[2,16,2304]{2,1,0:T(8,128)S(1)}, f32[8,128]{1,0:T(8,128)S(1)}) custom-call(s32[1,4]{1,0:T(1,128)} %len_hbm.3, s32[1,1]{1,0:T(1,128)} %bitcast.3.off_hbm, s32[1,4]{1,0:T(1,128)} %inc_hbm.3, bf16[16,512]{1,0:T(8,128)(2,1)} %bitcast.5, bf16[512,4608]{1,0:T(8,128)(2,1)} %grad_hbm.3), custom_call_target="tpu_custom_call" | custom-call | flops 113246208 | bytes 2359296 | tf_op jit(solution)/shard_map/pallas_call | solution.py:385
  3.3 3.1 %collective-permute-start = (f32[16,2304]{1,0:T(8,128)S(1)}, f32[16,2304]{1,0:T(8,128)S(1)}, u32[]{:S(2)}, u32[]{:S(2)}) collective-permute-start(f32[16,2304]{1,0:T(8,128)S(1)} %get-tuple-element.27), channel_id=1, source_target_pairs={{0,1},{1,0},{2,3},{3,2},{4,5},{5,4},{6,7},{7,6},{8,10},{9,11},{10,... | collective-permute-start | bytes 442376 | tf_op jit(solution)/shard_map/ppermute | solution.py:352
  6.4 2.0 %shard_map.71 = (f32[16,2304]{1,0:T(8,128)S(1)}, f32[2,16,2304]{2,1,0:T(8,128)S(1)}, f32[8,128]{1,0:T(8,128)S(1)}) custom-call(s32[1,4]{1,0:T(1,128)} %len_hbm.3, s32[1,1]{1,0:T(1,128)} %bitcast.4.off_hbm, s32[1,4]{1,0:T(1,128)} %inc_hbm.3, bf16[16,512]{1,0:T(8,128)(2,1)} %bitcast.6, bf16[512,4608]{1,0:T(8,128)(2,1)} %grad_hbm.3), custom_call_target="tpu_custom_call" | custom-call | flops 113246208 | bytes 2359296 | tf_op jit(solution)/shard_map/pallas_call | solution.py:385
  8.4 0.1 collective-permute-start.2
  8.5 1.0 %collective-permute-done.recv_ref = f32[16,2304]{1,0:T(8,128)S(1)} collective-permute-done((f32[16,2304]{1,0:T(8,128)S(1)}, f32[16,2304]{1,0:T(8,128)S(1)}, u32[]{:S(2)}, u32[]{:S(2)}) %collective-permute-start) | collective-permute-done | bytes 147488 | tf_op jit(solution)/shard_map/ppermute | solution.py:352
  9.5 0.1 shard_map.69
  9.6 2.1 %collective-permute-start.1 = (f32[16,2304]{1,0:T(8,128)S(1)}, f32[16,2304]{1,0:T(8,128)S(1)}, u32[]{:S(2)}, u32[]{:S(2)}) collective-permute-start(f32[16,2304]{1,0:T(8,128)S(1)} %get-tuple-element.30), channel_id=1, source_target_pairs={{0,2},{1,3},{2,0},{3,1},{4,6},{5,7},{6,4},{7,5},{8,9},{9,8},{10,11... | collective-permute-start | bytes 442376 | tf_op jit(solution)/shard_map/ppermute | solution.py:352
  11.7 3.0 %collective-permute-done.2.recv_ref = f32[16,2304]{1,0:T(8,128)S(1)} collective-permute-done((f32[16,2304]{1,0:T(8,128)S(1)}, f32[16,2304]{1,0:T(8,128)S(1)}, u32[]{:S(2)}, u32[]{:S(2)}) %collective-permute-start.2) | collective-permute-done | bytes 147488 | tf_op jit(solution)/shard_map/ppermute | solution.py:352
  14.8 2.1 %collective-permute-start.3 = (f32[16,2304]{1,0:T(8,128)S(1)}, f32[16,2304]{1,0:T(8,128)S(1)}, u32[]{:S(2)}, u32[]{:S(2)}) collective-permute-start(f32[16,2304]{1,0:T(8,128)S(1)} %get-tuple-element.36), channel_id=1, source_target_pairs={{0,2},{1,3},{2,0},{3,1},{4,6},{5,7},{6,4},{7,5},{8,9},{9,8},{10,11... | collective-permute-start | bytes 442376 | tf_op jit(solution)/shard_map/ppermute | solution.py:352
  16.9 2.6 %collective-permute-start.4 = (bf16[16,2304]{1,0:T(8,128)(2,1)S(1)}, bf16[16,2304]{1,0:T(8,128)(2,1)S(1)}, u32[]{:S(2)}, u32[]{:S(2)}) collective-permute-start(bf16[16,2304]{1,0:T(8,128)(2,1)S(1)} %get-tuple-element.38.refs_2_), channel_id=1, source_target_pairs={{0,4},{1,5},{2,6},{3,7},{4,0},{5,1},{6,2},{7,3},{8,12},{9,13},{10,... | collective-permute-start | bytes 221192 | tf_op jit(solution)/shard_map/ppermute | solution.py:352
  19.6 1.0 %collective-permute-done.3.recv_ref = f32[16,2304]{1,0:T(8,128)S(1)} collective-permute-done((f32[16,2304]{1,0:T(8,128)S(1)}, f32[16,2304]{1,0:T(8,128)S(1)}, u32[]{:S(2)}, u32[]{:S(2)}) %collective-permute-start.3) | collective-permute-done | bytes 147488 | tf_op jit(solution)/shard_map/ppermute | solution.py:352
  20.6 3.1 %collective-permute-start.5 = (bf16[16,2304]{1,0:T(8,128)(2,1)S(1)}, bf16[16,2304]{1,0:T(8,128)(2,1)S(1)}, u32[]{:S(2)}, u32[]{:S(2)}) collective-permute-start(bf16[16,2304]{1,0:T(8,128)(2,1)S(1)} %get-tuple-element.39.refs_3_), channel_id=1, source_target_pairs={{0,4},{1,5},{2,6},{3,7},{4,0},{5,1},{6,2},{7,3},{8,12},{9,13},{10,... | collective-permute-start | bytes 221192 | tf_op jit(solution)/shard_map/ppermute | solution.py:352
  23.7 2.3 %collective-permute-done.5.refs_5_ = bf16[16,2304]{1,0:T(8,128)(2,1)S(1)} collective-permute-done((bf16[16,2304]{1,0:T(8,128)(2,1)S(1)}, bf16[16,2304]{1,0:T(8,128)(2,1)S(1)}, u32[]{:S(2)}, u32[]{:S(2)}) %collective-permute-start.5) | collective-permute-done | bytes 73760 | tf_op jit(solution)/shard_map/ppermute | solution.py:352
  26.0 0.6 %shard_map.74 = (f32[2,16,576]{2,1,0:T(8,128)S(1)}, f32[2,16,576]{2,1,0:T(8,128)S(1)}, f32[16,128]{1,0:T(8,128)S(1)}) custom-call(f32[16,2304]{1,0:T(8,128)S(1)} %get-tuple-element.31.refs_0_, f32[16,2304]{1,0:T(8,128)S(1)} %get-tuple-element.37.refs_1_, bf16[16,2304]{1,0:T(8,128)(2,1)S(1)} %get-tuple-element.38.refs_2_, ...), custom_call_target="tpu_custom_call" | custom-call | tf_op jit(solution)/shard_map/pallas_call | solution.py:362
  26.6 0.1 collective-permute-start.6
  26.6 1.3 %collective-permute-done.6.recv_ref.core_ref = f32[2,16,576]{2,1,0:T(8,128)S(1)} collective-permute-done((f32[2,16,576]{2,1,0:T(8,128)S(1)}, f32[2,16,576]{2,1,0:T(8,128)S(1)}, u32[]{:S(2)}, u32[]{:S(2)}) %collective-permute-start.6) | collective-permute-done | bytes 73760 | tf_op jit(solution)/shard_map/ppermute | solution.py:356
  27.9 1.5 %collective-permute-start.7 = (f32[16,576]{1,0:T(8,128)S(1)}, f32[16,576]{1,0:T(8,128)S(1)}, u32[]{:S(2)}, u32[]{:S(2)}) collective-permute-start(f32[16,576]{1,0:T(8,128)S(1)} %shard_map.75), channel_id=1, source_target_pairs={{0,16},{8,24},{16,0},{24,8},{1,17},{9,25},{17,1},{25,9},{2,18},{10... | collective-permute-start | bytes 110600 | tf_op jit(solution)/shard_map/ppermute | solution.py:356
  29.5 2.5 %collective-permute-done.7.recv_ref = f32[16,576]{1,0:T(8,128)S(1)} collective-permute-done((f32[16,576]{1,0:T(8,128)S(1)}, f32[16,576]{1,0:T(8,128)S(1)}, u32[]{:S(2)}, u32[]{:S(2)}) %collective-permute-start.7) | collective-permute-done | bytes 36896 | tf_op jit(solution)/shard_map/ppermute | solution.py:356
  32.0 0.1 shard_map.76
  32.1 2.5 %collective-permute-start.8 = (f32[16,384]{1,0:T(8,128)S(1)}, f32[16,384]{1,0:T(8,128)S(1)}, u32[]{:S(2)}, u32[]{:S(2)}) collective-permute-start(f32[16,384]{1,0:T(8,128)S(1)} %get-tuple-element.44), channel_id=1, source_target_pairs={{0,2},{1,3},{2,0},{3,1},{4,6},{5,7},{6,4},{7,5},{8,10},{9,11},{10,... | collective-permute-start | bytes 73736 | tf_op jit(solution)/shard_map/ppermute | solution.py:352
  34.6 1.8 %collective-permute-done.8.recv_ref = f32[16,384]{1,0:T(8,128)S(1)} collective-permute-done((f32[16,384]{1,0:T(8,128)S(1)}, f32[16,384]{1,0:T(8,128)S(1)}, u32[]{:S(2)}, u32[]{:S(2)}) %collective-permute-start.8) | collective-permute-done | bytes 24608 | tf_op jit(solution)/shard_map/ppermute | solution.py:352
  36.4 0.1 shard_map.77
  36.5 3.7 %collective-permute-done.9.recv_ref = f32[16,256]{1,0:T(8,128)S(1)} collective-permute-done((f32[16,256]{1,0:T(8,128)S(1)}, f32[16,256]{1,0:T(8,128)S(1)}, u32[]{:S(2)}, u32[]{:S(2)}) %collective-permute-start.9) | collective-permute-done | bytes 16416 | tf_op jit(solution)/shard_map/ppermute | solution.py:352
  40.2 0.6 %shard_map.78 = (f32[16,144]{1,0:T(8,128)}, f32[1,4]{1,0:T(1,128)}) custom-call(f32[16,144]{1,0:T(8,128)S(1)} %get-tuple-element.45.keep_ref, f32[16,256]{1,0:T(8,128)S(1)} %collective-permute-done.9.recv_ref, f32[16,128]{1,0:T(8,128)S(1)} %get-tuple-element.47.norm_ref), custom_call_target="tpu_custom_call" | custom-call | tf_op jit(solution)/shard_map/pallas_call | solution.py:450
  (7 shorter events, 0.1 us)
Async XLA Ops:
  3.3 6.2 %collective-permute-start = (f32[16,2304]{1,0:T(8,128)S(1)}, f32[16,2304]{1,0:T(8,128)S(1)}, u32[]{:S(2)}, u32[]{:S(2)}) collective-permute-start(f32[16,2304]{1,0:T(8,128)S(1)} %get-tuple-element.27), channel_id=1, source_target_pairs={{0,1},{1,0},{2,3},{3,2},{4,5},{5,4},{6,7},{7,6},{8,10},{9,11},{10,... | collective-permute-start | bytes 442376 | tf_op jit(solution)/shard_map/ppermute | solution.py:352
  8.4 6.3 %collective-permute-start.2 = (f32[16,2304]{1,0:T(8,128)S(1)}, f32[16,2304]{1,0:T(8,128)S(1)}, u32[]{:S(2)}, u32[]{:S(2)}) collective-permute-start(f32[16,2304]{1,0:T(8,128)S(1)} %get-tuple-element.33), channel_id=1, source_target_pairs={{0,1},{1,0},{2,3},{3,2},{4,5},{5,4},{6,7},{7,6},{8,10},{9,11},{10,... | collective-permute-start | bytes 442376 | tf_op jit(solution)/shard_map/ppermute | solution.py:352
  9.6 7.3 %collective-permute-start.1 = (f32[16,2304]{1,0:T(8,128)S(1)}, f32[16,2304]{1,0:T(8,128)S(1)}, u32[]{:S(2)}, u32[]{:S(2)}) collective-permute-start(f32[16,2304]{1,0:T(8,128)S(1)} %get-tuple-element.30), channel_id=1, source_target_pairs={{0,2},{1,3},{2,0},{3,1},{4,6},{5,7},{6,4},{7,5},{8,9},{9,8},{10,11... | collective-permute-start | bytes 442376 | tf_op jit(solution)/shard_map/ppermute | solution.py:352
  14.8 5.8 %collective-permute-start.3 = (f32[16,2304]{1,0:T(8,128)S(1)}, f32[16,2304]{1,0:T(8,128)S(1)}, u32[]{:S(2)}, u32[]{:S(2)}) collective-permute-start(f32[16,2304]{1,0:T(8,128)S(1)} %get-tuple-element.36), channel_id=1, source_target_pairs={{0,2},{1,3},{2,0},{3,1},{4,6},{5,7},{6,4},{7,5},{8,9},{9,8},{10,11... | collective-permute-start | bytes 442376 | tf_op jit(solution)/shard_map/ppermute | solution.py:352
  16.9 6.8 %collective-permute-start.4 = (bf16[16,2304]{1,0:T(8,128)(2,1)S(1)}, bf16[16,2304]{1,0:T(8,128)(2,1)S(1)}, u32[]{:S(2)}, u32[]{:S(2)}) collective-permute-start(bf16[16,2304]{1,0:T(8,128)(2,1)S(1)} %get-tuple-element.38.refs_2_), channel_id=1, source_target_pairs={{0,4},{1,5},{2,6},{3,7},{4,0},{5,1},{6,2},{7,3},{8,12},{9,13},{10,... | collective-permute-start | bytes 221192 | tf_op jit(solution)/shard_map/ppermute | solution.py:352
  20.6 5.4 %collective-permute-start.5 = (bf16[16,2304]{1,0:T(8,128)(2,1)S(1)}, bf16[16,2304]{1,0:T(8,128)(2,1)S(1)}, u32[]{:S(2)}, u32[]{:S(2)}) collective-permute-start(bf16[16,2304]{1,0:T(8,128)(2,1)S(1)} %get-tuple-element.39.refs_3_), channel_id=1, source_target_pairs={{0,4},{1,5},{2,6},{3,7},{4,0},{5,1},{6,2},{7,3},{8,12},{9,13},{10,... | collective-permute-start | bytes 221192 | tf_op jit(solution)/shard_map/ppermute | solution.py:352
  26.6 1.3 %collective-permute-start.6 = (f32[2,16,576]{2,1,0:T(8,128)S(1)}, f32[2,16,576]{2,1,0:T(8,128)S(1)}, u32[]{:S(2)}, u32[]{:S(2)}) collective-permute-start(f32[2,16,576]{2,1,0:T(8,128)S(1)} %get-tuple-element.41), channel_id=1, source_target_pairs={{0,8},{8,0},{16,24},{24,16},{1,9},{9,1},{17,25},{25,17},{2,10},{10... | collective-permute-start | bytes 221192 | tf_op jit(solution)/shard_map/ppermute | solution.py:356
  27.9 4.1 %collective-permute-start.7 = (f32[16,576]{1,0:T(8,128)S(1)}, f32[16,576]{1,0:T(8,128)S(1)}, u32[]{:S(2)}, u32[]{:S(2)}) collective-permute-start(f32[16,576]{1,0:T(8,128)S(1)} %shard_map.75), channel_id=1, source_target_pairs={{0,16},{8,24},{16,0},{24,8},{1,17},{9,25},{17,1},{25,9},{2,18},{10... | collective-permute-start | bytes 110600 | tf_op jit(solution)/shard_map/ppermute | solution.py:356
  32.1 4.3 %collective-permute-start.8 = (f32[16,384]{1,0:T(8,128)S(1)}, f32[16,384]{1,0:T(8,128)S(1)}, u32[]{:S(2)}, u32[]{:S(2)}) collective-permute-start(f32[16,384]{1,0:T(8,128)S(1)} %get-tuple-element.44), channel_id=1, source_target_pairs={{0,2},{1,3},{2,0},{3,1},{4,6},{5,7},{6,4},{7,5},{8,10},{9,11},{10,... | collective-permute-start | bytes 73736 | tf_op jit(solution)/shard_map/ppermute | solution.py:352
  36.5 3.7 %collective-permute-start.9 = (f32[16,256]{1,0:T(8,128)S(1)}, f32[16,256]{1,0:T(8,128)S(1)}, u32[]{:S(2)}, u32[]{:S(2)}) collective-permute-start(f32[16,256]{1,0:T(8,128)S(1)} %get-tuple-element.46), channel_id=1, source_target_pairs={{0,1},{1,0},{2,3},{3,2},{4,5},{5,4},{6,7},{7,6},{8,9},{9,8},{10,11... | collective-permute-start | bytes 49160 | tf_op jit(solution)/shard_map/ppermute | solution.py:352

commit v6 on v5

--- a/solution.py
+++ b/solution.py
@@ -149,13 +149,13 @@
 
 
 def partials_kernel(
-    half, n_ctx, docs, chunks, len_hbm, off_hbm, inc_hbm, inner_hbm, grad_hbm, *refs
+    n_ctx, docs, chunks, len_hbm, off_hbm, inc_hbm, inner_hbm, grad_hbm, *refs
 ):
-    send_ref, keep_ref, flag_ref, grad_buf, inner_ref, spread = refs[:6]
-    len_ref, off_ref, inc_ref, small_sems, sems = refs[6:]
+    send_refs, (keep_ref, flag_ref, grad_buf, inner_ref, spread) = refs[:PARTS], refs[PARTS : PARTS + 5]
+    len_ref, off_ref, inc_ref, small_sems, sems = refs[PARTS + 5 :]
     rank, rows = inner_ref.shape
-    features = send_ref.shape[1]
-    width = features // chunks
+    part = send_refs[0].shape[1]
+    width = grad_hbm.shape[1] // chunks
     small = [
         pltpu.make_async_copy(len_hbm, len_ref, small_sems.at[0]),
         pltpu.make_async_copy(off_hbm, off_ref, small_sems.at[1]),
@@ -164,7 +164,7 @@
     ]
     copies = [
         pltpu.make_async_copy(
-            grad_hbm.at[:, pl.ds(half * features + j * width, width)], grad_buf.at[j], sems.at[j]
+            grad_hbm.at[:, pl.ds(j * width, width)], grad_buf.at[j], sems.at[j]
         )
         for j in range(chunks)
     ]
@@ -236,13 +236,16 @@
         columns = slice(j * width, (j + 1) * width)
         keep_ref[0, :, columns] = product[:rank]
         keep_ref[1, :, columns] = product[rank : 2 * rank]
-        send_ref[:, columns] = product[2 * rank :]
-
-
-def fold_kernel(keep_ref, recv_ref, fact_ref, send_ref, left_ref):
+        at = j * width % part
+        send_refs[j * width // part][:, at : at + width] = product[2 * rank :]
+
+
+def fold_kernel(half, keep_ref, recv_ref, fact_ref, send_ref, left_ref):
+    width = send_ref.shape[1]
+    columns = slice(half * width, (half + 1) * width)
     received = recv_ref[...]
-    send_ref[...] = keep_ref[1] + fact_ref[2:3, 0:1] * received
-    left_ref[...] = keep_ref[0] + fact_ref[1:2, 0:1] * received
+    send_ref[...] = keep_ref[1, :, columns] + fact_ref[2:3, 0:1] * received
+    left_ref[...] = keep_ref[0, :, columns] + fact_ref[1:2, 0:1] * received
 
 
 def round_kernel(keep_ref, recv_ref, own_ref, mine_ref):
@@ -377,47 +380,47 @@
     hbm = pl.BlockSpec(memory_space=pl.ANY)
     parts = PARTS
     part = features // parts
-    chunks = max(1, part // 768)
+    chunks = max(1, features // 1152)
     column = ((rank, 128), f32)
     single = ((rank, part), f32)
 
-    def partials(half):
-        return pl.pallas_call(
-            functools.partial(partials_kernel, half, n_ctx, docs, chunks),
-            out_shape=[
-                pltpu.VMEM(*single),
-                pltpu.VMEM((2, rank, part), f32),
-                pltpu.VMEM((8, 128), f32),
-            ],
-            in_specs=[hbm] * 5,
-            out_specs=[vmem] * 3,
-            scratch_shapes=[
-                pltpu.VMEM((chunks, rows, part // chunks), jnp.bfloat16),
-                pltpu.VMEM((rank, rows), jnp.bfloat16),
-                pltpu.VMEM((3 * rank, rows), jnp.bfloat16),
-                pltpu.SMEM(doc_lengths.shape, jnp.int32),
-                pltpu.SMEM((1, 1), jnp.int32),
-                pltpu.SMEM(included.shape, jnp.int32),
-                pltpu.SemaphoreType.DMA((4,)),
-                pltpu.SemaphoreType.DMA((chunks,)),
-            ],
-            cost_estimate=pl.CostEstimate(
-                flops=2 * 3 * rank * rows * part,
-                bytes_accessed=2 * rows * part,
-                transcendentals=0,
-            ),
-        )(doc_lengths, slab_offset[:, None], included, adapter_inner.T, out_grad)
+    *sends, keep, flag = pl.pallas_call(
+        functools.partial(partials_kernel, n_ctx, docs, chunks),
+        out_shape=[
+            *[pltpu.VMEM(*single)] * parts,
+            pltpu.VMEM((2, rank, features), f32),
+            pltpu.VMEM((8, 128), f32),
+        ],
+        in_specs=[hbm] * 5,
+        out_specs=[vmem] * (parts + 2),
+        scratch_shapes=[
+            pltpu.VMEM((chunks, rows, features // chunks), jnp.bfloat16),
+            pltpu.VMEM((rank, rows), jnp.bfloat16),
+            pltpu.VMEM((3 * rank, rows), jnp.bfloat16),
+            pltpu.SMEM(doc_lengths.shape, jnp.int32),
+            pltpu.SMEM((1, 1), jnp.int32),
+            pltpu.SMEM(included.shape, jnp.int32),
+            pltpu.SemaphoreType.DMA((4,)),
+            pltpu.SemaphoreType.DMA((chunks,)),
+        ],
+        cost_estimate=pl.CostEstimate(
+            flops=2 * 3 * rank * rows * features,
+            bytes_accessed=2 * rows * features,
+            transcendentals=0,
+        ),
+    )(doc_lengths, slab_offset[:, None], included, adapter_inner.T, out_grad)
 
     even, odd = halving_orders(n_ctx)
     rounds = list(zip(even, odd))
     owns, mines, others = [], [], []
+    firsts = [exchange(send, n_dp, n_ctx, *rounds[0]) for send in sends]
     for half in range(parts):
-        send, keep, flag = partials(half)
-        received = exchange(send, n_dp, n_ctx, *rounds[0])
-        send, keep = in_vmem(fold_kernel, [single, single], keep, received, flag)
+        send, left = in_vmem(
+            functools.partial(fold_kernel, half), [single, single], keep, firsts[half], flag
+        )
         received = exchange(send, n_dp, n_ctx, *rounds[1])
         own, mine = in_vmem(
-            round_kernel, [single, ((rank, part), jnp.bfloat16)], keep, received
+            round_kernel, [single, ((rank, part), jnp.bfloat16)], left, received
         )
         owns.append(own)
         mines.append(mine)
@@ -469,7 +472,7 @@
         and n_ctx == 2 * docs
         and docs <= adapter_inner.shape[1]
         and 2 * (rows - 2) + (docs - 2) * LONGEST < n_ctx * rows
-        and out_grad.shape[1] % (768 * PARTS) == 0
+        and out_grad.shape[1] % (1152 * PARTS) == 0
     )
     plan = halving_plan if halving else chain_plan
     return plan(out_grad, adapter_inner, doc_lengths, slab_offset, included)

time: 41 us -> 38.7 us (0.944)
  Pallas kernels: 5.6 us -> 4.48 us
  waiting for transfers between devices: 16.7 us -> 15.7 us
    pallas_call x2 -> x1, Pallas kernels: 4.03 us -> 2.9 us  [halving_plan(): pl.pallas_call(functools.partial(partials_kernel, n_ctx, docs, chunks), o...]
    ppermute x8, waiting for transfers between devices: 12.9 us -> 11.9 us  [exchange(): return lax.ppermute(block, ('dp', 'ctx'), route)]
  transfers between devices with their start and end apart: 10 -> 10, of which waited for: 8 -> 8; matrix products, arithmetic and copies ran while one was open for 0% -> 0% of each run, Pallas kernels for 5% -> 1%
where the time goes in v6:
time: 38.7 us; the launch traced here: 38.6 us
  starting transfers between devices  17.1 us (44%)
  waiting for transfers between devices  15.7 us (41%)
  Pallas kernels  4.48 us (12%)
  between operations  1.32 us (3%)
    ppermute x8, starting transfers between devices, exchange(): return lax.ppermute(block, ('dp', 'ctx'), route)  15.5 us
    ppermute x8, waiting for transfers between devices, exchange(): return lax.ppermute(block, ('dp', 'ctx'), route)  11.9 us
    ppermute x2, waiting for transfers between devices, swap_dp(): return lax.ppermute(block, 'dp', [(d, d ^ 1 << bit) for d in range(n_dp)])  3.78 us
    pallas_call x1, Pallas kernels, halving_plan(): pl.pallas_call(functools.partial(partials_kernel, n_ctx, docs, chunks), o...  2.9 us
    ppermute x2, starting transfers between devices, swap_dp(): return lax.ppermute(block, 'dp', [(d, d ^ 1 << bit) for d in range(n_dp)])  1.62 us
    pallas_call x8, Pallas kernels, in_vmem(): pl.pallas_call(kernel, out_shape=[pltpu.VMEM(shape, dtype) for shape, dty...  0.98 us
  transfers between devices with their start and end apart: 10, of which 8 were waited for; matrix products, arithmetic and copies ran while one was open for 0% of the time, Pallas kernels for 1%

profile of v6, /device:TPU:0, one launch (start us, length us, event | category | flops | bytes accessed | tf_op | source)
XLA Modules:
  0.0 38.6 jit_solution(4277358924768337183)
XLA Ops:
  1.3 2.9 %shard_map.68 = (f32[16,2304]{1,0:T(8,128)S(1)}, f32[16,2304]{1,0:T(8,128)S(1)}, f32[2,16,4608]{2,1,0:T(8,128)S(1)}, f32[8,128]{1,0:T(8,128)S(1)}) custom-call(s32[1,4]{1,0:T(1,128)} %len_hbm.1, s32[1,1]{1,0:T(1,128)} %bitcast.3.off_hbm, s32[1,4]{1,0:T(1,128)} %inc_hbm.1, bf16[16,512]{1,0:T(8,128)(2,1)} %bitcast.4, bf16[512,4608]{1,0:T(8,128)(2,1)} %grad_hbm.1), custom_call_target="tpu_custom_call" | custom-call | flops 226492416 | bytes 4718592 | tf_op jit(solution)/shard_map/pallas_call | solution.py:387
  4.2 3.1 %collective-permute-start = (f32[16,2304]{1,0:T(8,128)S(1)}, f32[16,2304]{1,0:T(8,128)S(1)}, u32[]{:S(2)}, u32[]{:S(2)}) collective-permute-start(f32[16,2304]{1,0:T(8,128)S(1)} %get-tuple-element.25), channel_id=1, source_target_pairs={{0,1},{1,0},{2,3},{3,2},{4,5},{5,4},{6,7},{7,6},{8,10},{9,11},{10,... | collective-permute-start | bytes 442376 | tf_op jit(solution)/shard_map/ppermute | solution.py:355
  7.2 0.1 collective-permute-start.2
  7.3 3.0 %collective-permute-done.recv_ref = f32[16,2304]{1,0:T(8,128)S(1)} collective-permute-done((f32[16,2304]{1,0:T(8,128)S(1)}, f32[16,2304]{1,0:T(8,128)S(1)}, u32[]{:S(2)}, u32[]{:S(2)}) %collective-permute-start) | collective-permute-done | bytes 147488 | tf_op jit(solution)/shard_map/ppermute | solution.py:355
  10.4 2.1 %collective-permute-start.1 = (f32[16,2304]{1,0:T(8,128)S(1)}, f32[16,2304]{1,0:T(8,128)S(1)}, u32[]{:S(2)}, u32[]{:S(2)}) collective-permute-start(f32[16,2304]{1,0:T(8,128)S(1)} %get-tuple-element.28), channel_id=1, source_target_pairs={{0,2},{1,3},{2,0},{3,1},{4,6},{5,7},{6,4},{7,5},{8,9},{9,8},{10,11... | collective-permute-start | bytes 442376 | tf_op jit(solution)/shard_map/ppermute | solution.py:355
  12.6 0.1 shard_map.71
  12.7 1.5 %collective-permute-start.3 = (f32[16,2304]{1,0:T(8,128)S(1)}, f32[16,2304]{1,0:T(8,128)S(1)}, u32[]{:S(2)}, u32[]{:S(2)}) collective-permute-start(f32[16,2304]{1,0:T(8,128)S(1)} %get-tuple-element.32), channel_id=1, source_target_pairs={{0,2},{1,3},{2,0},{3,1},{4,6},{5,7},{6,4},{7,5},{8,9},{9,8},{10,11... | collective-permute-start | bytes 442376 | tf_op jit(solution)/shard_map/ppermute | solution.py:355
  14.2 1.5 %collective-permute-done.1.recv_ref = f32[16,2304]{1,0:T(8,128)S(1)} collective-permute-done((f32[16,2304]{1,0:T(8,128)S(1)}, f32[16,2304]{1,0:T(8,128)S(1)}, u32[]{:S(2)}, u32[]{:S(2)}) %collective-permute-start.1) | collective-permute-done | bytes 147488 | tf_op jit(solution)/shard_map/ppermute | solution.py:355
  15.7 3.1 %collective-permute-start.4 = (bf16[16,2304]{1,0:T(8,128)(2,1)S(1)}, bf16[16,2304]{1,0:T(8,128)(2,1)S(1)}, u32[]{:S(2)}, u32[]{:S(2)}) collective-permute-start(bf16[16,2304]{1,0:T(8,128)(2,1)S(1)} %get-tuple-element.34.refs_2_), channel_id=1, source_target_pairs={{0,4},{1,5},{2,6},{3,7},{4,0},{5,1},{6,2},{7,3},{8,12},{9,13},{10,... | collective-permute-start | bytes 221192 | tf_op jit(solution)/shard_map/ppermute | solution.py:355
  18.9 2.5 %collective-permute-start.5 = (bf16[16,2304]{1,0:T(8,128)(2,1)S(1)}, bf16[16,2304]{1,0:T(8,128)(2,1)S(1)}, u32[]{:S(2)}, u32[]{:S(2)}) collective-permute-start(bf16[16,2304]{1,0:T(8,128)(2,1)S(1)} %get-tuple-element.35.refs_3_), channel_id=1, source_target_pairs={{0,4},{1,5},{2,6},{3,7},{4,0},{5,1},{6,2},{7,3},{8,12},{9,13},{10,... | collective-permute-start | bytes 221192 | tf_op jit(solution)/shard_map/ppermute | solution.py:355
  21.3 1.9 %collective-permute-done.4.refs_4_ = bf16[16,2304]{1,0:T(8,128)(2,1)S(1)} collective-permute-done((bf16[16,2304]{1,0:T(8,128)(2,1)S(1)}, bf16[16,2304]{1,0:T(8,128)(2,1)S(1)}, u32[]{:S(2)}, u32[]{:S(2)}) %collective-permute-start.4) | collective-permute-done | bytes 73760 | tf_op jit(solution)/shard_map/ppermute | solution.py:355
  23.2 1.0 %collective-permute-done.5.refs_5_ = bf16[16,2304]{1,0:T(8,128)(2,1)S(1)} collective-permute-done((bf16[16,2304]{1,0:T(8,128)(2,1)S(1)}, bf16[16,2304]{1,0:T(8,128)(2,1)S(1)}, u32[]{:S(2)}, u32[]{:S(2)}) %collective-permute-start.5) | collective-permute-done | bytes 73760 | tf_op jit(solution)/shard_map/ppermute | solution.py:355
  24.2 0.6 %shard_map.73 = (f32[2,16,576]{2,1,0:T(8,128)S(1)}, f32[2,16,576]{2,1,0:T(8,128)S(1)}, f32[16,128]{1,0:T(8,128)S(1)}) custom-call(f32[16,2304]{1,0:T(8,128)S(1)} %get-tuple-element.29.refs_0_, f32[16,2304]{1,0:T(8,128)S(1)} %get-tuple-element.33.refs_1_, bf16[16,2304]{1,0:T(8,128)(2,1)S(1)} %get-tuple-element.34.refs_2_, ...), custom_call_target="tpu_custom_call" | custom-call | tf_op jit(solution)/shard_map/pallas_call | solution.py:365
  24.7 0.1 collective-permute-start.6
  24.8 1.3 %collective-permute-done.6.recv_ref.core_ref = f32[2,16,576]{2,1,0:T(8,128)S(1)} collective-permute-done((f32[2,16,576]{2,1,0:T(8,128)S(1)}, f32[2,16,576]{2,1,0:T(8,128)S(1)}, u32[]{:S(2)}, u32[]{:S(2)}) %collective-permute-start.6) | collective-permute-done | bytes 73760 | tf_op jit(solution)/shard_map/ppermute | solution.py:359
  26.1 1.5 %collective-permute-start.7 = (f32[16,576]{1,0:T(8,128)S(1)}, f32[16,576]{1,0:T(8,128)S(1)}, u32[]{:S(2)}, u32[]{:S(2)}) collective-permute-start(f32[16,576]{1,0:T(8,128)S(1)} %shard_map.74), channel_id=1, source_target_pairs={{0,16},{8,24},{16,0},{24,8},{1,17},{9,25},{17,1},{25,9},{2,18},{10... | collective-permute-start | bytes 110600 | tf_op jit(solution)/shard_map/ppermute | solution.py:359
  27.6 2.5 %collective-permute-done.7.recv_ref = f32[16,576]{1,0:T(8,128)S(1)} collective-permute-done((f32[16,576]{1,0:T(8,128)S(1)}, f32[16,576]{1,0:T(8,128)S(1)}, u32[]{:S(2)}, u32[]{:S(2)}) %collective-permute-start.7) | collective-permute-done | bytes 36896 | tf_op jit(solution)/shard_map/ppermute | solution.py:359
  30.2 0.1 shard_map.75
  30.2 1.6 %collective-permute-start.8 = (f32[16,384]{1,0:T(8,128)S(1)}, f32[16,384]{1,0:T(8,128)S(1)}, u32[]{:S(2)}, u32[]{:S(2)}) collective-permute-start(f32[16,384]{1,0:T(8,128)S(1)} %get-tuple-element.40), channel_id=1, source_target_pairs={{0,2},{1,3},{2,0},{3,1},{4,6},{5,7},{6,4},{7,5},{8,10},{9,11},{10,... | collective-permute-start | bytes 73736 | tf_op jit(solution)/shard_map/ppermute | solution.py:355
  31.8 2.3 %collective-permute-done.8.recv_ref = f32[16,384]{1,0:T(8,128)S(1)} collective-permute-done((f32[16,384]{1,0:T(8,128)S(1)}, f32[16,384]{1,0:T(8,128)S(1)}, u32[]{:S(2)}, u32[]{:S(2)}) %collective-permute-start.8) | collective-permute-done | bytes 24608 | tf_op jit(solution)/shard_map/ppermute | solution.py:355
  34.1 0.1 shard_map.76
  34.2 1.5 %collective-permute-start.9 = (f32[16,256]{1,0:T(8,128)S(1)}, f32[16,256]{1,0:T(8,128)S(1)}, u32[]{:S(2)}, u32[]{:S(2)}) collective-permute-start(f32[16,256]{1,0:T(8,128)S(1)} %get-tuple-element.42), channel_id=1, source_target_pairs={{0,1},{1,0},{2,3},{3,2},{4,5},{5,4},{6,7},{7,6},{8,9},{9,8},{10,11... | collective-permute-start | bytes 49160 | tf_op jit(solution)/shard_map/ppermute | solution.py:355
  35.7 2.2 %collective-permute-done.9.recv_ref = f32[16,256]{1,0:T(8,128)S(1)} collective-permute-done((f32[16,256]{1,0:T(8,128)S(1)}, f32[16,256]{1,0:T(8,128)S(1)}, u32[]{:S(2)}, u32[]{:S(2)}) %collective-permute-start.9) | collective-permute-done | bytes 16416 | tf_op jit(solution)/shard_map/ppermute | solution.py:355
  38.0 0.6 %shard_map.77 = (f32[16,144]{1,0:T(8,128)}, f32[1,4]{1,0:T(1,128)}) custom-call(f32[16,144]{1,0:T(8,128)S(1)} %get-tuple-element.41.keep_ref, f32[16,256]{1,0:T(8,128)S(1)} %collective-permute-done.9.recv_ref, f32[16,128]{1,0:T(8,128)S(1)} %get-tuple-element.43.norm_ref), custom_call_target="tpu_custom_call" | custom-call | tf_op jit(solution)/shard_map/pallas_call | solution.py:453
  (6 shorter events, 0.1 us)
Async XLA Ops:
  4.2 6.2 %collective-permute-start = (f32[16,2304]{1,0:T(8,128)S(1)}, f32[16,2304]{1,0:T(8,128)S(1)}, u32[]{:S(2)}, u32[]{:S(2)}) collective-permute-start(f32[16,2304]{1,0:T(8,128)S(1)} %get-tuple-element.25), channel_id=1, source_target_pairs={{0,1},{1,0},{2,3},{3,2},{4,5},{5,4},{6,7},{7,6},{8,10},{9,11},{10,... | collective-permute-start | bytes 442376 | tf_op jit(solution)/shard_map/ppermute | solution.py:355
  7.2 5.3 %collective-permute-start.2 = (f32[16,2304]{1,0:T(8,128)S(1)}, f32[16,2304]{1,0:T(8,128)S(1)}, u32[]{:S(2)}, u32[]{:S(2)}) collective-permute-start(f32[16,2304]{1,0:T(8,128)S(1)} %get-tuple-element.30), channel_id=1, source_target_pairs={{0,1},{1,0},{2,3},{3,2},{4,5},{5,4},{6,7},{7,6},{8,10},{9,11},{10,... | collective-permute-start | bytes 442376 | tf_op jit(solution)/shard_map/ppermute | solution.py:355
  10.4 5.3 %collective-permute-start.1 = (f32[16,2304]{1,0:T(8,128)S(1)}, f32[16,2304]{1,0:T(8,128)S(1)}, u32[]{:S(2)}, u32[]{:S(2)}) collective-permute-start(f32[16,2304]{1,0:T(8,128)S(1)} %get-tuple-element.28), channel_id=1, source_target_pairs={{0,2},{1,3},{2,0},{3,1},{4,6},{5,7},{6,4},{7,5},{8,9},{9,8},{10,11... | collective-permute-start | bytes 442376 | tf_op jit(solution)/shard_map/ppermute | solution.py:355
  12.7 6.2 %collective-permute-start.3 = (f32[16,2304]{1,0:T(8,128)S(1)}, f32[16,2304]{1,0:T(8,128)S(1)}, u32[]{:S(2)}, u32[]{:S(2)}) collective-permute-start(f32[16,2304]{1,0:T(8,128)S(1)} %get-tuple-element.32), channel_id=1, source_target_pairs={{0,2},{1,3},{2,0},{3,1},{4,6},{5,7},{6,4},{7,5},{8,9},{9,8},{10,11... | collective-permute-start | bytes 442376 | tf_op jit(solution)/shard_map/ppermute | solution.py:355
  15.7 7.5 %collective-permute-start.4 = (bf16[16,2304]{1,0:T(8,128)(2,1)S(1)}, bf16[16,2304]{1,0:T(8,128)(2,1)S(1)}, u32[]{:S(2)}, u32[]{:S(2)}) collective-permute-start(bf16[16,2304]{1,0:T(8,128)(2,1)S(1)} %get-tuple-element.34.refs_2_), channel_id=1, source_target_pairs={{0,4},{1,5},{2,6},{3,7},{4,0},{5,1},{6,2},{7,3},{8,12},{9,13},{10,... | collective-permute-start | bytes 221192 | tf_op jit(solution)/shard_map/ppermute | solution.py:355
  18.9 5.3 %collective-permute-start.5 = (bf16[16,2304]{1,0:T(8,128)(2,1)S(1)}, bf16[16,2304]{1,0:T(8,128)(2,1)S(1)}, u32[]{:S(2)}, u32[]{:S(2)}) collective-permute-start(bf16[16,2304]{1,0:T(8,128)(2,1)S(1)} %get-tuple-element.35.refs_3_), channel_id=1, source_target_pairs={{0,4},{1,5},{2,6},{3,7},{4,0},{5,1},{6,2},{7,3},{8,12},{9,13},{10,... | collective-permute-start | bytes 221192 | tf_op jit(solution)/shard_map/ppermute | solution.py:355
  24.7 1.3 %collective-permute-start.6 = (f32[2,16,576]{2,1,0:T(8,128)S(1)}, f32[2,16,576]{2,1,0:T(8,128)S(1)}, u32[]{:S(2)}, u32[]{:S(2)}) collective-permute-start(f32[2,16,576]{2,1,0:T(8,128)S(1)} %get-tuple-element.37), channel_id=1, source_target_pairs={{0,8},{8,0},{16,24},{24,16},{1,9},{9,1},{17,25},{25,17},{2,10},{10... | collective-permute-start | bytes 221192 | tf_op jit(solution)/shard_map/ppermute | solution.py:359
  26.1 4.1 %collective-permute-start.7 = (f32[16,576]{1,0:T(8,128)S(1)}, f32[16,576]{1,0:T(8,128)S(1)}, u32[]{:S(2)}, u32[]{:S(2)}) collective-permute-start(f32[16,576]{1,0:T(8,128)S(1)} %shard_map.74), channel_id=1, source_target_pairs={{0,16},{8,24},{16,0},{24,8},{1,17},{9,25},{17,1},{25,9},{2,18},{10... | collective-permute-start | bytes 110600 | tf_op jit(solution)/shard_map/ppermute | solution.py:359
  30.2 3.8 %collective-permute-start.8 = (f32[16,384]{1,0:T(8,128)S(1)}, f32[16,384]{1,0:T(8,128)S(1)}, u32[]{:S(2)}, u32[]{:S(2)}) collective-permute-start(f32[16,384]{1,0:T(8,128)S(1)} %get-tuple-element.40), channel_id=1, source_target_pairs={{0,2},{1,3},{2,0},{3,1},{4,6},{5,7},{6,4},{7,5},{8,10},{9,11},{10,... | collective-permute-start | bytes 73736 | tf_op jit(solution)/shard_map/ppermute | solution.py:355
  34.2 3.7 %collective-permute-start.9 = (f32[16,256]{1,0:T(8,128)S(1)}, f32[16,256]{1,0:T(8,128)S(1)}, u32[]{:S(2)}, u32[]{:S(2)}) collective-permute-start(f32[16,256]{1,0:T(8,128)S(1)} %get-tuple-element.42), channel_id=1, source_target_pairs={{0,1},{1,0},{2,3},{3,2},{4,5},{5,4},{6,7},{7,6},{8,9},{9,8},{10,11... | collective-permute-start | bytes 49160 | tf_op jit(solution)/shard_map/ppermute | solution.py:355

commit v7 on v6

--- a/solution.py
+++ b/solution.py
@@ -269,21 +269,29 @@
     return relative(first, low) + relative(second, low)
 
 
-def clip_kernel(n_dp, n_ctx, docs, parts, *refs):
-    own_refs, mine_refs, other_refs = refs[:parts], refs[parts : 2 * parts], refs[2 * parts : 3 * parts]
-    flag_ref, send_ref, keep_ref, norm_ref = refs[3 * parts :]
-    slab = send_ref.shape[2]
+def gather(own_ref, mine_ref, other_ref):
+    other = other_ref[...].astype(jnp.float32)
+    seen = mine_ref[...].astype(jnp.float32) + other
+    return own_ref[...] + other, jnp.sum(seen * seen, keepdims=True)
+
+
+def gather_kernel(own_ref, mine_ref, other_ref, whole_ref, square_ref):
+    whole, square = gather(own_ref, mine_ref, other_ref)
+    whole_ref[...] = whole
+    square_ref[...] = jnp.broadcast_to(square, square_ref.shape)
+
+
+def clip_kernel(sending, n_dp, n_ctx, parts, *refs):
+    whole_refs, square_refs = refs[: parts - 1], refs[parts - 1 : 2 * (parts - 1)]
+    own_ref, mine_ref, other_ref, flag_ref, pieces_ref, *norm_refs = refs[2 * (parts - 1) :]
+    slab = pieces_ref.shape[2]
     span = 2 * slab
     places = n_ctx // 2
     width = slab // places
-    square = None
-    wholes = []
-    for own_ref, mine_ref, other_ref in zip(own_refs, mine_refs, other_refs):
-        other = other_ref[...].astype(jnp.float32)
-        whole = mine_ref[...].astype(jnp.float32) + other
-        wholes.append(own_ref[...] + other)
-        term = jnp.sum(whole * whole, keepdims=True)
-        square = term if square is None else square + term
+    last, square = gather(own_ref, mine_ref, other_ref)
+    wholes = [ref[...] for ref in whole_refs] + [last]
+    for ref in square_refs:
+        square = square + ref[0:1, 0:1]
     norm = jnp.sqrt(square)
     factor = flag_ref[0:1, 0:1] * clip_norm / jnp.maximum(norm, clip_norm)
     me = lax.axis_index("ctx")
@@ -297,15 +305,14 @@
         base = d % (n_dp // parts) * span
         halves.append(
             jnp.where(upper, whole[:, base + slab : base + span], whole[:, base : base + slab])
-            * factor
         )
-    for target, ref in ((0, keep_ref), (1, send_ref)):
-        for x in range(n_dp // 2):
-            piece = jnp.where(core == target, halves[2 * x], halves[2 * x + 1])
-            pieces = relative([piece[:, q * width : (q + 1) * width] for q in range(places)], low)
-            ref[chip ^ x] = jnp.concatenate(pieces, axis=1)
-    rows = lax.broadcasted_iota(jnp.int32, norm_ref.shape, 0).astype(jnp.float32)
-    norm_ref[...] = jnp.where(rows == flag_ref[3:4, :], norm, 0.0)
+    for x in range(n_dp // 2):
+        piece = jnp.where(core == sending, halves[2 * x], halves[2 * x + 1])
+        pieces = relative([piece[:, q * width : (q + 1) * width] for q in range(places)], low)
+        pieces_ref[chip ^ x] = jnp.concatenate(pieces, axis=1) * factor
+    for norm_ref in norm_refs:
+        rows = lax.broadcasted_iota(jnp.int32, norm_ref.shape, 0).astype(jnp.float32)
+        norm_ref[...] = jnp.where(rows == flag_ref[3:4, :], norm, 0.0)
 
 
 def core_kernel(keep_ref, recv_ref, send_ref):
@@ -412,7 +419,7 @@
 
     even, odd = halving_orders(n_ctx)
     rounds = list(zip(even, odd))
-    owns, mines, others = [], [], []
+    wholes, squares = [], []
     firsts = [exchange(send, n_dp, n_ctx, *rounds[0]) for send in sends]
     for half in range(parts):
         send, left = in_vmem(
@@ -422,19 +429,18 @@
         own, mine = in_vmem(
             round_kernel, [single, ((rank, part), jnp.bfloat16)], left, received
         )
-        owns.append(own)
-        mines.append(mine)
-        others.append(exchange(mine, n_dp, n_ctx, *rounds[-1]))
+        other = exchange(mine, n_dp, n_ctx, *rounds[-1])
+        if half < parts - 1:
+            whole, square = in_vmem(gather_kernel, [single, ((8, 128), f32)], own, mine, other)
+            wholes.append(whole)
+            squares.append(square)
     slab = features // (2 * n_dp)
     pieces = ((n_dp // 2, rank, slab), f32)
-    send, keep, norms = in_vmem(
-        functools.partial(clip_kernel, n_dp, n_ctx, docs, parts),
-        [pieces, pieces, column],
-        *owns,
-        *mines,
-        *others,
-        flag,
-    )
+    document = (*wholes, *squares, own, mine, other, flag)
+    clip = functools.partial(clip_kernel, 1, n_dp, n_ctx, parts)
+    (send,) = in_vmem(clip, [pieces], *document)
+    clip = functools.partial(clip_kernel, 0, n_dp, n_ctx, parts)
+    keep, norms = in_vmem(clip, [pieces, column], *document)
     core = swap_dp(send, n_dp, 0)
     (send,) = in_vmem(core_kernel, [((rank, slab), f32)], keep, core)
     received = swap_dp(send, n_dp, 1)

time: 38.7 us -> 38.5 us (level)
  waiting for transfers between devices: 15.7 us -> 15.1 us
    pallas_call x8 -> x10, Pallas kernels: 0.98 us -> 1.27 us  [in_vmem(): pl.pallas_call(kernel, out_shape=[pltpu.VMEM(shape, dtype) for shape, dty...]
  transfers between devices with their start and end apart: 10 -> 10, of which waited for: 8 -> 8; matrix products, arithmetic and copies ran while one was open for 0% -> 0% of each run, Pallas kernels for 1% -> 2%
where the time goes in v7:
time: 38.5 us; the launch traced here: 38.3 us
  starting transfers between devices  17.1 us (44%)
  waiting for transfers between devices  15.1 us (39%)
  Pallas kernels  4.78 us (12%)
  between operations  1.34 us (3%)
    ppermute x8, starting transfers between devices, exchange(): return lax.ppermute(block, ('dp', 'ctx'), route)  15.5 us
    ppermute x8, waiting for transfers between devices, exchange(): return lax.ppermute(block, ('dp', 'ctx'), route)  11.7 us
    ppermute x2, waiting for transfers between devices, swap_dp(): return lax.ppermute(block, 'dp', [(d, d ^ 1 << bit) for d in range(n_dp)])  3.42 us
    pallas_call x1, Pallas kernels, halving_plan(): pl.pallas_call(functools.partial(partials_kernel, n_ctx, docs, chunks), o...  2.9 us
    ppermute x2, starting transfers between devices, swap_dp(): return lax.ppermute(block, 'dp', [(d, d ^ 1 << bit) for d in range(n_dp)])  1.62 us
    pallas_call x10, Pallas kernels, in_vmem(): pl.pallas_call(kernel, out_shape=[pltpu.VMEM(shape, dtype) for shape, dty...  1.27 us
  transfers between devices with their start and end apart: 10, of which 8 were waited for; matrix products, arithmetic and copies ran while one was open for 0% of the time, Pallas kernels for 2%

profile of v7, /device:TPU:0, one launch (start us, length us, event | category | flops | bytes accessed | tf_op | source)
XLA Modules:
  0.0 38.3 jit_solution(1581346861402424828)
XLA Ops:
  1.3 2.9 %shard_map.68 = (f32[16,2304]{1,0:T(8,128)S(1)}, f32[16,2304]{1,0:T(8,128)S(1)}, f32[2,16,4608]{2,1,0:T(8,128)S(1)}, f32[8,128]{1,0:T(8,128)S(1)}) custom-call(s32[1,4]{1,0:T(1,128)} %len_hbm.1, s32[1,1]{1,0:T(1,128)} %bitcast.3.off_hbm, s32[1,4]{1,0:T(1,128)} %inc_hbm.1, bf16[16,512]{1,0:T(8,128)(2,1)} %bitcast.4, bf16[512,4608]{1,0:T(8,128)(2,1)} %grad_hbm.1), custom_call_target="tpu_custom_call" | custom-call | flops 226492416 | bytes 4718592 | tf_op jit(solution)/shard_map/pallas_call | solution.py:394
  4.2 3.1 %collective-permute-start = (f32[16,2304]{1,0:T(8,128)S(1)}, f32[16,2304]{1,0:T(8,128)S(1)}, u32[]{:S(2)}, u32[]{:S(2)}) collective-permute-start(f32[16,2304]{1,0:T(8,128)S(1)} %get-tuple-element.26), channel_id=1, source_target_pairs={{0,1},{1,0},{2,3},{3,2},{4,5},{5,4},{6,7},{7,6},{8,10},{9,11},{10,... | collective-permute-start | bytes 442376 | tf_op jit(solution)/shard_map/ppermute | solution.py:362
  7.2 0.1 collective-permute-start.3
  7.3 3.0 %collective-permute-done.recv_ref = f32[16,2304]{1,0:T(8,128)S(1)} collective-permute-done((f32[16,2304]{1,0:T(8,128)S(1)}, f32[16,2304]{1,0:T(8,128)S(1)}, u32[]{:S(2)}, u32[]{:S(2)}) %collective-permute-start) | collective-permute-done | bytes 147488 | tf_op jit(solution)/shard_map/ppermute | solution.py:362
  10.4 2.1 %collective-permute-start.1 = (f32[16,2304]{1,0:T(8,128)S(1)}, f32[16,2304]{1,0:T(8,128)S(1)}, u32[]{:S(2)}, u32[]{:S(2)}) collective-permute-start(f32[16,2304]{1,0:T(8,128)S(1)} %get-tuple-element.29), channel_id=1, source_target_pairs={{0,2},{1,3},{2,0},{3,1},{4,6},{5,7},{6,4},{7,5},{8,9},{9,8},{10,11... | collective-permute-start | bytes 442376 | tf_op jit(solution)/shard_map/ppermute | solution.py:362
  12.7 1.5 %collective-permute-start.4 = (f32[16,2304]{1,0:T(8,128)S(1)}, f32[16,2304]{1,0:T(8,128)S(1)}, u32[]{:S(2)}, u32[]{:S(2)}) collective-permute-start(f32[16,2304]{1,0:T(8,128)S(1)} %get-tuple-element.36), channel_id=1, source_target_pairs={{0,2},{1,3},{2,0},{3,1},{4,6},{5,7},{6,4},{7,5},{8,9},{9,8},{10,11... | collective-permute-start | bytes 442376 | tf_op jit(solution)/shard_map/ppermute | solution.py:362
  14.2 1.5 %collective-permute-done.1.recv_ref = f32[16,2304]{1,0:T(8,128)S(1)} collective-permute-done((f32[16,2304]{1,0:T(8,128)S(1)}, f32[16,2304]{1,0:T(8,128)S(1)}, u32[]{:S(2)}, u32[]{:S(2)}) %collective-permute-start.1) | collective-permute-done | bytes 147488 | tf_op jit(solution)/shard_map/ppermute | solution.py:362
  15.7 3.1 %collective-permute-start.2 = (bf16[16,2304]{1,0:T(8,128)(2,1)S(1)}, bf16[16,2304]{1,0:T(8,128)(2,1)S(1)}, u32[]{:S(2)}, u32[]{:S(2)}) collective-permute-start(bf16[16,2304]{1,0:T(8,128)(2,1)S(1)} %get-tuple-element.31.mine_ref), channel_id=1, source_target_pairs={{0,4},{1,5},{2,6},{3,7},{4,0},{5,1},{6,2},{7,3},{8,12},{9,13},{10,... | collective-permute-start | bytes 221192 | tf_op jit(solution)/shard_map/ppermute | solution.py:362
  18.9 2.5 %collective-permute-start.5 = (bf16[16,2304]{1,0:T(8,128)(2,1)S(1)}, bf16[16,2304]{1,0:T(8,128)(2,1)S(1)}, u32[]{:S(2)}, u32[]{:S(2)}) collective-permute-start(bf16[16,2304]{1,0:T(8,128)(2,1)S(1)} %get-tuple-element.38.refs_3_), channel_id=1, source_target_pairs={{0,4},{1,5},{2,6},{3,7},{4,0},{5,1},{6,2},{7,3},{8,12},{9,13},{10,... | collective-permute-start | bytes 221192 | tf_op jit(solution)/shard_map/ppermute | solution.py:362
  21.3 1.9 %collective-permute-done.2.other_ref = bf16[16,2304]{1,0:T(8,128)(2,1)S(1)} collective-permute-done((bf16[16,2304]{1,0:T(8,128)(2,1)S(1)}, bf16[16,2304]{1,0:T(8,128)(2,1)S(1)}, u32[]{:S(2)}, u32[]{:S(2)}) %collective-permute-start.2) | collective-permute-done | bytes 73760 | tf_op jit(solution)/shard_map/ppermute | solution.py:362
  23.2 0.2 shard_map.71
  23.4 0.8 %collective-permute-done.5.refs_4_ = bf16[16,2304]{1,0:T(8,128)(2,1)S(1)} collective-permute-done((bf16[16,2304]{1,0:T(8,128)(2,1)S(1)}, bf16[16,2304]{1,0:T(8,128)(2,1)S(1)}, u32[]{:S(2)}, u32[]{:S(2)}) %collective-permute-start.5) | collective-permute-done | bytes 73760 | tf_op jit(solution)/shard_map/ppermute | solution.py:362
  24.2 0.3 shard_map.75
  24.6 0.3 shard_map.74
  25.0 0.9 %collective-permute-done.6.recv_ref.core_ref = f32[2,16,576]{2,1,0:T(8,128)S(1)} collective-permute-done((f32[2,16,576]{2,1,0:T(8,128)S(1)}, f32[2,16,576]{2,1,0:T(8,128)S(1)}, u32[]{:S(2)}, u32[]{:S(2)}) %collective-permute-start.6) | collective-permute-done | bytes 73760 | tf_op jit(solution)/shard_map/ppermute | solution.py:366
  25.9 1.5 %collective-permute-start.7 = (f32[16,576]{1,0:T(8,128)S(1)}, f32[16,576]{1,0:T(8,128)S(1)}, u32[]{:S(2)}, u32[]{:S(2)}) collective-permute-start(f32[16,576]{1,0:T(8,128)S(1)} %shard_map.76), channel_id=1, source_target_pairs={{0,16},{8,24},{16,0},{24,8},{1,17},{9,25},{17,1},{25,9},{2,18},{10... | collective-permute-start | bytes 110600 | tf_op jit(solution)/shard_map/ppermute | solution.py:366
  27.4 2.5 %collective-permute-done.7.recv_ref = f32[16,576]{1,0:T(8,128)S(1)} collective-permute-done((f32[16,576]{1,0:T(8,128)S(1)}, f32[16,576]{1,0:T(8,128)S(1)}, u32[]{:S(2)}, u32[]{:S(2)}) %collective-permute-start.7) | collective-permute-done | bytes 36896 | tf_op jit(solution)/shard_map/ppermute | solution.py:366
  29.9 0.1 shard_map.77
  30.0 1.6 %collective-permute-start.8 = (f32[16,384]{1,0:T(8,128)S(1)}, f32[16,384]{1,0:T(8,128)S(1)}, u32[]{:S(2)}, u32[]{:S(2)}) collective-permute-start(f32[16,384]{1,0:T(8,128)S(1)} %get-tuple-element.42), channel_id=1, source_target_pairs={{0,2},{1,3},{2,0},{3,1},{4,6},{5,7},{6,4},{7,5},{8,10},{9,11},{10,... | collective-permute-start | bytes 73736 | tf_op jit(solution)/shard_map/ppermute | solution.py:362
  31.6 2.3 %collective-permute-done.8.recv_ref = f32[16,384]{1,0:T(8,128)S(1)} collective-permute-done((f32[16,384]{1,0:T(8,128)S(1)}, f32[16,384]{1,0:T(8,128)S(1)}, u32[]{:S(2)}, u32[]{:S(2)}) %collective-permute-start.8) | collective-permute-done | bytes 24608 | tf_op jit(solution)/shard_map/ppermute | solution.py:362
  33.9 0.1 shard_map.78
  34.0 1.5 %collective-permute-start.9 = (f32[16,256]{1,0:T(8,128)S(1)}, f32[16,256]{1,0:T(8,128)S(1)}, u32[]{:S(2)}, u32[]{:S(2)}) collective-permute-start(f32[16,256]{1,0:T(8,128)S(1)} %get-tuple-element.44), channel_id=1, source_target_pairs={{0,1},{1,0},{2,3},{3,2},{4,5},{5,4},{6,7},{7,6},{8,9},{9,8},{10,11... | collective-permute-start | bytes 49160 | tf_op jit(solution)/shard_map/ppermute | solution.py:362
  35.5 2.2 %collective-permute-done.9.recv_ref = f32[16,256]{1,0:T(8,128)S(1)} collective-permute-done((f32[16,256]{1,0:T(8,128)S(1)}, f32[16,256]{1,0:T(8,128)S(1)}, u32[]{:S(2)}, u32[]{:S(2)}) %collective-permute-start.9) | collective-permute-done | bytes 16416 | tf_op jit(solution)/shard_map/ppermute | solution.py:362
  37.7 0.6 %shard_map.79 = (f32[16,144]{1,0:T(8,128)}, f32[1,4]{1,0:T(1,128)}) custom-call(f32[16,144]{1,0:T(8,128)S(1)} %get-tuple-element.43.keep_ref, f32[16,256]{1,0:T(8,128)S(1)} %collective-permute-done.9.recv_ref, f32[16,128]{1,0:T(8,128)S(1)} %get-tuple-element.45.norm_ref), custom_call_target="tpu_custom_call" | custom-call | tf_op jit(solution)/shard_map/pallas_call | solution.py:459
  (8 shorter events, 0.3 us)
Async XLA Ops:
  4.2 6.2 %collective-permute-start = (f32[16,2304]{1,0:T(8,128)S(1)}, f32[16,2304]{1,0:T(8,128)S(1)}, u32[]{:S(2)}, u32[]{:S(2)}) collective-permute-start(f32[16,2304]{1,0:T(8,128)S(1)} %get-tuple-element.26), channel_id=1, source_target_pairs={{0,1},{1,0},{2,3},{3,2},{4,5},{5,4},{6,7},{7,6},{8,10},{9,11},{10,... | collective-permute-start | bytes 442376 | tf_op jit(solution)/shard_map/ppermute | solution.py:362
  7.2 5.3 %collective-permute-start.3 = (f32[16,2304]{1,0:T(8,128)S(1)}, f32[16,2304]{1,0:T(8,128)S(1)}, u32[]{:S(2)}, u32[]{:S(2)}) collective-permute-start(f32[16,2304]{1,0:T(8,128)S(1)} %get-tuple-element.34), channel_id=1, source_target_pairs={{0,1},{1,0},{2,3},{3,2},{4,5},{5,4},{6,7},{7,6},{8,10},{9,11},{10,... | collective-permute-start | bytes 442376 | tf_op jit(solution)/shard_map/ppermute | solution.py:362
  10.4 5.3 %collective-permute-start.1 = (f32[16,2304]{1,0:T(8,128)S(1)}, f32[16,2304]{1,0:T(8,128)S(1)}, u32[]{:S(2)}, u32[]{:S(2)}) collective-permute-start(f32[16,2304]{1,0:T(8,128)S(1)} %get-tuple-element.29), channel_id=1, source_target_pairs={{0,2},{1,3},{2,0},{3,1},{4,6},{5,7},{6,4},{7,5},{8,9},{9,8},{10,11... | collective-permute-start | bytes 442376 | tf_op jit(solution)/shard_map/ppermute | solution.py:362
  12.7 6.2 %collective-permute-start.4 = (f32[16,2304]{1,0:T(8,128)S(1)}, f32[16,2304]{1,0:T(8,128)S(1)}, u32[]{:S(2)}, u32[]{:S(2)}) collective-permute-start(f32[16,2304]{1,0:T(8,128)S(1)} %get-tuple-element.36), channel_id=1, source_target_pairs={{0,2},{1,3},{2,0},{3,1},{4,6},{5,7},{6,4},{7,5},{8,9},{9,8},{10,11... | collective-permute-start | bytes 442376 | tf_op jit(solution)/shard_map/ppermute | solution.py:362
  15.7 7.5 %collective-permute-start.2 = (bf16[16,2304]{1,0:T(8,128)(2,1)S(1)}, bf16[16,2304]{1,0:T(8,128)(2,1)S(1)}, u32[]{:S(2)}, u32[]{:S(2)}) collective-permute-start(bf16[16,2304]{1,0:T(8,128)(2,1)S(1)} %get-tuple-element.31.mine_ref), channel_id=1, source_target_pairs={{0,4},{1,5},{2,6},{3,7},{4,0},{5,1},{6,2},{7,3},{8,12},{9,13},{10,... | collective-permute-start | bytes 221192 | tf_op jit(solution)/shard_map/ppermute | solution.py:362
  18.9 5.3 %collective-permute-start.5 = (bf16[16,2304]{1,0:T(8,128)(2,1)S(1)}, bf16[16,2304]{1,0:T(8,128)(2,1)S(1)}, u32[]{:S(2)}, u32[]{:S(2)}) collective-permute-start(bf16[16,2304]{1,0:T(8,128)(2,1)S(1)} %get-tuple-element.38.refs_3_), channel_id=1, source_target_pairs={{0,4},{1,5},{2,6},{3,7},{4,0},{5,1},{6,2},{7,3},{8,12},{9,13},{10,... | collective-permute-start | bytes 221192 | tf_op jit(solution)/shard_map/ppermute | solution.py:362
  24.5 1.3 %collective-permute-start.6 = (f32[2,16,576]{2,1,0:T(8,128)S(1)}, f32[2,16,576]{2,1,0:T(8,128)S(1)}, u32[]{:S(2)}, u32[]{:S(2)}) collective-permute-start(f32[2,16,576]{2,1,0:T(8,128)S(1)} %shard_map.75), channel_id=1, source_target_pairs={{0,8},{8,0},{16,24},{24,16},{1,9},{9,1},{17,25},{25,17},{2,10},{10... | collective-permute-start | bytes 221192 | tf_op jit(solution)/shard_map/ppermute | solution.py:366
  25.9 4.1 %collective-permute-start.7 = (f32[16,576]{1,0:T(8,128)S(1)}, f32[16,576]{1,0:T(8,128)S(1)}, u32[]{:S(2)}, u32[]{:S(2)}) collective-permute-start(f32[16,576]{1,0:T(8,128)S(1)} %shard_map.76), channel_id=1, source_target_pairs={{0,16},{8,24},{16,0},{24,8},{1,17},{9,25},{17,1},{25,9},{2,18},{10... | collective-permute-start | bytes 110600 | tf_op jit(solution)/shard_map/ppermute | solution.py:366
  30.0 3.8 %collective-permute-start.8 = (f32[16,384]{1,0:T(8,128)S(1)}, f32[16,384]{1,0:T(8,128)S(1)}, u32[]{:S(2)}, u32[]{:S(2)}) collective-permute-start(f32[16,384]{1,0:T(8,128)S(1)} %get-tuple-element.42), channel_id=1, source_target_pairs={{0,2},{1,3},{2,0},{3,1},{4,6},{5,7},{6,4},{7,5},{8,10},{9,11},{10,... | collective-permute-start | bytes 73736 | tf_op jit(solution)/shard_map/ppermute | solution.py:362
  34.0 3.7 %collective-permute-start.9 = (f32[16,256]{1,0:T(8,128)S(1)}, f32[16,256]{1,0:T(8,128)S(1)}, u32[]{:S(2)}, u32[]{:S(2)}) collective-permute-start(f32[16,256]{1,0:T(8,128)S(1)} %get-tuple-element.44), channel_id=1, source_target_pairs={{0,1},{1,0},{2,3},{3,2},{4,5},{5,4},{6,7},{7,6},{8,9},{9,8},{10,11... | collective-permute-start | bytes 49160 | tf_op jit(solution)/shard_map/ppermute | solution.py:362

commit v8 on v7

--- a/solution.py
+++ b/solution.py
@@ -240,18 +240,15 @@
         send_refs[j * width // part][:, at : at + width] = product[2 * rank :]
 
 
-def fold_kernel(half, keep_ref, recv_ref, fact_ref, send_ref, left_ref):
-    width = send_ref.shape[1]
+def fold_kernel(half, place, keep_ref, recv_ref, fact_ref, out_ref):
+    width = out_ref.shape[1]
     columns = slice(half * width, (half + 1) * width)
-    received = recv_ref[...]
-    send_ref[...] = keep_ref[1, :, columns] + fact_ref[2:3, 0:1] * received
-    left_ref[...] = keep_ref[0, :, columns] + fact_ref[1:2, 0:1] * received
-
-
-def round_kernel(keep_ref, recv_ref, own_ref, mine_ref):
-    own = keep_ref[...] + recv_ref[...]
-    own_ref[...] = own
-    mine_ref[...] = own.astype(jnp.bfloat16)
+    weight = fact_ref[place + 1 : place + 2, 0:1]
+    out_ref[...] = keep_ref[place, :, columns] + weight * recv_ref[...]
+
+
+def round_kernel(keep_ref, recv_ref, out_ref):
+    out_ref[...] = (keep_ref[...] + recv_ref[...]).astype(out_ref.dtype)
 
 
 def swapped(pieces, bit):
@@ -308,7 +305,7 @@
         )
     for x in range(n_dp // 2):
         piece = jnp.where(core == sending, halves[2 * x], halves[2 * x + 1])
-        pieces = relative([piece[:, q * width : (q + 1) * width] for q in range(places)], low)
+        pieces = relative([piece[:, q * width : (q + 1) * width] for q in range(places)], low ^ (places - 1))
         pieces_ref[chip ^ x] = jnp.concatenate(pieces, axis=1) * factor
     for norm_ref in norm_refs:
         rows = lax.broadcasted_iota(jnp.int32, norm_ref.shape, 0).astype(jnp.float32)
@@ -319,28 +316,39 @@
     send_ref[...] = keep_ref[1] + recv_ref[1]
 
 
-def with_norms(block, norms, send_ref):
-    width = block.shape[1]
-    spare = send_ref.shape[1] - width
-    send_ref[...] = jnp.concatenate([block, norms[:, :spare]], axis=1)
-
-
-def chip_kernel(keep_ref, core_ref, recv_ref, norm_ref, send_ref, left_ref):
-    total = keep_ref[0] + core_ref[0] + recv_ref[...]
-    half = total.shape[1] // 2
-    left_ref[...] = total[:, :half]
-    with_norms(total[:, half:], norm_ref[...], send_ref)
-
-
-def step_kernel(keep_ref, recv_ref, norm_ref, send_ref, left_ref, norms_ref):
+def with_norms(total, norms, send_ref):
+    lanes = lax.broadcasted_iota(jnp.int32, send_ref.shape, 1)
+    send_ref[...] = jnp.where(
+        lanes < total.shape[1] // 2, total[:, : send_ref.shape[1]], norms[:, 0:1]
+    )
+
+
+def chip_total(keep_ref, core_ref, recv_ref):
+    return keep_ref[0] + core_ref[0] + recv_ref[...]
+
+
+def chip_send_kernel(keep_ref, core_ref, recv_ref, norm_ref, send_ref):
+    with_norms(chip_total(keep_ref, core_ref, recv_ref), norm_ref[...], send_ref)
+
+
+def chip_left_kernel(keep_ref, core_ref, recv_ref, left_ref):
+    left_ref[...] = chip_total(keep_ref, core_ref, recv_ref)[:, left_ref.shape[1] :]
+
+
+def step_total(keep_ref, recv_ref, norm_ref):
     width = keep_ref.shape[1]
-    half = width // 2
     received = recv_ref[...]
-    total = keep_ref[...] + received[:, :width]
-    norms = norm_ref[...] + received[:, width : width + 1]
-    left_ref[...] = total[:, :half]
+    return keep_ref[...] + received[:, :width], norm_ref[...] + received[:, width : width + 1]
+
+
+def step_send_kernel(keep_ref, recv_ref, norm_ref, send_ref):
+    with_norms(*step_total(keep_ref, recv_ref, norm_ref), send_ref)
+
+
+def step_left_kernel(keep_ref, recv_ref, norm_ref, left_ref, norms_ref):
+    total, norms = step_total(keep_ref, recv_ref, norm_ref)
+    left_ref[...] = total[:, left_ref.shape[1] :]
     norms_ref[...] = norms
-    with_norms(total[:, half:], norms, send_ref)
 
 
 def last_kernel(docs, keep_ref, recv_ref, norm_ref, out_ref, norms_ref):
@@ -422,13 +430,12 @@
     wholes, squares = [], []
     firsts = [exchange(send, n_dp, n_ctx, *rounds[0]) for send in sends]
     for half in range(parts):
-        send, left = in_vmem(
-            functools.partial(fold_kernel, half), [single, single], keep, firsts[half], flag
-        )
+        pair = (keep, firsts[half], flag)
+        (send,) = in_vmem(functools.partial(fold_kernel, half, 1), [single], *pair)
         received = exchange(send, n_dp, n_ctx, *rounds[1])
-        own, mine = in_vmem(
-            round_kernel, [single, ((rank, part), jnp.bfloat16)], left, received
-        )
+        (left,) = in_vmem(functools.partial(fold_kernel, half, 0), [single], *pair)
+        (mine,) = in_vmem(round_kernel, [((rank, part), jnp.bfloat16)], left, received)
+        (own,) = in_vmem(round_kernel, [single], left, received)
         other = exchange(mine, n_dp, n_ctx, *rounds[-1])
         if half < parts - 1:
             whole, square = in_vmem(gather_kernel, [single, ((8, 128), f32)], own, mine, other)
@@ -450,11 +457,15 @@
 
     width = slab // 2
     steps = list(reversed(range(bits_of(n_ctx // 2))))
-    send, keep = in_vmem(chip_kernel, shapes(width), keep, core, received, norms)
+    wide, narrow = shapes(width)
+    (send,) = in_vmem(chip_send_kernel, [wide], keep, core, received, norms)
+    (keep,) = in_vmem(chip_left_kernel, [narrow], keep, core, received)
     for bit in steps[:-1]:
         width //= 2
         received = exchange(send, n_dp, n_ctx, bit, bit)
-        send, keep, norms = in_vmem(step_kernel, shapes(width) + [column], keep, received, norms)
+        wide, narrow = shapes(width)
+        (send,) = in_vmem(step_send_kernel, [wide], keep, received, norms)
+        keep, norms = in_vmem(step_left_kernel, [narrow, column], keep, received, norms)
     received = exchange(send, n_dp, n_ctx, steps[-1], steps[-1])
     result, norms = pl.pallas_call(
         functools.partial(last_kernel, docs),

time: 38.5 us -> 38.5 us (level)
    pallas_call x10 -> x16, Pallas kernels: 1.27 us -> 1.53 us  [in_vmem(): pl.pallas_call(kernel, out_shape=[pltpu.VMEM(shape, dtype) for shape, dty...]
  transfers between devices with their start and end apart: 10 -> 10, of which waited for: 8 -> 8; matrix products, arithmetic and copies ran while one was open for 0% -> 0% of each run, Pallas kernels for 2% -> 3%
where the time goes in v8:
time: 38.5 us; the launch traced here: 38.3 us
  starting transfers between devices  17.1 us (44%)
  waiting for transfers between devices  14.8 us (38%)
  Pallas kernels  5.04 us (13%)
  between operations  1.37 us (4%)
    ppermute x8, starting transfers between devices, exchange(): return lax.ppermute(block, ('dp', 'ctx'), route)  15.5 us
    ppermute x8, waiting for transfers between devices, exchange(): return lax.ppermute(block, ('dp', 'ctx'), route)  11.4 us
    ppermute x2, waiting for transfers between devices, swap_dp(): return lax.ppermute(block, 'dp', [(d, d ^ 1 << bit) for d in range(n_dp)])  3.42 us
    pallas_call x1, Pallas kernels, halving_plan(): pl.pallas_call(functools.partial(partials_kernel, n_ctx, docs, chunks), o...  2.9 us
    ppermute x2, starting transfers between devices, swap_dp(): return lax.ppermute(block, 'dp', [(d, d ^ 1 << bit) for d in range(n_dp)])  1.62 us
    pallas_call x16, Pallas kernels, in_vmem(): pl.pallas_call(kernel, out_shape=[pltpu.VMEM(shape, dtype) for shape, dty...  1.53 us
  transfers between devices with their start and end apart: 10, of which 8 were waited for; matrix products, arithmetic and copies ran while one was open for 0% of the time, Pallas kernels for 3%

profile of v8, /device:TPU:0, one launch (start us, length us, event | category | flops | bytes accessed | tf_op | source)
XLA Modules:
  0.0 38.3 jit_solution(5046360359371557676)
XLA Ops:
  1.3 2.9 %shard_map.68 = (f32[16,2304]{1,0:T(8,128)S(1)}, f32[16,2304]{1,0:T(8,128)S(1)}, f32[2,16,4608]{2,1,0:T(8,128)S(1)}, f32[8,128]{1,0:T(8,128)S(1)}) custom-call(s32[1,4]{1,0:T(1,128)} %len_hbm.1, s32[1,1]{1,0:T(1,128)} %bitcast.3.off_hbm, s32[1,4]{1,0:T(1,128)} %inc_hbm.1, bf16[16,512]{1,0:T(8,128)(2,1)} %bitcast.4, bf16[512,4608]{1,0:T(8,128)(2,1)} %grad_hbm.1), custom_call_target="tpu_custom_call" | custom-call | flops 226492416 | bytes 4718592 | tf_op jit(solution)/shard_map/pallas_call | solution.py:402
  4.2 3.1 %collective-permute-start = (f32[16,2304]{1,0:T(8,128)S(1)}, f32[16,2304]{1,0:T(8,128)S(1)}, u32[]{:S(2)}, u32[]{:S(2)}) collective-permute-start(f32[16,2304]{1,0:T(8,128)S(1)} %get-tuple-element.15), channel_id=1, source_target_pairs={{0,1},{1,0},{2,3},{3,2},{4,5},{5,4},{6,7},{7,6},{8,10},{9,11},{10,... | collective-permute-start | bytes 442376 | tf_op jit(solution)/shard_map/ppermute | solution.py:370
  7.2 0.1 collective-permute-start.3
  7.3 3.0 %collective-permute-done.recv_ref = f32[16,2304]{1,0:T(8,128)S(1)} collective-permute-done((f32[16,2304]{1,0:T(8,128)S(1)}, f32[16,2304]{1,0:T(8,128)S(1)}, u32[]{:S(2)}, u32[]{:S(2)}) %collective-permute-start) | collective-permute-done | bytes 147488 | tf_op jit(solution)/shard_map/ppermute | solution.py:370
  10.4 2.1 %collective-permute-start.1 = (f32[16,2304]{1,0:T(8,128)S(1)}, f32[16,2304]{1,0:T(8,128)S(1)}, u32[]{:S(2)}, u32[]{:S(2)}) collective-permute-start(f32[16,2304]{1,0:T(8,128)S(1)} %shard_map.70), channel_id=1, source_target_pairs={{0,2},{1,3},{2,0},{3,1},{4,6},{5,7},{6,4},{7,5},{8,9},{9,8},{10,11... | collective-permute-start | bytes 442376 | tf_op jit(solution)/shard_map/ppermute | solution.py:370
  12.6 1.5 %collective-permute-start.4 = (f32[16,2304]{1,0:T(8,128)S(1)}, f32[16,2304]{1,0:T(8,128)S(1)}, u32[]{:S(2)}, u32[]{:S(2)}) collective-permute-start(f32[16,2304]{1,0:T(8,128)S(1)} %shard_map.75), channel_id=1, source_target_pairs={{0,2},{1,3},{2,0},{3,1},{4,6},{5,7},{6,4},{7,5},{8,9},{9,8},{10,11... | collective-permute-start | bytes 442376 | tf_op jit(solution)/shard_map/ppermute | solution.py:370
  14.3 1.4 %collective-permute-done.1.recv_ref = f32[16,2304]{1,0:T(8,128)S(1)} collective-permute-done((f32[16,2304]{1,0:T(8,128)S(1)}, f32[16,2304]{1,0:T(8,128)S(1)}, u32[]{:S(2)}, u32[]{:S(2)}) %collective-permute-start.1) | collective-permute-done | bytes 147488 | tf_op jit(solution)/shard_map/ppermute | solution.py:370
  15.7 3.1 %collective-permute-start.2 = (bf16[16,2304]{1,0:T(8,128)(2,1)S(1)}, bf16[16,2304]{1,0:T(8,128)(2,1)S(1)}, u32[]{:S(2)}, u32[]{:S(2)}) collective-permute-start(bf16[16,2304]{1,0:T(8,128)(2,1)S(1)} %shard_map.72.mine_ref), channel_id=1, source_target_pairs={{0,4},{1,5},{2,6},{3,7},{4,0},{5,1},{6,2},{7,3},{8,12},{9,13},{10,... | collective-permute-start | bytes 221192 | tf_op jit(solution)/shard_map/ppermute | solution.py:370
  18.8 2.5 %collective-permute-start.5 = (bf16[16,2304]{1,0:T(8,128)(2,1)S(1)}, bf16[16,2304]{1,0:T(8,128)(2,1)S(1)}, u32[]{:S(2)}, u32[]{:S(2)}) collective-permute-start(bf16[16,2304]{1,0:T(8,128)(2,1)S(1)} %shard_map.77.refs_3_), channel_id=1, source_target_pairs={{0,4},{1,5},{2,6},{3,7},{4,0},{5,1},{6,2},{7,3},{8,12},{9,13},{10,... | collective-permute-start | bytes 221192 | tf_op jit(solution)/shard_map/ppermute | solution.py:370
  21.3 1.9 %collective-permute-done.2.other_ref = bf16[16,2304]{1,0:T(8,128)(2,1)S(1)} collective-permute-done((bf16[16,2304]{1,0:T(8,128)(2,1)S(1)}, bf16[16,2304]{1,0:T(8,128)(2,1)S(1)}, u32[]{:S(2)}, u32[]{:S(2)}) %collective-permute-start.2) | collective-permute-done | bytes 73760 | tf_op jit(solution)/shard_map/ppermute | solution.py:370
  23.2 0.2 shard_map.73
  23.4 0.8 %collective-permute-done.5.refs_4_ = bf16[16,2304]{1,0:T(8,128)(2,1)S(1)} collective-permute-done((bf16[16,2304]{1,0:T(8,128)(2,1)S(1)}, bf16[16,2304]{1,0:T(8,128)(2,1)S(1)}, u32[]{:S(2)}, u32[]{:S(2)}) %collective-permute-start.5) | collective-permute-done | bytes 73760 | tf_op jit(solution)/shard_map/ppermute | solution.py:370
  24.2 0.3 shard_map.79
  24.6 0.4 shard_map.78
  24.9 0.9 %collective-permute-done.6.recv_ref.core_ref = f32[2,16,576]{2,1,0:T(8,128)S(1)} collective-permute-done((f32[2,16,576]{2,1,0:T(8,128)S(1)}, f32[2,16,576]{2,1,0:T(8,128)S(1)}, u32[]{:S(2)}, u32[]{:S(2)}) %collective-permute-start.6) | collective-permute-done | bytes 73760 | tf_op jit(solution)/shard_map/ppermute | solution.py:374
  25.9 1.5 %collective-permute-start.7 = (f32[16,576]{1,0:T(8,128)S(1)}, f32[16,576]{1,0:T(8,128)S(1)}, u32[]{:S(2)}, u32[]{:S(2)}) collective-permute-start(f32[16,576]{1,0:T(8,128)S(1)} %shard_map.80), channel_id=1, source_target_pairs={{0,16},{8,24},{16,0},{24,8},{1,17},{9,25},{17,1},{25,9},{2,18},{10... | collective-permute-start | bytes 110600 | tf_op jit(solution)/shard_map/ppermute | solution.py:374
  27.4 2.5 %collective-permute-done.7.recv_ref = f32[16,576]{1,0:T(8,128)S(1)} collective-permute-done((f32[16,576]{1,0:T(8,128)S(1)}, f32[16,576]{1,0:T(8,128)S(1)}, u32[]{:S(2)}, u32[]{:S(2)}) %collective-permute-start.7) | collective-permute-done | bytes 36896 | tf_op jit(solution)/shard_map/ppermute | solution.py:374
  30.0 1.6 %collective-permute-start.8 = (f32[16,384]{1,0:T(8,128)S(1)}, f32[16,384]{1,0:T(8,128)S(1)}, u32[]{:S(2)}, u32[]{:S(2)}) collective-permute-start(f32[16,384]{1,0:T(8,128)S(1)} %shard_map.82), channel_id=1, source_target_pairs={{0,2},{1,3},{2,0},{3,1},{4,6},{5,7},{6,4},{7,5},{8,10},{9,11},{10,... | collective-permute-start | bytes 73736 | tf_op jit(solution)/shard_map/ppermute | solution.py:370
  31.6 0.1 shard_map.81.keep_ref
  31.7 2.2 %collective-permute-done.8.recv_ref = f32[16,384]{1,0:T(8,128)S(1)} collective-permute-done((f32[16,384]{1,0:T(8,128)S(1)}, f32[16,384]{1,0:T(8,128)S(1)}, u32[]{:S(2)}, u32[]{:S(2)}) %collective-permute-start.8) | collective-permute-done | bytes 24608 | tf_op jit(solution)/shard_map/ppermute | solution.py:370
  33.8 0.1 shard_map.84
  34.0 1.5 %collective-permute-start.9 = (f32[16,256]{1,0:T(8,128)S(1)}, f32[16,256]{1,0:T(8,128)S(1)}, u32[]{:S(2)}, u32[]{:S(2)}) collective-permute-start(f32[16,256]{1,0:T(8,128)S(1)} %shard_map.84), channel_id=1, source_target_pairs={{0,1},{1,0},{2,3},{3,2},{4,5},{5,4},{6,7},{7,6},{8,9},{9,8},{10,11... | collective-permute-start | bytes 49160 | tf_op jit(solution)/shard_map/ppermute | solution.py:370
  35.6 2.1 %collective-permute-done.9.recv_ref = f32[16,256]{1,0:T(8,128)S(1)} collective-permute-done((f32[16,256]{1,0:T(8,128)S(1)}, f32[16,256]{1,0:T(8,128)S(1)}, u32[]{:S(2)}, u32[]{:S(2)}) %collective-permute-start.9) | collective-permute-done | bytes 16416 | tf_op jit(solution)/shard_map/ppermute | solution.py:370
  37.7 0.6 %shard_map.85 = (f32[16,144]{1,0:T(8,128)}, f32[1,4]{1,0:T(1,128)}) custom-call(f32[16,144]{1,0:T(8,128)S(1)} %get-tuple-element.22.keep_ref, f32[16,256]{1,0:T(8,128)S(1)} %collective-permute-done.9.recv_ref, f32[16,128]{1,0:T(8,128)S(1)} %get-tuple-element.23.norm_ref), custom_call_target="tpu_custom_call" | custom-call | tf_op jit(solution)/shard_map/pallas_call | solution.py:470
  (14 shorter events, 0.5 us)
Async XLA Ops:
  4.2 6.2 %collective-permute-start = (f32[16,2304]{1,0:T(8,128)S(1)}, f32[16,2304]{1,0:T(8,128)S(1)}, u32[]{:S(2)}, u32[]{:S(2)}) collective-permute-start(f32[16,2304]{1,0:T(8,128)S(1)} %get-tuple-element.15), channel_id=1, source_target_pairs={{0,1},{1,0},{2,3},{3,2},{4,5},{5,4},{6,7},{7,6},{8,10},{9,11},{10,... | collective-permute-start | bytes 442376 | tf_op jit(solution)/shard_map/ppermute | solution.py:370
  7.2 5.3 %collective-permute-start.3 = (f32[16,2304]{1,0:T(8,128)S(1)}, f32[16,2304]{1,0:T(8,128)S(1)}, u32[]{:S(2)}, u32[]{:S(2)}) collective-permute-start(f32[16,2304]{1,0:T(8,128)S(1)} %get-tuple-element.19), channel_id=1, source_target_pairs={{0,1},{1,0},{2,3},{3,2},{4,5},{5,4},{6,7},{7,6},{8,10},{9,11},{10,... | collective-permute-start | bytes 442376 | tf_op jit(solution)/shard_map/ppermute | solution.py:370
  10.4 5.3 %collective-permute-start.1 = (f32[16,2304]{1,0:T(8,128)S(1)}, f32[16,2304]{1,0:T(8,128)S(1)}, u32[]{:S(2)}, u32[]{:S(2)}) collective-permute-start(f32[16,2304]{1,0:T(8,128)S(1)} %shard_map.70), channel_id=1, source_target_pairs={{0,2},{1,3},{2,0},{3,1},{4,6},{5,7},{6,4},{7,5},{8,9},{9,8},{10,11... | collective-permute-start | bytes 442376 | tf_op jit(solution)/shard_map/ppermute | solution.py:370
  12.6 6.2 %collective-permute-start.4 = (f32[16,2304]{1,0:T(8,128)S(1)}, f32[16,2304]{1,0:T(8,128)S(1)}, u32[]{:S(2)}, u32[]{:S(2)}) collective-permute-start(f32[16,2304]{1,0:T(8,128)S(1)} %shard_map.75), channel_id=1, source_target_pairs={{0,2},{1,3},{2,0},{3,1},{4,6},{5,7},{6,4},{7,5},{8,9},{9,8},{10,11... | collective-permute-start | bytes 442376 | tf_op jit(solution)/shard_map/ppermute | solution.py:370
  15.7 7.5 %collective-permute-start.2 = (bf16[16,2304]{1,0:T(8,128)(2,1)S(1)}, bf16[16,2304]{1,0:T(8,128)(2,1)S(1)}, u32[]{:S(2)}, u32[]{:S(2)}) collective-permute-start(bf16[16,2304]{1,0:T(8,128)(2,1)S(1)} %shard_map.72.mine_ref), channel_id=1, source_target_pairs={{0,4},{1,5},{2,6},{3,7},{4,0},{5,1},{6,2},{7,3},{8,12},{9,13},{10,... | collective-permute-start | bytes 221192 | tf_op jit(solution)/shard_map/ppermute | solution.py:370
  18.8 5.3 %collective-permute-start.5 = (bf16[16,2304]{1,0:T(8,128)(2,1)S(1)}, bf16[16,2304]{1,0:T(8,128)(2,1)S(1)}, u32[]{:S(2)}, u32[]{:S(2)}) collective-permute-start(bf16[16,2304]{1,0:T(8,128)(2,1)S(1)} %shard_map.77.refs_3_), channel_id=1, source_target_pairs={{0,4},{1,5},{2,6},{3,7},{4,0},{5,1},{6,2},{7,3},{8,12},{9,13},{10,... | collective-permute-start | bytes 221192 | tf_op jit(solution)/shard_map/ppermute | solution.py:370
  24.5 1.3 %collective-permute-start.6 = (f32[2,16,576]{2,1,0:T(8,128)S(1)}, f32[2,16,576]{2,1,0:T(8,128)S(1)}, u32[]{:S(2)}, u32[]{:S(2)}) collective-permute-start(f32[2,16,576]{2,1,0:T(8,128)S(1)} %shard_map.79), channel_id=1, source_target_pairs={{0,8},{8,0},{16,24},{24,16},{1,9},{9,1},{17,25},{25,17},{2,10},{10... | collective-permute-start | bytes 221192 | tf_op jit(solution)/shard_map/ppermute | solution.py:374
  25.9 4.1 %collective-permute-start.7 = (f32[16,576]{1,0:T(8,128)S(1)}, f32[16,576]{1,0:T(8,128)S(1)}, u32[]{:S(2)}, u32[]{:S(2)}) collective-permute-start(f32[16,576]{1,0:T(8,128)S(1)} %shard_map.80), channel_id=1, source_target_pairs={{0,16},{8,24},{16,0},{24,8},{1,17},{9,25},{17,1},{25,9},{2,18},{10... | collective-permute-start | bytes 110600 | tf_op jit(solution)/shard_map/ppermute | solution.py:374
  30.0 3.8 %collective-permute-start.8 = (f32[16,384]{1,0:T(8,128)S(1)}, f32[16,384]{1,0:T(8,128)S(1)}, u32[]{:S(2)}, u32[]{:S(2)}) collective-permute-start(f32[16,384]{1,0:T(8,128)S(1)} %shard_map.82), channel_id=1, source_target_pairs={{0,2},{1,3},{2,0},{3,1},{4,6},{5,7},{6,4},{7,5},{8,10},{9,11},{10,... | collective-permute-start | bytes 73736 | tf_op jit(solution)/shard_map/ppermute | solution.py:370
  34.0 3.7 %collective-permute-start.9 = (f32[16,256]{1,0:T(8,128)S(1)}, f32[16,256]{1,0:T(8,128)S(1)}, u32[]{:S(2)}, u32[]{:S(2)}) collective-permute-start(f32[16,256]{1,0:T(8,128)S(1)} %shard_map.84), channel_id=1, source_target_pairs={{0,1},{1,0},{2,3},{3,2},{4,5},{5,4},{6,7},{7,6},{8,9},{9,8},{10,11... | collective-permute-start | bytes 49160 | tf_op jit(solution)/shard_map/ppermute | solution.py:370

commit v9 on v7

--- a/solution.py
+++ b/solution.py
@@ -168,7 +168,7 @@
         )
         for j in range(chunks)
     ]
-    for copy in small + copies:
+    for copy in copies[:1] + small + copies[1:]:
         copy.start()
     for copy in small:
         copy.wait()

time: 38.5 us -> 38.5 us (level)
  no operation moved by 1% of the time
where the time goes in v9:
time: 38.5 us; the launch traced here: 38.3 us
  starting transfers between devices  17.1 us (44%)
  waiting for transfers between devices  15.1 us (39%)
  Pallas kernels  4.78 us (12%)
  between operations  1.34 us (3%)
    ppermute x8, starting transfers between devices, exchange(): return lax.ppermute(block, ('dp', 'ctx'), route)  15.5 us
    ppermute x8, waiting for transfers between devices, exchange(): return lax.ppermute(block, ('dp', 'ctx'), route)  11.7 us
    ppermute x2, waiting for transfers between devices, swap_dp(): return lax.ppermute(block, 'dp', [(d, d ^ 1 << bit) for d in range(n_dp)])  3.42 us
    pallas_call x1, Pallas kernels, halving_plan(): pl.pallas_call(functools.partial(partials_kernel, n_ctx, docs, chunks), o...  2.9 us
    ppermute x2, starting transfers between devices, swap_dp(): return lax.ppermute(block, 'dp', [(d, d ^ 1 << bit) for d in range(n_dp)])  1.62 us
    pallas_call x10, Pallas kernels, in_vmem(): pl.pallas_call(kernel, out_shape=[pltpu.VMEM(shape, dtype) for shape, dty...  1.27 us
  transfers between devices with their start and end apart: 10, of which 8 were waited for; matrix products, arithmetic and copies ran while one was open for 0% of the time, Pallas kernels for 2%

profile of v9, /device:TPU:0, one launch (start us, length us, event | category | flops | bytes accessed | tf_op | source)
XLA Modules:
  0.0 38.3 jit_solution(16811853267337571428)
XLA Ops:
  1.3 2.9 %shard_map.68 = (f32[16,2304]{1,0:T(8,128)S(1)}, f32[16,2304]{1,0:T(8,128)S(1)}, f32[2,16,4608]{2,1,0:T(8,128)S(1)}, f32[8,128]{1,0:T(8,128)S(1)}) custom-call(s32[1,4]{1,0:T(1,128)} %len_hbm.1, s32[1,1]{1,0:T(1,128)} %bitcast.3.off_hbm, s32[1,4]{1,0:T(1,128)} %inc_hbm.1, bf16[16,512]{1,0:T(8,128)(2,1)} %bitcast.4, bf16[512,4608]{1,0:T(8,128)(2,1)} %grad_hbm.1), custom_call_target="tpu_custom_call" | custom-call | flops 226492416 | bytes 4718592 | tf_op jit(solution)/shard_map/pallas_call | solution.py:394
  4.2 3.1 %collective-permute-start = (f32[16,2304]{1,0:T(8,128)S(1)}, f32[16,2304]{1,0:T(8,128)S(1)}, u32[]{:S(2)}, u32[]{:S(2)}) collective-permute-start(f32[16,2304]{1,0:T(8,128)S(1)} %get-tuple-element.26), channel_id=1, source_target_pairs={{0,1},{1,0},{2,3},{3,2},{4,5},{5,4},{6,7},{7,6},{8,10},{9,11},{10,... | collective-permute-start | bytes 442376 | tf_op jit(solution)/shard_map/ppermute | solution.py:362
  7.2 0.1 collective-permute-start.3
  7.3 3.0 %collective-permute-done.recv_ref = f32[16,2304]{1,0:T(8,128)S(1)} collective-permute-done((f32[16,2304]{1,0:T(8,128)S(1)}, f32[16,2304]{1,0:T(8,128)S(1)}, u32[]{:S(2)}, u32[]{:S(2)}) %collective-permute-start) | collective-permute-done | bytes 147488 | tf_op jit(solution)/shard_map/ppermute | solution.py:362
  10.4 2.1 %collective-permute-start.1 = (f32[16,2304]{1,0:T(8,128)S(1)}, f32[16,2304]{1,0:T(8,128)S(1)}, u32[]{:S(2)}, u32[]{:S(2)}) collective-permute-start(f32[16,2304]{1,0:T(8,128)S(1)} %get-tuple-element.29), channel_id=1, source_target_pairs={{0,2},{1,3},{2,0},{3,1},{4,6},{5,7},{6,4},{7,5},{8,9},{9,8},{10,11... | collective-permute-start | bytes 442376 | tf_op jit(solution)/shard_map/ppermute | solution.py:362
  12.7 1.5 %collective-permute-start.4 = (f32[16,2304]{1,0:T(8,128)S(1)}, f32[16,2304]{1,0:T(8,128)S(1)}, u32[]{:S(2)}, u32[]{:S(2)}) collective-permute-start(f32[16,2304]{1,0:T(8,128)S(1)} %get-tuple-element.36), channel_id=1, source_target_pairs={{0,2},{1,3},{2,0},{3,1},{4,6},{5,7},{6,4},{7,5},{8,9},{9,8},{10,11... | collective-permute-start | bytes 442376 | tf_op jit(solution)/shard_map/ppermute | solution.py:362
  14.2 1.5 %collective-permute-done.1.recv_ref = f32[16,2304]{1,0:T(8,128)S(1)} collective-permute-done((f32[16,2304]{1,0:T(8,128)S(1)}, f32[16,2304]{1,0:T(8,128)S(1)}, u32[]{:S(2)}, u32[]{:S(2)}) %collective-permute-start.1) | collective-permute-done | bytes 147488 | tf_op jit(solution)/shard_map/ppermute | solution.py:362
  15.7 3.1 %collective-permute-start.2 = (bf16[16,2304]{1,0:T(8,128)(2,1)S(1)}, bf16[16,2304]{1,0:T(8,128)(2,1)S(1)}, u32[]{:S(2)}, u32[]{:S(2)}) collective-permute-start(bf16[16,2304]{1,0:T(8,128)(2,1)S(1)} %get-tuple-element.31.mine_ref), channel_id=1, source_target_pairs={{0,4},{1,5},{2,6},{3,7},{4,0},{5,1},{6,2},{7,3},{8,12},{9,13},{10,... | collective-permute-start | bytes 221192 | tf_op jit(solution)/shard_map/ppermute | solution.py:362
  18.9 2.5 %collective-permute-start.5 = (bf16[16,2304]{1,0:T(8,128)(2,1)S(1)}, bf16[16,2304]{1,0:T(8,128)(2,1)S(1)}, u32[]{:S(2)}, u32[]{:S(2)}) collective-permute-start(bf16[16,2304]{1,0:T(8,128)(2,1)S(1)} %get-tuple-element.38.refs_3_), channel_id=1, source_target_pairs={{0,4},{1,5},{2,6},{3,7},{4,0},{5,1},{6,2},{7,3},{8,12},{9,13},{10,... | collective-permute-start | bytes 221192 | tf_op jit(solution)/shard_map/ppermute | solution.py:362
  21.3 1.9 %collective-permute-done.2.other_ref = bf16[16,2304]{1,0:T(8,128)(2,1)S(1)} collective-permute-done((bf16[16,2304]{1,0:T(8,128)(2,1)S(1)}, bf16[16,2304]{1,0:T(8,128)(2,1)S(1)}, u32[]{:S(2)}, u32[]{:S(2)}) %collective-permute-start.2) | collective-permute-done | bytes 73760 | tf_op jit(solution)/shard_map/ppermute | solution.py:362
  23.2 0.2 shard_map.71
  23.4 0.8 %collective-permute-done.5.refs_4_ = bf16[16,2304]{1,0:T(8,128)(2,1)S(1)} collective-permute-done((bf16[16,2304]{1,0:T(8,128)(2,1)S(1)}, bf16[16,2304]{1,0:T(8,128)(2,1)S(1)}, u32[]{:S(2)}, u32[]{:S(2)}) %collective-permute-start.5) | collective-permute-done | bytes 73760 | tf_op jit(solution)/shard_map/ppermute | solution.py:362
  24.2 0.3 shard_map.75
  24.6 0.3 shard_map.74
  25.0 0.9 %collective-permute-done.6.recv_ref.core_ref = f32[2,16,576]{2,1,0:T(8,128)S(1)} collective-permute-done((f32[2,16,576]{2,1,0:T(8,128)S(1)}, f32[2,16,576]{2,1,0:T(8,128)S(1)}, u32[]{:S(2)}, u32[]{:S(2)}) %collective-permute-start.6) | collective-permute-done | bytes 73760 | tf_op jit(solution)/shard_map/ppermute | solution.py:366
  25.9 1.5 %collective-permute-start.7 = (f32[16,576]{1,0:T(8,128)S(1)}, f32[16,576]{1,0:T(8,128)S(1)}, u32[]{:S(2)}, u32[]{:S(2)}) collective-permute-start(f32[16,576]{1,0:T(8,128)S(1)} %shard_map.76), channel_id=1, source_target_pairs={{0,16},{8,24},{16,0},{24,8},{1,17},{9,25},{17,1},{25,9},{2,18},{10... | collective-permute-start | bytes 110600 | tf_op jit(solution)/shard_map/ppermute | solution.py:366
  27.4 2.5 %collective-permute-done.7.recv_ref = f32[16,576]{1,0:T(8,128)S(1)} collective-permute-done((f32[16,576]{1,0:T(8,128)S(1)}, f32[16,576]{1,0:T(8,128)S(1)}, u32[]{:S(2)}, u32[]{:S(2)}) %collective-permute-start.7) | collective-permute-done | bytes 36896 | tf_op jit(solution)/shard_map/ppermute | solution.py:366
  29.9 0.1 shard_map.77
  30.0 1.6 %collective-permute-start.8 = (f32[16,384]{1,0:T(8,128)S(1)}, f32[16,384]{1,0:T(8,128)S(1)}, u32[]{:S(2)}, u32[]{:S(2)}) collective-permute-start(f32[16,384]{1,0:T(8,128)S(1)} %get-tuple-element.42), channel_id=1, source_target_pairs={{0,2},{1,3},{2,0},{3,1},{4,6},{5,7},{6,4},{7,5},{8,10},{9,11},{10,... | collective-permute-start | bytes 73736 | tf_op jit(solution)/shard_map/ppermute | solution.py:362
  31.6 2.3 %collective-permute-done.8.recv_ref = f32[16,384]{1,0:T(8,128)S(1)} collective-permute-done((f32[16,384]{1,0:T(8,128)S(1)}, f32[16,384]{1,0:T(8,128)S(1)}, u32[]{:S(2)}, u32[]{:S(2)}) %collective-permute-start.8) | collective-permute-done | bytes 24608 | tf_op jit(solution)/shard_map/ppermute | solution.py:362
  33.9 0.1 shard_map.78
  34.0 1.5 %collective-permute-start.9 = (f32[16,256]{1,0:T(8,128)S(1)}, f32[16,256]{1,0:T(8,128)S(1)}, u32[]{:S(2)}, u32[]{:S(2)}) collective-permute-start(f32[16,256]{1,0:T(8,128)S(1)} %get-tuple-element.44), channel_id=1, source_target_pairs={{0,1},{1,0},{2,3},{3,2},{4,5},{5,4},{6,7},{7,6},{8,9},{9,8},{10,11... | collective-permute-start | bytes 49160 | tf_op jit(solution)/shard_map/ppermute | solution.py:362
  35.5 2.2 %collective-permute-done.9.recv_ref = f32[16,256]{1,0:T(8,128)S(1)} collective-permute-done((f32[16,256]{1,0:T(8,128)S(1)}, f32[16,256]{1,0:T(8,128)S(1)}, u32[]{:S(2)}, u32[]{:S(2)}) %collective-permute-start.9) | collective-permute-done | bytes 16416 | tf_op jit(solution)/shard_map/ppermute | solution.py:362
  37.7 0.6 %shard_map.79 = (f32[16,144]{1,0:T(8,128)}, f32[1,4]{1,0:T(1,128)}) custom-call(f32[16,144]{1,0:T(8,128)S(1)} %get-tuple-element.43.keep_ref, f32[16,256]{1,0:T(8,128)S(1)} %collective-permute-done.9.recv_ref, f32[16,128]{1,0:T(8,128)S(1)} %get-tuple-element.45.norm_ref), custom_call_target="tpu_custom_call" | custom-call | tf_op jit(solution)/shard_map/pallas_call | solution.py:459
  (8 shorter events, 0.3 us)
Async XLA Ops:
  4.2 6.2 %collective-permute-start = (f32[16,2304]{1,0:T(8,128)S(1)}, f32[16,2304]{1,0:T(8,128)S(1)}, u32[]{:S(2)}, u32[]{:S(2)}) collective-permute-start(f32[16,2304]{1,0:T(8,128)S(1)} %get-tuple-element.26), channel_id=1, source_target_pairs={{0,1},{1,0},{2,3},{3,2},{4,5},{5,4},{6,7},{7,6},{8,10},{9,11},{10,... | collective-permute-start | bytes 442376 | tf_op jit(solution)/shard_map/ppermute | solution.py:362
  7.2 5.3 %collective-permute-start.3 = (f32[16,2304]{1,0:T(8,128)S(1)}, f32[16,2304]{1,0:T(8,128)S(1)}, u32[]{:S(2)}, u32[]{:S(2)}) collective-permute-start(f32[16,2304]{1,0:T(8,128)S(1)} %get-tuple-element.34), channel_id=1, source_target_pairs={{0,1},{1,0},{2,3},{3,2},{4,5},{5,4},{6,7},{7,6},{8,10},{9,11},{10,... | collective-permute-start | bytes 442376 | tf_op jit(solution)/shard_map/ppermute | solution.py:362
  10.4 5.3 %collective-permute-start.1 = (f32[16,2304]{1,0:T(8,128)S(1)}, f32[16,2304]{1,0:T(8,128)S(1)}, u32[]{:S(2)}, u32[]{:S(2)}) collective-permute-start(f32[16,2304]{1,0:T(8,128)S(1)} %get-tuple-element.29), channel_id=1, source_target_pairs={{0,2},{1,3},{2,0},{3,1},{4,6},{5,7},{6,4},{7,5},{8,9},{9,8},{10,11... | collective-permute-start | bytes 442376 | tf_op jit(solution)/shard_map/ppermute | solution.py:362
  12.7 6.2 %collective-permute-start.4 = (f32[16,2304]{1,0:T(8,128)S(1)}, f32[16,2304]{1,0:T(8,128)S(1)}, u32[]{:S(2)}, u32[]{:S(2)}) collective-permute-start(f32[16,2304]{1,0:T(8,128)S(1)} %get-tuple-element.36), channel_id=1, source_target_pairs={{0,2},{1,3},{2,0},{3,1},{4,6},{5,7},{6,4},{7,5},{8,9},{9,8},{10,11... | collective-permute-start | bytes 442376 | tf_op jit(solution)/shard_map/ppermute | solution.py:362
  15.7 7.5 %collective-permute-start.2 = (bf16[16,2304]{1,0:T(8,128)(2,1)S(1)}, bf16[16,2304]{1,0:T(8,128)(2,1)S(1)}, u32[]{:S(2)}, u32[]{:S(2)}) collective-permute-start(bf16[16,2304]{1,0:T(8,128)(2,1)S(1)} %get-tuple-element.31.mine_ref), channel_id=1, source_target_pairs={{0,4},{1,5},{2,6},{3,7},{4,0},{5,1},{6,2},{7,3},{8,12},{9,13},{10,... | collective-permute-start | bytes 221192 | tf_op jit(solution)/shard_map/ppermute | solution.py:362
  18.9 5.3 %collective-permute-start.5 = (bf16[16,2304]{1,0:T(8,128)(2,1)S(1)}, bf16[16,2304]{1,0:T(8,128)(2,1)S(1)}, u32[]{:S(2)}, u32[]{:S(2)}) collective-permute-start(bf16[16,2304]{1,0:T(8,128)(2,1)S(1)} %get-tuple-element.38.refs_3_), channel_id=1, source_target_pairs={{0,4},{1,5},{2,6},{3,7},{4,0},{5,1},{6,2},{7,3},{8,12},{9,13},{10,... | collective-permute-start | bytes 221192 | tf_op jit(solution)/shard_map/ppermute | solution.py:362
  24.5 1.3 %collective-permute-start.6 = (f32[2,16,576]{2,1,0:T(8,128)S(1)}, f32[2,16,576]{2,1,0:T(8,128)S(1)}, u32[]{:S(2)}, u32[]{:S(2)}) collective-permute-start(f32[2,16,576]{2,1,0:T(8,128)S(1)} %shard_map.75), channel_id=1, source_target_pairs={{0,8},{8,0},{16,24},{24,16},{1,9},{9,1},{17,25},{25,17},{2,10},{10... | collective-permute-start | bytes 221192 | tf_op jit(solution)/shard_map/ppermute | solution.py:366
  25.9 4.1 %collective-permute-start.7 = (f32[16,576]{1,0:T(8,128)S(1)}, f32[16,576]{1,0:T(8,128)S(1)}, u32[]{:S(2)}, u32[]{:S(2)}) collective-permute-start(f32[16,576]{1,0:T(8,128)S(1)} %shard_map.76), channel_id=1, source_target_pairs={{0,16},{8,24},{16,0},{24,8},{1,17},{9,25},{17,1},{25,9},{2,18},{10... | collective-permute-start | bytes 110600 | tf_op jit(solution)/shard_map/ppermute | solution.py:366
  30.0 3.8 %collective-permute-start.8 = (f32[16,384]{1,0:T(8,128)S(1)}, f32[16,384]{1,0:T(8,128)S(1)}, u32[]{:S(2)}, u32[]{:S(2)}) collective-permute-start(f32[16,384]{1,0:T(8,128)S(1)} %get-tuple-element.42), channel_id=1, source_target_pairs={{0,2},{1,3},{2,0},{3,1},{4,6},{5,7},{6,4},{7,5},{8,10},{9,11},{10,... | collective-permute-start | bytes 73736 | tf_op jit(solution)/shard_map/ppermute | solution.py:362
  34.0 3.7 %collective-permute-start.9 = (f32[16,256]{1,0:T(8,128)S(1)}, f32[16,256]{1,0:T(8,128)S(1)}, u32[]{:S(2)}, u32[]{:S(2)}) collective-permute-start(f32[16,256]{1,0:T(8,128)S(1)} %get-tuple-element.44), channel_id=1, source_target_pairs={{0,1},{1,0},{2,3},{3,2},{4,5},{5,4},{6,7},{7,6},{8,9},{9,8},{10,11... | collective-permute-start | bytes 49160 | tf_op jit(solution)/shard_map/ppermute | solution.py:362
